TPU v7x, 32 devices: a whole 2x2x4 slice. The times are simulated.
32 devices in a mesh: shard: 4 (over y, x), ctx: 2 (over core), tp: 4 (over z).
Axes of the slice: x: 2, y: 2, z: 4, core: 2. Of those that a mesh axis runs over, the one named last changes fastest.
Arguments:
- hidden_in: bfloat16 [2048, 2048], P(('shard', 'ctx')), may hold values from -6 to 6
- cotangent: bfloat16 [2048, 2048], P(('shard', 'ctx')), may hold values from -6 to 6
- teacher_out: bfloat16 [2048, 2048], P(('shard', 'ctx')), may hold values from -6 to 6
- teacher_mix: bfloat16 [2048, 2048], P(('shard', 'ctx')), may hold values from -6 to 6
- valid_mask: int32 [2048], P(('shard', 'ctx')), may hold values from 0 to 1, as said below
- doc_start: int32 [2048], P(('shard', 'ctx')), may hold values 0 or 1
- attn_gain: bfloat16 [2048], P(('shard', 'ctx')), may hold values from 0.5 to 1.5
- w_query: bfloat16 [2048, 2048], P(('shard', 'ctx'), 'tp'), may hold values from -0.125 to 0.125
- w_key: bfloat16 [2048, 2048], P(('shard', 'ctx'), 'tp'), may hold values from -0.125 to 0.125
- w_value: bfloat16 [2048, 2048], P(('shard', 'ctx'), 'tp'), may hold values from -0.125 to 0.125
- w_forget: bfloat16 [2048, 256], P(('shard', 'ctx'), 'tp'), may hold values from -0.125 to 0.125
- forget_bias: bfloat16 [4, 64], P('tp', ('shard', 'ctx')), may hold values from 1 to 8
- head_gain: bfloat16 [4, 512], P('tp', ('shard', 'ctx')), may hold values from 0.5 to 1.5
- w_outgate: bfloat16 [2048, 2048], P(('shard', 'ctx'), 'tp'), may hold values from -0.125 to 0.125
- w_out: bfloat16 [2048, 2048], P(('shard', 'ctx'), 'tp'), may hold values from -0.25 to 0.25
- mlp_gain: bfloat16 [2048], P(('shard', 'ctx')), may hold values from 0.5 to 1.5
- w_gate: bfloat16 [2048, 5632], P(('shard', 'ctx'), 'tp'), may hold values from -0.125 to 0.125
- w_up: bfloat16 [2048, 5632], P(('shard', 'ctx'), 'tp'), may hold values from -0.125 to 0.125
- w_down: bfloat16 [2048, 5632], P(('shard', 'ctx'), 'tp'), may hold values from -0.15625 to 0.15625
Outputs:
- output: bfloat16 [2048, 2048], P(('shard', 'ctx'))
- loss_out: float32 [], replicated
- loss_mix: float32 [], replicated
- input_grad: float32 [2048, 2048], P(('shard', 'ctx'))
- grad_attn_gain: float32 [2048], P(('shard', 'ctx'))
- grad_query: float32 [2048, 2048], P(('shard', 'ctx'), 'tp')
- grad_key: float32 [2048, 2048], P(('shard', 'ctx'), 'tp')
- grad_value: float32 [2048, 2048], P(('shard', 'ctx'), 'tp')
- grad_forget: float32 [2048, 256], P(('shard', 'ctx'), 'tp')
- grad_forget_bias: float32 [4, 64], P('tp', ('shard', 'ctx'))
- grad_head_gain: float32 [4, 512], P('tp', ('shard', 'ctx'))
- grad_outgate: float32 [2048, 2048], P(('shard', 'ctx'), 'tp')
- grad_out_proj: float32 [2048, 2048], P(('shard', 'ctx'), 'tp')
- grad_mlp_gain: float32 [2048], P(('shard', 'ctx'))
- grad_gate: float32 [2048, 5632], P(('shard', 'ctx'), 'tp')
- grad_up: float32 [2048, 5632], P(('shard', 'ctx'), 'tp')
- grad_down: float32 [2048, 5632], P(('shard', 'ctx'), 'tp')
Inputs may be any that keep to these rules, and one draw needn't show every extreme that they name: `valid_mask`: the first token is always counted.
All inputs are finite; a program needn't handle non-finite values. No bound on the sum of `doc_start` on one device may be relied on, other than what follows from the above.
Results may differ from a plain program's by a relative error of at most 0.015.
Values may be sent and summed in bfloat16 or wider, within the bound.
A program may use at most 192 MiB of HBM per device.

v0:
```python
import jax
import jax.numpy as jnp
from jax import lax
from jax.sharding import PartitionSpec as P

D = 2048
GROUP = 64


EPSILON = 1e-06
GATE_NORM = 8.0
HIGH = lax.Precision.HIGHEST


def passed_along(value, axis, steps):
    count = lax.axis_size(axis)
    leading, last = (max(0, -steps), min(count, count - steps))
    return lax.ppermute(value, axis, [(source, source + steps) for source in range(leading, last)])


def norm_rows(tensor, gain_row):
    return (
        tensor * lax.rsqrt(jnp.mean(tensor * tensor, axis=-1, keepdims=True) + EPSILON) * gain_row
    )


def rounded(tensor):
    return lax.optimization_barrier(tensor.astype(jnp.bfloat16)).astype(jnp.float32)


def project(activ, weight):
    return jnp.dot(activ, weight, preferred_element_type=jnp.float32)


def project_back(grads, weight):
    return lax.dot_general(
        grads, weight, (((1,), (1,)), ((), ())), preferred_element_type=jnp.float32
    )


def outer_sum(activ, grads):
    return lax.dot_general(
        activ, grads, (((0,), (0,)), ((), ())), preferred_element_type=jnp.float32
    )


def group_tail(log_decay, resets):
    cum_log = jnp.cumsum(log_decay, axis=1)
    counts = jnp.cumsum(resets, axis=1)
    same_end = (counts == counts[:, -1:]).astype(jnp.float32)
    lag_log = jnp.where(same_end[..., None] > 0, cum_log[:, -1:, :] - cum_log, 0.0)
    tail_decay = jnp.exp(lag_log) * same_end[..., None]
    carry_keep = (counts[:, -1] == 0).astype(jnp.float32)
    last_decay = jnp.exp(cum_log[:, -1, :]) * carry_keep[:, None]
    return (cum_log, counts, tail_decay, last_decay)


def group_decay(log_decay, resets):
    cum_log, counts, tail_decay, last_decay = group_tail(log_decay, resets)
    position = jnp.arange(log_decay.shape[1])
    causal = position[:, None] >= position[None, :]
    same_doc = (counts[:, :, None] == counts[:, None, :]) & causal[None]
    log_gap = cum_log[:, :, None, :] - cum_log[:, None, :, :]
    within = jnp.where(
        same_doc[..., None], jnp.exp(jnp.where(same_doc[..., None], log_gap, 0.0)), 0.0
    )
    live_mask = (counts == 0).astype(jnp.float32)
    head_decay = jnp.exp(cum_log) * live_mask[..., None]
    return (within, head_decay, tail_decay, last_decay)


def score_block(carried, pieces):
    query_feats, key_feats, log_decay, resets = pieces
    within, head_decay, tail_decay, last_decay = group_decay(log_decay, resets)
    write_rate = 1.0 - jnp.exp(log_decay)
    scaling = query_feats.shape[-1] ** (-0.5)
    pair_dots = jnp.einsum("btd,bsd->bts", query_feats, key_feats, precision=HIGH)
    inner_term = jnp.einsum(
        "bts,btsm->btm", pair_dots, within * write_rate[:, None], precision=HIGH
    )
    outer_term = head_decay * jnp.einsum("btd,bmd->btm", query_feats, carried, precision=HIGH)
    new_state = last_decay[..., None] * carried + jnp.einsum(
        "bsm,bsd->bmd", tail_decay * write_rate, key_feats, precision=HIGH
    )
    return (new_state, scaling * (inner_term + outer_term))


def value_block(carried, pieces):
    slot_probs, values, log_decay, resets = pieces
    within, head_decay, tail_decay, last_decay = group_decay(log_decay, resets)
    write_rate = 1.0 - jnp.exp(log_decay)
    mixing = jnp.einsum("btm,btsm->bts", slot_probs, within * write_rate[:, None], precision=HIGH)
    result = jnp.einsum("bts,bsd->btd", mixing, values, precision=HIGH)
    result = result + jnp.einsum("btm,bmd->btd", slot_probs * head_decay, carried, precision=HIGH)
    new_state = last_decay[..., None] * carried + jnp.einsum(
        "bsm,bsd->bmd", tail_decay * write_rate, values, precision=HIGH
    )
    return (new_state, result)


def end_block(carried, pieces):
    decay_prod, key_state, value_state = carried
    key_feats, values, log_decay, resets = pieces
    _, _, tail_decay, last_decay = group_tail(log_decay, resets)
    weighted = tail_decay * (1.0 - jnp.exp(log_decay))
    key_next = last_decay[..., None] * key_state + jnp.einsum(
        "bsm,bsd->bmd", weighted, key_feats, precision=HIGH
    )
    value_next = last_decay[..., None] * value_state + jnp.einsum(
        "bsm,bsd->bmd", weighted, values, precision=HIGH
    )
    return ((decay_prod * last_decay, key_next, value_next), None)


def to_blocks(tensor, length):
    shaped = tensor.reshape((tensor.shape[0], tensor.shape[1] // length, length) + tensor.shape[2:])
    return jnp.moveaxis(shaped, 1, 0)


def from_blocks(tensor):
    joined = jnp.moveaxis(tensor, 0, 1)
    return joined.reshape((joined.shape[0], joined.shape[1] * joined.shape[2]) + joined.shape[3:])


def run_scores(query_feats, key_feats, log_decay, resets, start_state):
    pieces = (
        to_blocks(query_feats, GROUP),
        to_blocks(key_feats, GROUP),
        to_blocks(log_decay, GROUP),
        to_blocks(resets, GROUP),
    )
    _, scores = lax.scan(jax.checkpoint(score_block), start_state, pieces)
    return from_blocks(scores)


def run_values(slot_probs, values, log_decay, resets, start_state):
    pieces = (
        to_blocks(slot_probs, GROUP),
        to_blocks(values, GROUP),
        to_blocks(log_decay, GROUP),
        to_blocks(resets, GROUP),
    )
    _, mixed_out = lax.scan(jax.checkpoint(value_block), start_state, pieces)
    return from_blocks(mixed_out)


def end_states(key_feats, values, log_decay, resets):
    heads_dev = key_feats.shape[0]
    start = (
        jnp.ones((heads_dev, log_decay.shape[2]), jnp.float32),
        jnp.zeros((heads_dev, log_decay.shape[2], key_feats.shape[2]), jnp.float32),
        jnp.zeros((heads_dev, log_decay.shape[2], values.shape[2]), jnp.float32),
    )
    pieces = (
        to_blocks(key_feats, GROUP),
        to_blocks(values, GROUP),
        to_blocks(log_decay, GROUP),
        to_blocks(resets, GROUP),
    )
    final, _ = lax.scan(jax.checkpoint(end_block), start, pieces)
    return final


def post_norm(mix_tokens, gate_pre, gain_rows):
    normed = norm_rows(mix_tokens, gain_rows)
    return (normed * jax.nn.silu(gate_pre.reshape(mix_tokens.shape))).reshape(gate_pre.shape)


def to_heads(tensor, heads_dev):
    return tensor.reshape(tensor.shape[0], heads_dev, -1).transpose(1, 0, 2).astype(jnp.float32)


def from_heads(tensor):
    return tensor.transpose(1, 0, 2).reshape(tensor.shape[1], -1)


def per_device(
    hidden_in,
    cotangent,
    teacher_out,
    teacher_mix,
    valid_mask,
    doc_start,
    attn_gain,
    w_query,
    w_key,
    w_value,
    w_forget,
    forget_bias,
    head_gain,
    w_outgate,
    w_out,
    mlp_gain,
    w_gate,
    w_up,
    w_down,
):
    rows_dev = hidden_in.shape[0]
    heads_dev = forget_bias.shape[0]
    tokens_all = rows_dev * lax.axis_size(("shard", "ctx"))
    mask_flat = valid_mask.astype(jnp.float32)
    mask_rows = mask_flat[:, None]
    (
        gain_attn,
        query_w,
        key_w,
        value_w,
        forget_w,
        bias_f,
        gain_head,
        outgate_w,
        out_w,
        gain_mlp,
        gate_w,
        up_w,
        down_w,
    ) = (
        lax.all_gather(attn_gain, ("shard", "ctx"), axis=0, tiled=True),
        lax.all_gather(w_query, ("shard", "ctx"), axis=0, tiled=True),
        lax.all_gather(w_key, ("shard", "ctx"), axis=0, tiled=True),
        lax.all_gather(w_value, ("shard", "ctx"), axis=0, tiled=True),
        lax.all_gather(w_forget, ("shard", "ctx"), axis=0, tiled=True),
        lax.all_gather(forget_bias, ("shard", "ctx"), axis=1, tiled=True),
        lax.all_gather(head_gain, ("shard", "ctx"), axis=1, tiled=True),
        lax.all_gather(w_outgate, ("shard", "ctx"), axis=0, tiled=True),
        lax.all_gather(w_out, ("shard", "ctx"), axis=0, tiled=True),
        lax.all_gather(mlp_gain, ("shard", "ctx"), axis=0, tiled=True),
        lax.all_gather(w_gate, ("shard", "ctx"), axis=0, tiled=True),
        lax.all_gather(w_up, ("shard", "ctx"), axis=0, tiled=True),
        lax.all_gather(w_down, ("shard", "ctx"), axis=0, tiled=True),
    )
    hidden_f = hidden_in.astype(jnp.float32)
    attn_scale = gain_attn.astype(jnp.float32)
    normed_in = norm_rows(hidden_f, attn_scale).astype(jnp.bfloat16)
    query_pre = project(normed_in, query_w)
    keys_pre = project(normed_in, key_w)
    query_bf = jax.nn.silu(query_pre).astype(jnp.bfloat16)
    keys_bf = jax.nn.silu(keys_pre).astype(jnp.bfloat16)
    values_bf = project(normed_in, value_w).astype(jnp.bfloat16)
    forget_pre = project(normed_in, forget_w) + bias_f.astype(jnp.float32).reshape(-1)
    log_decay = jax.nn.log_sigmoid(forget_pre) / GATE_NORM
    gate_pre = project(normed_in, outgate_w)
    query_heads = to_heads(query_bf, heads_dev)
    keys_heads = to_heads(keys_bf, heads_dev)
    values_heads = to_heads(values_bf, heads_dev)
    decay_heads = to_heads(log_decay, heads_dev)
    resets = doc_start.astype(jnp.float32)[None]

    def local_ends(key_arg, value_arg, decay_arg):
        return end_states(key_arg, value_arg, decay_arg, resets)

    (decay_dev, keys_end, values_end), end_back = jax.vjp(
        local_ends, keys_heads, values_heads, decay_heads
    )

    def relay_step(turn, carried):
        return passed_along(
            (
                decay_dev[..., None] * carried[0] + keys_end,
                decay_dev[..., None] * carried[1] + values_end,
            ),
            "ctx",
            1,
        )

    keys_in, values_in = lax.fori_loop(
        0,
        lax.axis_size("ctx") - 1,
        relay_step,
        (jnp.zeros_like(keys_end), jnp.zeros_like(values_end)),
    )
    scores = run_scores(query_heads, keys_heads, decay_heads, resets, keys_in)
    probs_exact = jax.nn.softmax(scores, axis=-1)
    probs_low = rounded(probs_exact)
    slot_mix = run_values(probs_low, values_heads, decay_heads, resets, values_in)
    mix_tokens = slot_mix.transpose(1, 0, 2)
    head_scale = gain_head.astype(jnp.float32)
    gated_bf = post_norm(mix_tokens, gate_pre, head_scale).astype(jnp.bfloat16)
    branch = lax.psum(project_back(gated_bf, out_w), "tp")
    middle = hidden_f + branch
    mlp_scale = gain_mlp.astype(jnp.float32)
    normed_mid = norm_rows(middle, mlp_scale).astype(jnp.bfloat16)
    gate_val = project(normed_mid, gate_w)
    up_val = project(normed_mid, up_w)
    hidden_units = (jax.nn.silu(gate_val) * up_val).astype(jnp.bfloat16)
    result = middle + lax.psum(project_back(hidden_units, down_w), "tp")
    diff_out = result - teacher_out.astype(jnp.float32)
    diff_mix = branch - teacher_mix.astype(jnp.float32)
    part_out = jnp.sum(mask_rows * diff_out * diff_out)
    part_mix = jnp.sum(mask_rows * diff_mix * diff_mix)
    count_total, total_out, total_mix = lax.psum(
        (jnp.sum(mask_flat), part_out, part_mix), ("shard", "ctx")
    )
    loss_scale = tokens_all / count_total
    grad_result = cotangent.astype(jnp.float32) + loss_scale * mask_rows * diff_out
    grad_mlp = grad_result.astype(jnp.bfloat16)
    grad_units = project(grad_mlp, down_w)
    down_grad = outer_sum(grad_mlp, hidden_units)

    def unit_product(gate_arg, up_arg):
        return jax.nn.silu(gate_arg) * up_arg

    _, unit_back = jax.vjp(unit_product, gate_val, up_val)
    grad_gate_f, grad_up_f = unit_back(grad_units)
    grad_gate_val = grad_gate_f.astype(jnp.bfloat16)
    grad_up_val = grad_up_f.astype(jnp.bfloat16)
    gate_grad = outer_sum(normed_mid, grad_gate_val)
    up_grad = outer_sum(normed_mid, grad_up_val)
    grad_mid_norm = lax.psum(
        project_back(grad_gate_val, gate_w) + project_back(grad_up_val, up_w), "tp"
    )
    _, mid_back = jax.vjp(norm_rows, middle, mlp_scale)
    grad_mid_part, mlp_gain_grad = mid_back(grad_mid_norm)
    grad_middle = grad_mid_part + grad_result
    grad_branch = (grad_middle + loss_scale * mask_rows * diff_mix).astype(jnp.bfloat16)
    grad_gated = project(grad_branch, out_w)
    out_grad = outer_sum(grad_branch, gated_bf)
    _, post_back = jax.vjp(post_norm, mix_tokens, gate_pre, head_scale)
    grad_mix_tok, grad_gate_pre, head_gain_grad = post_back(grad_gated)
    prob_shift = probs_low - probs_exact

    def attend(query_arg, key_arg, value_arg, decay_arg, keys_start, values_start):
        score_arg = run_scores(query_arg, key_arg, decay_arg, resets, keys_start)
        prob_arg = jax.nn.softmax(score_arg, axis=-1) + prob_shift
        return run_values(prob_arg, value_arg, decay_arg, resets, values_start)

    _, attend_back = jax.vjp(
        attend, query_heads, keys_heads, values_heads, decay_heads, keys_in, values_in
    )
    grad_query_h, grad_keys_h, grad_values_h, grad_decay_h, carry_keys, carry_values = attend_back(
        grad_mix_tok.transpose(1, 0, 2)
    )

    def return_step(turn, carried):
        return passed_along(
            (
                carry_keys + decay_dev[..., None] * carried[0],
                carry_values + decay_dev[..., None] * carried[1],
            ),
            "ctx",
            -1,
        )

    end_keys, end_values = lax.fori_loop(
        0,
        lax.axis_size("ctx") - 1,
        return_step,
        (jnp.zeros_like(carry_keys), jnp.zeros_like(carry_values)),
    )
    decay_dev_grad = jnp.sum(end_keys * keys_in, axis=-1) + jnp.sum(end_values * values_in, axis=-1)
    more_keys, more_values, more_decay = end_back((decay_dev_grad, end_keys, end_values))
    grad_keys_h = grad_keys_h + more_keys
    grad_values_h = grad_values_h + more_values
    grad_decay_h = grad_decay_h + more_decay
    _, silu_query = jax.vjp(jax.nn.silu, query_pre)
    grad_query_pre = silu_query(from_heads(grad_query_h))[0].astype(jnp.bfloat16)
    _, silu_keys = jax.vjp(jax.nn.silu, keys_pre)
    grad_keys_pre = silu_keys(from_heads(grad_keys_h))[0].astype(jnp.bfloat16)
    grad_values_low = from_heads(grad_values_h).astype(jnp.bfloat16)

    def forget_map(forget_arg):
        return jax.nn.log_sigmoid(forget_arg) / GATE_NORM

    _, forget_back = jax.vjp(forget_map, forget_pre)
    grad_forget_pre = forget_back(from_heads(grad_decay_h))[0].astype(jnp.bfloat16)
    grad_gate_low = grad_gate_pre.astype(jnp.bfloat16)
    query_grad = outer_sum(normed_in, grad_query_pre)
    keys_grad = outer_sum(normed_in, grad_keys_pre)
    values_grad = outer_sum(normed_in, grad_values_low)
    forget_grad = outer_sum(normed_in, grad_forget_pre)
    outgate_grad = outer_sum(normed_in, grad_gate_low)
    bias_grad = jnp.sum(grad_forget_pre.astype(jnp.float32), axis=0).reshape(heads_dev, -1)
    grad_in_part = (
        project_back(grad_query_pre, query_w)
        + project_back(grad_keys_pre, key_w)
        + project_back(grad_values_low, value_w)
    )
    grad_in_part = (
        grad_in_part
        + project_back(grad_forget_pre, forget_w)
        + project_back(grad_gate_low, outgate_w)
    )
    grad_in_norm = lax.psum(grad_in_part, "tp")
    _, in_back = jax.vjp(norm_rows, hidden_f, attn_scale)
    grad_hidden, attn_gain_grad = in_back(grad_in_norm)
    input_grad = grad_hidden + grad_middle
    shares = tuple(
        (
            lax.psum_scatter(attn_gain_grad, ("shard", "ctx"), scatter_dimension=0, tiled=True),
            lax.psum_scatter(query_grad, ("shard", "ctx"), scatter_dimension=0, tiled=True),
            lax.psum_scatter(keys_grad, ("shard", "ctx"), scatter_dimension=0, tiled=True),
            lax.psum_scatter(values_grad, ("shard", "ctx"), scatter_dimension=0, tiled=True),
            lax.psum_scatter(forget_grad, ("shard", "ctx"), scatter_dimension=0, tiled=True),
            lax.psum_scatter(bias_grad, ("shard", "ctx"), scatter_dimension=1, tiled=True),
            lax.psum_scatter(head_gain_grad, ("shard", "ctx"), scatter_dimension=1, tiled=True),
            lax.psum_scatter(outgate_grad, ("shard", "ctx"), scatter_dimension=0, tiled=True),
            lax.psum_scatter(out_grad, ("shard", "ctx"), scatter_dimension=0, tiled=True),
            lax.psum_scatter(mlp_gain_grad, ("shard", "ctx"), scatter_dimension=0, tiled=True),
            lax.psum_scatter(gate_grad, ("shard", "ctx"), scatter_dimension=0, tiled=True),
            lax.psum_scatter(up_grad, ("shard", "ctx"), scatter_dimension=0, tiled=True),
            lax.psum_scatter(down_grad, ("shard", "ctx"), scatter_dimension=0, tiled=True),
        )
    )
    loss_out = total_out / (2.0 * D * count_total)
    loss_mix = total_mix / (2.0 * D * count_total)
    return (result.astype(jnp.bfloat16), loss_out, loss_mix, input_grad) + shares


def solution(mesh):
    return jax.shard_map(
        per_device,
        mesh=mesh,
        in_specs=(
            P(("shard", "ctx"), None),
            P(("shard", "ctx"), None),
            P(("shard", "ctx"), None),
            P(("shard", "ctx"), None),
            P(("shard", "ctx")),
            P(("shard", "ctx")),
            P(("shard", "ctx")),
            P(("shard", "ctx"), "tp"),
            P(("shard", "ctx"), "tp"),
            P(("shard", "ctx"), "tp"),
            P(("shard", "ctx"), "tp"),
            P("tp", ("shard", "ctx")),
            P("tp", ("shard", "ctx")),
            P(("shard", "ctx"), "tp"),
            P(("shard", "ctx"), "tp"),
            P(("shard", "ctx")),
            P(("shard", "ctx"), "tp"),
            P(("shard", "ctx"), "tp"),
            P(("shard", "ctx"), "tp"),
        ),
        out_specs=(
            P(("shard", "ctx"), None),
            P(),
            P(),
            P(("shard", "ctx"), None),
            P(("shard", "ctx")),
            P(("shard", "ctx"), "tp"),
            P(("shard", "ctx"), "tp"),
            P(("shard", "ctx"), "tp"),
            P(("shard", "ctx"), "tp"),
            P("tp", ("shard", "ctx")),
            P("tp", ("shard", "ctx")),
            P(("shard", "ctx"), "tp"),
            P(("shard", "ctx"), "tp"),
            P(("shard", "ctx")),
            P(("shard", "ctx"), "tp"),
            P(("shard", "ctx"), "tp"),
            P(("shard", "ctx"), "tp"),
        ),
        check_vma=False,
    )
```

profile of v0, /device:TPU:0, one launch (start us, length us, event | category | flops | bytes accessed | tf_op | source)
XLA Modules:
  0.0 1481.1 jit_solution(18292701896970657464)
XLA Ops:
  12.8 10.4 all-gather
  25.7 13.8 all-reduce.12
  39.5 9.6 all_gather.40
  51.6 3.1 multiply_convert_fusion.5
  54.8 15.5 %all-gather.13.cloned.1.call-done = bf16[2048,512]{1,0:T(8,128)(2,1)} async-done(((bf16[256,512]{1,0:T(8,128)(2,1)}), bf16[2048,512]{1,0:T(8,128)(2,1)}) %all-gather.13.cloned.1.call-update) | async-done | bytes 2097168 | tf_op jit(solution)/shard_map/all_gather | solution.py:221
  74.4 20.4 %while.157 = (s32[]{:T(128)}, f32[1,64]{1,0:T(1,128)S(1)}, f32[1,64,512]{2,1,0:T(8,128)S(1)}, f32[1,64,512]{2,1,0:T(8,128)S(1)}, f32[4,1,64]{2,1,0:T(1,128)}, /*...) while((s32[]{:T(128)}, f32[1,64]{1,0:T(1,128)S(1)}, ...), condition=%wide.region_4.5_spmd.clone, body=%wide.region_1.4_spmd.clone.sunk | while | flops 50897348 | bytes 1518861 | solution.py:160
  100.1 3.1 multiply_convert_fusion.4
  105.5 26.0 %while.152 = (s32[]{:T(128)}, f32[1,64,512]{2,1,0:T(8,128)S(1)}, f32[4,1,64,64]{3,2,1,0:T(8,128)S(1)}, f32[4,1,64,64]{3,2,1,0:T(8,128)S(1)}, f32[4,1,64]{2,1,0:T...) while((s32[]{:T(128)}, f32[1,64,512]{2,1,0:T(8,128)S(1)}, ...), condition=%wide.region_8.9_spmd, body=%wide.region_5.8_spmd.sunk | while | flops 80073024 | bytes 1262291 | solution.py:132
  133.5 34.7 %while.153 = (s32[]{:T(128)}, f32[1,64,512]{2,1,0:T(8,128)S(1)}, f32[4,1,64,512]{3,2,1,0:T(8,128)}, f32[4,1,64,64]{3,2,1,0:T(8,128)S(1)}, f32[4,1,64]{2,1,0:T(1,...) while((s32[]{:T(128)}, f32[1,64,512]{2,1,0:T(8,128)S(1)}, ...), condition=%wide.region_14.15_spmd, body=%wide.region_11.14_spmd.sunk | while | flops 80097600 | bytes 1408731 | solution.py:143
  134.7 4.0 fusion.602
  143.3 4.0 fusion.602
  152.0 4.0 fusion.602
  160.7 4.0 fusion.602
  170.3 3.4 multiply_convert_fusion.3
  173.7 3.7 fusion.392
  180.3 13.7 psum.52
  194.7 8.9 all-gather.1
  204.9 58.9 %all-reduce.18.cloned.1.call-done = f32[256,2048]{1,0:T(8,128)} async-done(((f32[256,2048]{1,0:T(8,128)}), f32[256,2048]{1,0:T(8,128)}) %all-reduce.18.cloned.1.call-update) | async-done | bytes 2097168 | tf_op jit(solution)/shard_map/psum | solution.py:279
  267.0 40.9 %all-gather.21.cloned.1.call-done = bf16[2048,1408]{1,0:T(8,128)(2,1)} async-done(((bf16[256,1408]{1,0:T(8,128)(2,1)}), bf16[2048,1408]{1,0:T(8,128)(2,1)}) %all-gather.21.cloned.1.call-update) | async-done | bytes 5767184 | tf_op jit(solution)/shard_map/all_gather | solution.py:228
  307.9 5.9 fusion.393
  313.8 39.2 %all-gather.23.cloned.1.call-done = bf16[2048,1408]{1,0:T(8,128)(2,1)} async-done(((bf16[256,1408]{1,0:T(8,128)(2,1)}), bf16[2048,1408]{1,0:T(8,128)(2,1)}) %all-gather.23.cloned.1.call-update) | async-done | bytes 5767184 | tf_op jit(solution)/shard_map/all_gather | solution.py:229
  353.0 6.5 multiply_convert_fusion.2
  359.6 38.6 %all-gather.25.cloned.1.call-done = bf16[2048,1408]{1,0:T(8,128)(2,1)} async-done(((bf16[256,1408]{1,0:T(8,128)(2,1)}), bf16[2048,1408]{1,0:T(8,128)(2,1)}) %all-gather.25.cloned.1.call-update) | async-done | bytes 5767184 | tf_op jit(solution)/shard_map/all_gather | solution.py:230
  398.1 6.0 fusion.394
  405.7 63.7 %while.156 = (s32[]{:T(128)}, f32[1,64,512]{2,1,0:T(8,128)S(1)}, f32[4,1,64,64]{3,2,1,0:T(8,128)}, f32[4,1,64,512]{3,2,1,0:T(8,128)}, f32[4,1,64,64]{3,2,1,0:T(8...) while((s32[]{:T(128)}, f32[1,64,512]{2,1,0:T(8,128)S(1)}, ...), condition=%wide.region_35.36_spmd.clone, body=%wide.region_32.35_spmd.clone.sunk | while | flops 80073024 | bytes 1558547 | solution.py:132
  413.0 3.1 fusion.634
  428.9 3.1 fusion.634
  444.8 3.1 fusion.634
  460.8 3.1 fusion.634
  469.4 21.0 %all-reduce.20.cloned.1.call-done = f32[256,2048]{1,0:T(8,128)} async-done(((f32[256,2048]{1,0:T(8,128)}), f32[256,2048]{1,0:T(8,128)}) %all-reduce.20.cloned.1.call-update) | async-done | bytes 2097168 | tf_op jit(solution)/shard_map/psum | solution.py:286
  490.5 3.1 multiply_add_fusion
  493.6 6.9 multiply_convert_fusion.1
  502.5 3.1 convolution_add_fusion.8
  506.7 44.9 %while.154 = (s32[]{:T(128)}, f32[1,64,512]{2,1,0:T(8,128)S(1)}, f32[4,1,64,512]{3,2,1,0:T(8,128)}, f32[4,1,64,64]{3,2,1,0:T(8,128)S(1)}, f32[4,1,64]{2,1,0:T(1,...) while((s32[]{:T(128)}, f32[1,64,512]{2,1,0:T(8,128)S(1)}, ...), condition=%wide.region_31.32_spmd, body=%wide.region_28.31_spmd.sunk | while | flops 25514180 | bytes 792779 | solution.py:143
  554.0 37.0 %all-reduce.22.cloned.1.call-done = f32[256,2048]{1,0:T(8,128)} async-done(((f32[256,2048]{1,0:T(8,128)}), f32[256,2048]{1,0:T(8,128)}) %all-reduce.22.cloned.1.call-update) | async-done | bytes 2097168 | tf_op jit(solution)/shard_map/psum | solution.py:309
  591.0 6.6 multiply_reduce_fusion.4
  604.9 70.2 %while.158 = (s32[]{:T(128)}, f32[1,64,512]{2,1,0:T(8,128)S(1)}, f32[4,1,64,64]{3,2,1,0:T(8,128)S(1)}, f32[4,1,64,512]{3,2,1,0:T(8,128)}, f32[4,1,64,64]{3,2,1,0...) while((s32[]{:T(128)}, f32[1,64,512]{2,1,0:T(8,128)S(1)}, ...), condition=%wide.region_47.48_spmd.clone, body=%wide.region_38.47_spmd.clone.sunk | while | flops 163393856 | bytes 4154033 | solution.py:143
  611.1 4.0 fusion.666
  628.6 4.0 fusion.666
  646.1 4.0 fusion.666
  663.7 4.0 fusion.666
  677.9 65.1 %while.159 = (s32[]{:T(128)}, f32[1,64,512]{2,1,0:T(8,128)S(1)}, f32[4,1,64,512]{3,2,1,0:T(8,128)}, f32[4,1,64,512]{3,2,1,0:T(8,128)}, f32[4,1,64,64]{3,2,1,0:T(...) while((s32[]{:T(128)}, f32[1,64,512]{2,1,0:T(8,128)S(1)}, ...), condition=%wide.region_58.59_spmd.clone, body=%wide.region_49.58_spmd.clone.sunk | while | flops 209576256 | bytes 4729045 | solution.py:132
  687.4 4.0 fusion.692
  703.7 4.0 fusion.692
  719.9 4.0 fusion.692
  736.1 4.0 fusion.692
  750.2 3.7 fusion.396
  756.5 31.1 %while.155 = (s32[]{:T(128)}, f32[1,64]{1,0:T(1,128)S(1)}, f32[1,64,512]{2,1,0:T(8,128)S(1)}, f32[1,64,512]{2,1,0:T(8,128)S(1)}, f32[4,1,64,512]{3,2,1,0:T(8,128...) while((s32[]{:T(128)}, f32[1,64]{1,0:T(1,128)S(1)}, ...), condition=%wide.region_68.69_spmd, body=%wide.region_61.68_spmd.sunk | while | flops 101499328 | bytes 3286075 | solution.py:160
  811.1 2.9 fusion.369
  818.5 7.3 fusion.349
  827.2 6.0 fusion.398
  834.4 6.0 fusion.399
  844.0 42.3 %all-reduce.24.cloned.1.call-done = f32[256,2048]{1,0:T(8,128)} async-done(((f32[256,2048]{1,0:T(8,128)}), f32[256,2048]{1,0:T(8,128)}) %all-reduce.24.cloned.1.call-update) | async-done | bytes 2097168 | tf_op jit(solution)/shard_map/psum | solution.py:383
  888.5 24.9 %all-reduce.11 = (f32[]{:T(128)}, f32[]{:T(128)}, f32[2048]{0:T(1024)S(1)}, f32[1,64]{1,0:T(1,128)S(1)}, f32[2048]{0:T(1024)S(1)}) all-reduce(f32[]{:T(128)} %get-tuple-element.1531, f32[]{:T(128)} %get-tuple-element.1534, f32[2048]{0:T(1024)S(1)} %get-tuple-element.1529, ...), channel_id=1, replica_groups=mesh['shard'=4,'ctx'=2,'tp'=4] {'shard','ctx'}, use_global_device_ids=true, to_apply=%region_20.21 | all-reduce | flops 4162 | bytes 33296 | tf_op jit(solution)/shard_map/psum | solution.py:291
  916.6 3.4 fusion.331
  920.0 3.0 reduce-scatter.20.cloned.1.call-done
  923.0 55.0 %reduce-scatter.24.cloned.1.call-done = f32[256,512]{1,0:T(8,128)} async-done(((f32[2048,512]{1,0:T(8,128)}), f32[256,512]{1,0:T(8,128)}) %reduce-scatter.24.cloned.1.call-update) | async-done | bytes 524304 | tf_op jit(solution)/shard_map/reduce_scatter | solution.py:397
  977.9 55.0 %reduce-scatter.14.cloned.1.call-done = f32[256,512]{1,0:T(8,128)} async-done(((f32[2048,512]{1,0:T(8,128)}), f32[256,512]{1,0:T(8,128)}) %reduce-scatter.14.cloned.1.call-update) | async-done | bytes 524304 | tf_op jit(solution)/shard_map/reduce_scatter | solution.py:390
  1032.9 55.0 %reduce-scatter.22.cloned.1.call-done = f32[256,512]{1,0:T(8,128)} async-done(((f32[2048,512]{1,0:T(8,128)}), f32[256,512]{1,0:T(8,128)}) %reduce-scatter.22.cloned.1.call-update) | async-done | bytes 524304 | tf_op jit(solution)/shard_map/reduce_scatter | solution.py:396
  1087.9 55.0 %reduce-scatter.18.cloned.1.call-done = f32[256,512]{1,0:T(8,128)} async-done(((f32[2048,512]{1,0:T(8,128)}), f32[256,512]{1,0:T(8,128)}) %reduce-scatter.18.cloned.1.call-update) | async-done | bytes 524304 | tf_op jit(solution)/shard_map/reduce_scatter | solution.py:392
  1142.8 55.1 %reduce-scatter.16.cloned.1.call-done = f32[256,512]{1,0:T(8,128)} async-done(((f32[2048,512]{1,0:T(8,128)}), f32[256,512]{1,0:T(8,128)}) %reduce-scatter.16.cloned.1.call-update) | async-done | bytes 524304 | tf_op jit(solution)/shard_map/reduce_scatter | solution.py:391
  1198.0 91.1 %reduce-scatter.30.cloned.1.call-done = f32[256,1408]{1,0:T(8,128)} async-done(((f32[2048,1408]{1,0:T(8,128)}), f32[256,1408]{1,0:T(8,128)}) %reduce-scatter.30.cloned.1.call-update) | async-done | bytes 1441808 | tf_op jit(solution)/shard_map/reduce_scatter | solution.py:401
  1289.1 91.2 %reduce-scatter.26.cloned.1.call-done = f32[256,1408]{1,0:T(8,128)} async-done(((f32[2048,1408]{1,0:T(8,128)}), f32[256,1408]{1,0:T(8,128)}) %reduce-scatter.26.cloned.1.call-update) | async-done | bytes 1441808 | tf_op jit(solution)/shard_map/reduce_scatter | solution.py:399
  1380.3 91.2 %reduce-scatter.28.cloned.1.call-done = f32[256,1408]{1,0:T(8,128)} async-done(((f32[2048,1408]{1,0:T(8,128)}), f32[256,1408]{1,0:T(8,128)}) %reduce-scatter.28.cloned.1.call-update) | async-done | bytes 1441808 | tf_op jit(solution)/shard_map/reduce_scatter | solution.py:400
  (928 shorter events, 366.9 us)
Async XLA Ops:
  7.2 16.1 %copy-start.78 = (u32[32]{0:T(128)S(1)}, u32[32]{0:T(128)}, u32[]{:S(2)}) copy-start(u32[32]{0:T(128)} %constant.481) | copy-start | bytes 388
  7.2 41.9 %copy-start = (bf16[256,2048]{1,0:T(8,128)(2,1)S(1)}, bf16[256,2048]{1,0:T(8,128)(2,1)}, u32[]{:S(2)}) copy-start(bf16[256,2048]{1,0:T(8,128)(2,1)} %param.35) | copy-start | bytes 3145732
  7.2 5.6 copy-start.80
  7.2 18.0 %copy-start.81 = (bf16[1,64]{1,0:T(2,128)(2,1)S(1)}, bf16[1,64]{1,0:T(2,128)(2,1)}, u32[]{:S(2)}) copy-start(bf16[1,64]{1,0:T(2,128)(2,1)} %param.47) | copy-start | bytes 388
  7.2 18.2 %copy-start.82 = (bf16[1,8]{1,0:T(2,128)(2,1)S(1)}, bf16[1,8]{1,0:T(2,128)(2,1)}, u32[]{:S(2)}) copy-start(bf16[1,8]{1,0:T(2,128)(2,1)} %param.46) | copy-start | bytes 52
  7.2 32.2 %copy-start.60 = (bf16[256,64]{0,1:T(8,128)(2,1)S(1)}, bf16[256,64]{0,1:T(8,128)(2,1)}, u32[]{:S(2)}) copy-start(bf16[256,64]{0,1:T(8,128)(2,1)} %param.45) | copy-start | bytes 98308
  7.3 44.4 %all-gather.11.cloned.1.call-start = ((), (), s32[]{:S(2)}) async-start(), calls=%async_computation.10 | async-start | bytes 2359296 | tf_op jit(solution)/shard_map/all_gather | solution.py:220
  8.0 62.3 %all-gather.13.cloned.1.call-start = ((), (), s32[]{:S(2)}) async-start(), calls=%async_computation.11 | async-start | bytes 2359296 | tf_op jit(solution)/shard_map/all_gather | solution.py:221
  8.7 91.4 %all-gather.15.cloned.1.call-start = ((), (), s32[]{:S(2)}) async-start(), calls=%async_computation.12 | async-start | bytes 2359296 | tf_op jit(solution)/shard_map/all_gather | solution.py:219
  9.5 160.8 %all-gather.17.cloned.1.call-start = ((), (), s32[]{:S(2)}) async-start(), calls=%async_computation.13 | async-start | bytes 2359296 | tf_op jit(solution)/shard_map/all_gather | solution.py:225
  10.1 40.3 %copy-start.79 = (s32[256]{0:T(256)S(1)}, s32[256]{0:T(256)}, u32[]{:S(2)}) copy-start(s32[256]{0:T(256)} %param.40) | copy-start | bytes 3076
  10.1 163.6 %all-gather.19.cloned.1.call-start = ((), (), s32[]{:S(2)}) async-start(), calls=%async_computation.14 | async-start | bytes 2359296 | tf_op jit(solution)/shard_map/all_gather | solution.py:226
  10.6 253.1 %all-reduce.18.cloned.1.call-start = ((), (), s32[]{:S(2)}) async-start(), calls=%async_computation.15 | async-start | bytes 4194304 | tf_op jit(solution)/shard_map/psum | solution.py:279
  12.8 157.4 %copy-start.54 = (f32[256]{0:T(256)}, f32[256]{0:T(256)S(1)}, u32[]{:S(2)}) copy-start(f32[256]{0:T(256)S(1)} %fusion.362) | copy-start | bytes 3076
  49.1 5.7 copy-start.37
  95.6 9.9 collective-permute-start.1
  103.3 29.3 %collective-permute-start = (f32[1,64,512]{2,1,0:T(8,128)}, f32[1,64,512]{2,1,0:T(8,128)S(1)}, u32[]{:S(2)}, u32[]{:S(2)}) collective-permute-start(f32[1,64,512]{2,1,0:T(8,128)} %get-tuple-element.1775), channel_id=1, source_target_pairs={{0,4},{1,5},{2,6},{3,7},{8,12},{9,13},{10,14},{11,15},{16,20},{17,... | collective-permute-start | bytes 393224 | tf_op jit(solution)/shard_map/while/body/eval_jaxpr/ppermute | solution.py:18
  105.5 99.4 %copy-start.5 = (f32[1,64,512]{2,1,0:T(8,128)}, f32[1,64,512]{2,1,0:T(8,128)S(1)}, u32[]{:S(2)}) copy-start(f32[1,64,512]{2,1,0:T(8,128)S(1)} %collective-permute-done.1) | copy-start | bytes 393220
  132.6 336.8 %copy-start.13 = (f32[1,64,512]{2,1,0:T(8,128)}, f32[1,64,512]{2,1,0:T(8,128)S(1)}, u32[]{:S(2)}) copy-start(f32[1,64,512]{2,1,0:T(8,128)S(1)} %collective-permute-done) | copy-start | bytes 393220
  168.2 5.4 copy-start.3
  177.4 17.3 %copy-start.83 = (bf16[256]{0:T(256)(128)(2,1)S(1)}, bf16[256]{0:T(256)(128)(2,1)}, u32[]{:S(2)}) copy-start(bf16[256]{0:T(256)(128)(2,1)} %param.50) | copy-start | bytes 1540
  177.5 130.5 %all-gather.21.cloned.1.call-start = ((), (), s32[]{:S(2)}) async-start(), calls=%async_computation.16 | async-start | bytes 6488064 | tf_op jit(solution)/shard_map/all_gather | solution.py:228
  178.2 174.8 %all-gather.23.cloned.1.call-start = ((), (), s32[]{:S(2)}) async-start(), calls=%async_computation.17 | async-start | bytes 6488064 | tf_op jit(solution)/shard_map/all_gather | solution.py:229
  179.0 219.2 %all-gather.25.cloned.1.call-start = ((), (), s32[]{:S(2)}) async-start(), calls=%async_computation.18 | async-start | bytes 6488064 | tf_op jit(solution)/shard_map/all_gather | solution.py:230
  179.7 310.8 %all-reduce.20.cloned.1.call-start = ((), (), s32[]{:S(2)}) async-start(), calls=%async_computation.19 | async-start | bytes 4194304 | tf_op jit(solution)/shard_map/psum | solution.py:286
  265.7 48.1 %copy-start.71 = (f32[256]{0:T(256)}, f32[256]{0:T(256)S(1)}, u32[]{:S(2)}) copy-start(f32[256]{0:T(256)S(1)} %get-tuple-element.1718) | copy-start | bytes 3076
  265.8 48.0 %copy-start.62 = (f32[256]{0:T(256)}, f32[256]{0:T(256)S(1)}, u32[]{:S(2)}) copy-start(f32[256]{0:T(256)S(1)} %fusion.363) | copy-start | bytes 3076
  404.2 186.8 %all-reduce.22.cloned.1.call-start = ((), (), s32[]{:S(2)}) async-start(), calls=%async_computation.20 | async-start | bytes 4194304 | tf_op jit(solution)/shard_map/psum | solution.py:309
  490.5 10.1 slice-start
  490.5 12.0 slice-start.2
  493.6 6.9 copy-start.9
  493.6 6.9 slice-start.1
  493.6 8.8 slice-start.3
  505.6 337.0 %reduce-scatter.32.cloned.1.call-start = ((), (), s32[]{:S(2)}) async-start(), calls=%async_computation.31 | async-start | bytes 294912
  506.7 44.9 %copy-start.25 = (f32[4,1,64,64]{3,2,1,0:T(8,128)S(1)}, f32[4,1,64,64]{3,2,1,0:T(8,128)}, u32[]{:S(2)}) copy-start(f32[4,1,64,64]{3,2,1,0:T(8,128)} %get-tuple-element.1141) | copy-start | bytes 196612
  551.8 123.3 %copy-start.57 = (f32[4,64]{1,0:T(4,128)}, f32[4,64]{1,0:T(4,128)S(1)}, u32[]{:S(2)}) copy-start(f32[4,64]{1,0:T(4,128)S(1)} %reduce_max.19) | copy-start | bytes 3076
  552.1 45.6 %copy-start.58 = (f32[4,64]{1,0:T(4,128)}, f32[4,64]{1,0:T(4,128)S(1)}, u32[]{:S(2)}) copy-start(f32[4,64]{1,0:T(4,128)S(1)} %fusion.355) | copy-start | bytes 3076
  554.0 43.7 %copy-start.72 = (f32[256]{0:T(256)S(1)}, f32[256]{0:T(256)}, u32[]{:S(2)}) copy-start(f32[256]{0:T(256)} %copy-done.71) | copy-start | bytes 3076
  554.0 43.7 %copy-start.63 = (f32[256]{0:T(256)S(1)}, f32[256]{0:T(256)}, u32[]{:S(2)}) copy-start(f32[256]{0:T(256)} %copy-done.62) | copy-start | bytes 3076
  554.0 43.7 %copy-start.66 = (f32[256]{0:T(256)S(1)}, f32[256]{0:T(256)}, u32[]{:S(2)}) copy-start(f32[256]{0:T(256)} %broadcast_multiply_fusion.5) | copy-start | bytes 3076
  591.0 6.7 copy-start.10
  591.0 6.7 copy-start.12
  591.0 6.7 copy-start.19
  591.0 6.7 copy-start.27
  604.8 70.5 %copy-start.59 = (f32[4,64]{1,0:T(4,128)S(1)}, f32[4,64]{1,0:T(4,128)}, u32[]{:S(2)}) copy-start(f32[4,64]{1,0:T(4,128)} %copy-done.58) | copy-start | bytes 3076
  604.8 73.0 %copy-start.2 = (f32[4,1,64,512]{3,2,1,0:T(8,128)S(1)}, f32[4,1,64,512]{3,2,1,0:T(8,128)}, u32[]{:S(2)}) copy-start(f32[4,1,64,512]{3,2,1,0:T(8,128)} %get-tuple-element.2786) | copy-start | bytes 1572868
  604.9 73.1 %copy-start.23 = (f32[1,64,512]{2,1,0:T(8,128)S(1)}, f32[1,64,512]{2,1,0:T(8,128)}, u32[]{:S(2)}) copy-start(f32[1,64,512]{2,1,0:T(8,128)} %custom-call.4) | copy-start | bytes 393220
  687.4 5.3 copy-start.53
  743.0 5.7 copy-start.44
  744.6 9.4 collective-permute-start.3
  745.8 8.2 collective-permute-start.2
  748.7 137.5 %all-reduce.24.cloned.1.call-start = ((), (), s32[]{:S(2)}) async-start(), calls=%async_computation.21 | async-start | bytes 4194304 | tf_op jit(solution)/shard_map/psum | solution.py:383
  800.1 122.8 %reduce-scatter.20.cloned.1.call-start = ((), (), s32[]{:S(2)}) async-start(), calls=%async_computation.25 | async-start | bytes 589824 | tf_op jit(solution)/shard_map/reduce_scatter | solution.py:393
  802.1 175.8 %reduce-scatter.24.cloned.1.call-start = ((), (), s32[]{:S(2)}) async-start(), calls=%async_computation.27 | async-start | bytes 4718592 | tf_op jit(solution)/shard_map/reduce_scatter | solution.py:397
  805.0 227.9 %reduce-scatter.14.cloned.1.call-start = ((), (), s32[]{:S(2)}) async-start(), calls=%async_computation.22 | async-start | bytes 4718592 | tf_op jit(solution)/shard_map/reduce_scatter | solution.py:390
  808.0 279.9 %reduce-scatter.22.cloned.1.call-start = ((), (), s32[]{:S(2)}) async-start(), calls=%async_computation.26 | async-start | bytes 4718592 | tf_op jit(solution)/shard_map/reduce_scatter | solution.py:396
  811.1 331.8 %reduce-scatter.18.cloned.1.call-start = ((), (), s32[]{:S(2)}) async-start(), calls=%async_computation.24 | async-start | bytes 4718592 | tf_op jit(solution)/shard_map/reduce_scatter | solution.py:392
  814.1 383.9 %reduce-scatter.16.cloned.1.call-start = ((), (), s32[]{:S(2)}) async-start(), calls=%async_computation.23 | async-start | bytes 4718592 | tf_op jit(solution)/shard_map/reduce_scatter | solution.py:391
  817.0 472.1 %reduce-scatter.30.cloned.1.call-start = ((), (), s32[]{:S(2)}) async-start(), calls=%async_computation.30 | async-start | bytes 12976128 | tf_op jit(solution)/shard_map/reduce_scatter | solution.py:401
  825.8 554.5 %reduce-scatter.26.cloned.1.call-start = ((), (), s32[]{:S(2)}) async-start(), calls=%async_computation.28 | async-start | bytes 12976128 | tf_op jit(solution)/shard_map/reduce_scatter | solution.py:399
  833.3 638.2 %reduce-scatter.28.cloned.1.call-start = ((), (), s32[]{:S(2)}) async-start(), calls=%async_computation.29 | async-start | bytes 12976128 | tf_op jit(solution)/shard_map/reduce_scatter | solution.py:400
  840.5 48.0 %copy-start.61 = (f32[2048]{0:T(1024)S(1)}, f32[2048]{0:T(1024)}, u32[]{:S(2)}) copy-start(f32[2048]{0:T(1024)} %get-tuple-element.1527) | copy-start | bytes 24580
  840.5 76.1 %copy-start.68 = (f32[256]{0:T(256)S(1)}, f32[256]{0:T(256)}, u32[]{:S(2)}) copy-start(f32[256]{0:T(256)} %copy-done.67) | copy-start | bytes 3076
  840.5 76.1 %copy-start.17 = (f32[256,2048]{1,0:T(8,128)S(1)}, f32[256,2048]{1,0:T(8,128)}, u32[]{:S(2)}) copy-start(f32[256,2048]{1,0:T(8,128)} %get-tuple-element.1717) | copy-start | bytes 6291460
  (80 other events, 214.5 us)
Sparse Core Ops, SparseCore 0:
  10.0 30.6 all-gather.10
  42.5 27.7 all-gather.12
  72.2 27.8 all-gather.14
  101.8 27.7 all-gather.16
  131.4 27.8 all-gather.18
  177.6 86.1 all-reduce.17
  265.7 42.2 all-gather.20
  309.8 43.1 all-gather.22
  354.9 43.1 all-gather.24
  404.3 86.1 all-reduce.19
  505.8 85.1 all-reduce.21
  748.8 33.6 reduce-scatter.31
  800.3 85.9 all-reduce.23
  889.7 33.1 reduce-scatter.19
  926.7 51.1 reduce-scatter.23
  981.7 51.1 reduce-scatter.13
  1036.7 51.1 reduce-scatter.21
  1091.7 51.1 reduce-scatter.17
  1146.8 51.1 reduce-scatter.15
  1201.9 87.1 reduce-scatter.29
  1293.1 87.1 reduce-scatter.25
  1384.4 87.1 reduce-scatter.27
where the time goes:
time: 1490 us; the launch traced here: 1480 us
  waiting for transfers between devices  853 us (57%)
  matrix products  245 us (16%)
  other arithmetic  139 us (9%)
  local copies, waits for them, and re-layouts  108 us (7%)
  blocking collectives  81.3 us (5%)
  between operations  23.6 us (2%)
  loops' own time  23.3 us (2%)
    reduce_scatter x1, waiting for transfers between devices, per_device(): lax.psum_scatter(gate_grad, ('shard', 'ctx'), scatter_dimension=0, tiled=...  91.2 us
    reduce_scatter x1, waiting for transfers between devices, per_device(): lax.psum_scatter(up_grad, ('shard', 'ctx'), scatter_dimension=0, tiled=True)  91.2 us
    reduce_scatter x1, waiting for transfers between devices, per_device(): lax.psum_scatter(down_grad, ('shard', 'ctx'), scatter_dimension=0, tiled=...  91.1 us
    psum x1, waiting for transfers between devices, per_device(): branch = lax.psum(project_back(gated_bf, out_w), 'tp')  58.9 us
    reduce_scatter x1, waiting for transfers between devices, per_device(): lax.psum_scatter(keys_grad, ('shard', 'ctx'), scatter_dimension=0, tiled=...  55.1 us
    reduce_scatter x1, waiting for transfers between devices, per_device(): lax.psum_scatter(query_grad, ('shard', 'ctx'), scatter_dimension=0, tiled...  55 us
    reduce_scatter x1, waiting for transfers between devices, per_device(): lax.psum_scatter(outgate_grad, ('shard', 'ctx'), scatter_dimension=0, til...  55 us
    reduce_scatter x1, waiting for transfers between devices, per_device(): lax.psum_scatter(values_grad, ('shard', 'ctx'), scatter_dimension=0, tile...  55 us
  transfers between devices with their start and end apart: 26, of which 18 were waited for; matrix products, arithmetic and copies ran while one was open for 21% of the time, Pallas kernels for 0%

commit v1 on v0

v1 whole, which is shorter than its diff:
```python
import functools

import jax
import jax.numpy as jnp
from jax import lax
from jax.experimental import pallas as pl
from jax.experimental.pallas import tpu as pltpu
from jax.sharding import PartitionSpec as P

F32 = jnp.float32
BF = jnp.bfloat16
EPSILON = 1e-06
GATE_NORM = 8.0


def dot_nn(a, b):
    return lax.dot_general(a, b, (((1,), (0,)), ((), ())), preferred_element_type=F32)


def dot_nt(a, b):
    return lax.dot_general(a, b, (((1,), (1,)), ((), ())), preferred_element_type=F32)


def dot_tn(a, b):
    return lax.dot_general(a, b, (((0,), (0,)), ((), ())), preferred_element_type=F32)


def halves(x):
    hi = x.astype(BF)
    return hi, (x - hi.astype(F32)).astype(BF)


def sigmoid(u):
    return 1.0 / (1.0 + jnp.exp(-u))


def n_levels(tokens):
    return tokens.bit_length() - 1


def span_matrix(level, tokens):
    t = lax.broadcasted_iota(jnp.int32, (tokens, tokens), 0)
    u = lax.broadcasted_iota(jnp.int32, (tokens, tokens), 1)
    depth = n_levels(tokens)
    if level == depth:
        keep = u <= t
    elif level == depth + 1:
        keep = u > t
    else:
        half = 1 << level
        edge = (t & ~(2 * half - 1)) + half
        odd = (t & half) > 0
        keep = (odd & (u >= edge) & (u <= t)) | (~odd & (u > t) & (u < edge))
    return keep.astype(F32).astype(BF)


def odd_rows(level, tokens, columns):
    t = lax.broadcasted_iota(jnp.int32, (tokens, columns), 0)
    return (t & (1 << level)) > 0


def same_pair(level, tokens):
    t = lax.broadcasted_iota(jnp.int32, (tokens, tokens), 0)
    u = lax.broadcasted_iota(jnp.int32, (tokens, tokens), 1)
    return (t >> (level + 1)) == (u >> (level + 1))


def ends_kernel(pre_ref, resets_ref, keys_ref, values_ref, spans_ref, total_ref, ends_ref):
    tokens, slots = pre_ref.shape
    depth = n_levels(tokens)
    width = keys_ref.shape[1]
    pre = pre_ref[...]
    log_decay = (jnp.minimum(pre, 0.0) - jnp.log1p(jnp.exp(-jnp.abs(pre)))) / GATE_NORM
    write = 1.0 - jnp.exp(log_decay)
    hi, lo = halves(log_decay)
    resets = jnp.broadcast_to(resets_ref[...], (tokens, slots)).astype(BF)
    stacked = jnp.concatenate([hi, lo, resets], axis=1)
    for level in range(depth + 2):
        sums = dot_nn(span_matrix(level, tokens), stacked)
        gap = sums[:, :slots] + sums[:, slots : 2 * slots]
        live = sums[:, 2 * slots :] < 0.5
        span = jnp.where(live, jnp.exp(gap), 0.0)
        spans_ref[level] = span
        if level == depth:
            total_ref[...] = span[tokens - 1 :, :]
        if level == depth + 1:
            hi, lo = halves(span * write)
            ends_ref[:, :width] = dot_tn(hi, keys_ref[...]) + dot_tn(lo, keys_ref[...])
            ends_ref[:, width:] = dot_tn(hi, values_ref[...]) + dot_tn(lo, values_ref[...])


def run_ends(pre, resets, keys, values):
    tokens, slots = pre.shape
    depth = n_levels(tokens)
    return pl.pallas_call(
        ends_kernel,
        out_shape=(
            jax.ShapeDtypeStruct((depth + 2, tokens, slots), F32),
            jax.ShapeDtypeStruct((1, slots), F32),
            jax.ShapeDtypeStruct((slots, keys.shape[1] + values.shape[1]), F32),
        ),
        name="slot_ends",
    )(pre, resets, keys, values)


def decay_write(pre):
    log_decay = (jnp.minimum(pre, 0.0) - jnp.log1p(jnp.exp(-jnp.abs(pre)))) / GATE_NORM
    return jnp.exp(log_decay)


def forward_kernel(
    query_ref, keys_ref, values_ref, pre_ref, spans_ref, state_ref, gate_ref, gain_ref,
    probs_ref, pairs_ref, mixing_ref, mix_ref, gated_ref,
):
    tokens, slots = pre_ref.shape
    depth = n_levels(tokens)
    width = keys_ref.shape[1]
    scaling = width ** (-0.5)
    write = 1.0 - decay_write(pre_ref[...])
    query = query_ref[...]
    pairs = dot_nt(query, keys_ref[...])
    pairs_ref[...] = pairs
    t = lax.broadcasted_iota(jnp.int32, (tokens, tokens), 0)
    u = lax.broadcasted_iota(jnp.int32, (tokens, tokens), 1)
    diagonal = jnp.sum(jnp.where(t == u, pairs, 0.0), axis=1, keepdims=True)
    state_hi, state_lo = halves(state_ref[:, :width])
    head = spans_ref[depth]
    raw = head * (dot_nt(query, state_hi) + dot_nt(query, state_lo)) + diagonal * write
    for level in range(depth):
        span = spans_ref[level]
        odd = odd_rows(level, tokens, slots)
        left, left_lo = halves(jnp.where(same_pair(level, tokens), pairs, 0.0))
        right, right_lo = halves(jnp.where(odd, 0.0, span * write))
        pulled = dot_nn(left, right) + dot_nn(left_lo, right) + dot_nn(left, right_lo)
        raw = raw + jnp.where(odd, span, 0.0) * pulled
    scores = scaling * raw
    scores = scores - jnp.max(scores, axis=1, keepdims=True)
    raised = jnp.exp(scores)
    probs = raised / jnp.sum(raised, axis=1, keepdims=True)
    probs_ref[...] = probs
    probs = probs.astype(BF).astype(F32)
    mixing = jnp.zeros((tokens, tokens), F32)
    for level in reversed(range(depth)):
        span = spans_ref[level]
        odd = odd_rows(level, tokens, slots)
        left, left_lo = halves(jnp.where(odd, span * probs, 0.0))
        right, right_lo = halves(jnp.where(odd, 0.0, span * write))
        pushed = dot_nt(left, right) + dot_nt(left_lo, right) + dot_nt(left, right_lo)
        mixing = jnp.where(same_pair(level, tokens), pushed, mixing)
    mixing = jnp.where(t == u, jnp.sum(probs * write, axis=1, keepdims=True), mixing)
    mixing, mixing_lo = halves(mixing)
    mixing_ref[...] = mixing
    state_hi, state_lo = halves(state_ref[:, width:])
    carried, carried_lo = halves(probs * head)
    mix = dot_nn(mixing, values_ref[...]) + dot_nn(mixing_lo, values_ref[...])
    mix = mix + dot_nn(carried, state_hi) + dot_nn(carried, state_lo) + dot_nn(carried_lo, state_hi)
    mix_ref[...] = mix
    scale = lax.rsqrt(jnp.mean(mix * mix, axis=1, keepdims=True) + EPSILON)
    gate = gate_ref[...]
    gated_ref[...] = (mix * scale * gain_ref[...] * (gate * sigmoid(gate))).astype(BF)


def run_forward(query, keys, values, pre, spans, state, gate, gain):
    tokens, slots = pre.shape
    width = keys.shape[1]
    return pl.pallas_call(
        forward_kernel,
        out_shape=(
            jax.ShapeDtypeStruct((tokens, slots), F32),
            jax.ShapeDtypeStruct((tokens, tokens), F32),
            jax.ShapeDtypeStruct((tokens, tokens), BF),
            jax.ShapeDtypeStruct((tokens, width), F32),
            jax.ShapeDtypeStruct((tokens, width), BF),
        ),
        name="slot_forward",
    )(query, keys, values, pre, spans, state, gate, gain)


def backward_kernel(
    grad_ref, query_ref, keys_ref, values_ref, pre_ref, spans_ref, state_ref, gate_ref, gain_ref,
    probs_ref, pairs_ref, mixing_ref, mix_ref,
    gquery_ref, gkeys_ref, gvalues_ref, ggate_ref, ggain_ref, gwrite_ref, glog_ref, carry_ref,
):
    tokens, slots = pre_ref.shape
    depth = n_levels(tokens)
    width = keys_ref.shape[1]
    scaling = width ** (-0.5)
    gate = gate_ref[...]
    sig = sigmoid(gate)
    silu = gate * sig
    gain = gain_ref[...]
    mix = mix_ref[...]
    scale = lax.rsqrt(jnp.mean(mix * mix, axis=1, keepdims=True) + EPSILON)
    normed = mix * scale
    grad = grad_ref[...]
    ggate_ref[...] = (grad * gain * normed * (sig * (1.0 + gate * (1.0 - sig)))).astype(BF)
    ggain_ref[...] = jnp.sum(grad * normed * silu, axis=0, keepdims=True)
    inner = grad * gain * silu
    mix_grad = scale * (inner - normed * jnp.mean(normed * inner, axis=1, keepdims=True))
    mix_low = mix_grad.astype(BF)

    write = 1.0 - decay_write(pre_ref[...])
    query, keys, values = query_ref[...], keys_ref[...], values_ref[...]
    pairs = pairs_ref[...]
    pairs_t = dot_nt(keys, query)
    mix_rest = (mix_grad - mix_low.astype(F32)).astype(BF)
    weigh = dot_nt(mix_low, values) + dot_nt(mix_rest, values)
    weigh_t = dot_nt(values, mix_low) + dot_nt(values, mix_rest)
    t = lax.broadcasted_iota(jnp.int32, (tokens, tokens), 0)
    u = lax.broadcasted_iota(jnp.int32, (tokens, tokens), 1)
    pair_diag = jnp.sum(jnp.where(t == u, pairs, 0.0), axis=1, keepdims=True)
    weigh_diag = jnp.sum(jnp.where(t == u, weigh, 0.0), axis=1, keepdims=True)
    head = spans_ref[depth]
    probs = probs_ref[...]
    probs_low = probs.astype(BF).astype(F32)

    vstate_hi, vstate_lo = halves(state_ref[:, width:])
    head_probs = head * (
        dot_nt(mix_low, vstate_hi) + dot_nt(mix_low, vstate_lo) + dot_nt(mix_rest, vstate_hi)
    )
    probs_grad = head_probs + weigh_diag * write
    row_values, row_keys = [], []
    for level in range(depth):
        span = spans_ref[level]
        odd = odd_rows(level, tokens, slots)
        same = same_pair(level, tokens)
        right, right_lo = halves(jnp.where(odd, 0.0, span * write))
        reach = jnp.where(odd, span, 0.0)
        left, left_lo = halves(jnp.where(same, weigh, 0.0))
        term = reach * (dot_nn(left, right) + dot_nn(left_lo, right) + dot_nn(left, right_lo))
        row_values.append(term)
        left, left_lo = halves(jnp.where(same, pairs, 0.0))
        row_keys.append(reach * (dot_nn(left, right) + dot_nn(left_lo, right) + dot_nn(left, right_lo)))
        probs_grad = probs_grad + term
    scores_grad = probs * (probs_grad - jnp.sum(probs_grad * probs, axis=1, keepdims=True))
    scores_grad = scaling * scores_grad

    kstate_hi, kstate_lo = halves(state_ref[:, :width])
    head_keys = head * (dot_nt(query, kstate_hi) + dot_nt(query, kstate_lo))
    gwrite = pair_diag * scores_grad + weigh_diag * probs_low
    glog = dot_tn(span_matrix(depth, tokens), (head_keys * scores_grad + head_probs * probs_low).astype(BF))
    gpairs = jnp.zeros((tokens, tokens), F32)
    for level in reversed(range(depth)):
        span = spans_ref[level]
        odd = odd_rows(level, tokens, slots)
        same = same_pair(level, tokens)
        reach = jnp.where(odd, span, 0.0)
        source = jnp.where(odd, 0.0, span)
        key_side, key_rest = halves(reach * scores_grad)
        value_side, value_rest = halves(reach * probs_low)
        seen, seen_rest = halves(jnp.where(same, pairs_t, 0.0))
        felt, felt_rest = halves(jnp.where(same, weigh_t, 0.0))
        sent, sent_rest = halves(source * write)
        pushed = dot_nt(key_side, sent) + dot_nt(key_rest, sent) + dot_nt(key_side, sent_rest)
        gpairs = jnp.where(same, pushed, gpairs)
        column = source * (
            dot_nn(seen, key_side) + dot_nn(seen, key_rest) + dot_nn(seen_rest, key_side)
            + dot_nn(felt, value_side) + dot_nn(felt, value_rest) + dot_nn(felt_rest, value_side)
        )
        gwrite = gwrite + column
        moved = column * write + row_values[level] * probs_low + row_keys[level] * scores_grad
        spread = span_matrix(level, tokens)
        moved, moved_rest = halves(moved)
        glog = glog + dot_tn(spread, moved) + dot_tn(spread, moved_rest)
    gpairs = jnp.where(t == u, jnp.sum(scores_grad * write, axis=1, keepdims=True), gpairs)
    gpairs, gpairs_rest = halves(gpairs)
    gwrite_ref[...] = gwrite
    glog_ref[...] = glog
    key_head, key_head_rest = halves(scores_grad * head)
    gquery_ref[...] = (
        dot_nn(gpairs, keys)
        + dot_nn(gpairs_rest, keys)
        + dot_nn(key_head, kstate_hi)
        + dot_nn(key_head, kstate_lo)
        + dot_nn(key_head_rest, kstate_hi)
    )
    gkeys_ref[...] = dot_tn(gpairs, query) + dot_tn(gpairs_rest, query)
    gvalues_ref[...] = dot_tn(mixing_ref[...], mix_low)
    carry_ref[:, :width] = dot_tn(key_head, query) + dot_tn(key_head_rest, query)
    carry_ref[:, width:] = dot_tn((probs_low * head).astype(BF), mix_low)


def run_backward(grad, query, keys, values, pre, spans, state, gate, gain, probs, pairs, mixing, mix):
    tokens, slots = pre.shape
    width = keys.shape[1]
    wide = jax.ShapeDtypeStruct((tokens, width), F32)
    narrow = jax.ShapeDtypeStruct((tokens, slots), F32)
    return pl.pallas_call(
        backward_kernel,
        out_shape=(
            wide, wide, wide,
            jax.ShapeDtypeStruct((tokens, width), BF),
            jax.ShapeDtypeStruct((1, width), F32),
            narrow, narrow,
            jax.ShapeDtypeStruct((slots, 2 * width), F32),
        ),
        name="slot_backward",
    )(grad, query, keys, values, pre, spans, state, gate, gain, probs, pairs, mixing, mix)


def finish_kernel(
    gquery_ref, gkeys_ref, gvalues_ref, ggate_ref, gwrite_ref, glog_ref,
    keys_ref, values_ref, pre_ref, spans_ref, query_pre_ref, keys_pre_ref,
    state_ref, total_ref, ends_ref, out_ref,
):
    tokens, slots = pre_ref.shape
    depth = n_levels(tokens)
    width = keys_ref.shape[1]
    pre = pre_ref[...]
    decay = decay_write(pre)
    write = 1.0 - decay
    keys, values = keys_ref[...], values_ref[...]
    ends = ends_ref[...]
    ends_low = ends.astype(BF)
    tail = spans_ref[depth + 1]
    sent = (tail * write).astype(BF)
    column = tail * (dot_nt(keys, ends_low[:, :width]) + dot_nt(values, ends_low[:, width:]))
    glog = glog_ref[...] + dot_tn(span_matrix(depth + 1, tokens), (column * write).astype(BF))
    carried = lax.dot_general(
        jnp.ones((1, 2 * width), F32), ends * state_ref[...], (((1,), (1,)), ((), ())),
        precision=lax.Precision.HIGHEST, preferred_element_type=F32,
    )
    glog = glog + carried * total_ref[...]
    glog = glog - decay * (gwrite_ref[...] + column)
    u = query_pre_ref[...]
    s = sigmoid(u)
    out_ref[:, :width] = (gquery_ref[...] * (s * (1.0 + u * (1.0 - s)))).astype(BF)
    u = keys_pre_ref[...]
    s = sigmoid(u)
    gkeys = gkeys_ref[...] + dot_nn(sent, ends_low[:, :width])
    out_ref[:, width : 2 * width] = (gkeys * (s * (1.0 + u * (1.0 - s)))).astype(BF)
    out_ref[:, 2 * width : 3 * width] = (gvalues_ref[...] + dot_nn(sent, ends_low[:, width:])).astype(BF)
    out_ref[:, 3 * width : 4 * width] = ggate_ref[...]
    gforget = glog * sigmoid(-pre) / GATE_NORM
    room = out_ref.shape[1] - 4 * width - slots
    out_ref[:, 4 * width :] = jnp.concatenate(
        [gforget.astype(BF), jnp.zeros((tokens, room), BF)], axis=1
    )


def run_finish(gquery, gkeys, gvalues, ggate, gwrite, glog, keys, values, pre, spans, query_pre, keys_pre, state, total, ends):
    tokens, slots = pre.shape
    width = keys.shape[1]
    return pl.pallas_call(
        finish_kernel,
        out_shape=jax.ShapeDtypeStruct((tokens, 4 * width + 128), BF),
        name="slot_finish",
    )(gquery, gkeys, gvalues, ggate, gwrite, glog, keys, values, pre, spans, query_pre, keys_pre, state, total, ends)


MESH = pl.DeviceIdType.MESH


def greet(axes_of_peers):
    barrier = pltpu.get_barrier_semaphore()
    for peer in axes_of_peers:
        pl.semaphore_signal(barrier, inc=1, device_id=peer, device_id_type=MESH)
    pl.semaphore_wait(barrier, len(axes_of_peers))


def tp_peers():
    count = lax.axis_size("tp")
    me = lax.axis_index("tp")
    return me, [lax.rem(me + k, count) for k in range(1, count)]


def sum_over_tp(partial_ref, landed, send_sems, recv_sems):
    me, peers = tp_peers()
    copies = []
    for k, peer in enumerate(peers):
        copy = pltpu.make_async_remote_copy(
            src_ref=partial_ref.at[peer],
            dst_ref=landed.at[k],
            send_sem=send_sems.at[k],
            recv_sem=recv_sems.at[k],
            device_id={"tp": peer},
            device_id_type=MESH,
        )
        copy.start()
        copies.append(copy)
    total = partial_ref[me].astype(F32)
    for k, copy in enumerate(copies):
        copy.wait()
        total = total + landed[k].astype(F32)
    return total


def spread_over_tp(rows_ref, full_ref, send_sems, recv_sems):
    me, peers = tp_peers()
    copies = []
    for k, peer in enumerate(peers):
        copy = pltpu.make_async_remote_copy(
            src_ref=rows_ref,
            dst_ref=full_ref.at[me],
            send_sem=send_sems.at[k],
            recv_sem=recv_sems.at[k],
            device_id={"tp": peer},
            device_id_type=MESH,
        )
        copy.start()
        copies.append(copy)
    full_ref[me] = rows_ref[...]
    for copy in copies:
        copy.wait()


def exchange_kernel(epilogue, n_in, n_rows, partial_ref, *refs):
    me, peers = tp_peers()
    inputs = refs[:n_in]
    full_ref = refs[n_in]
    outputs = refs[n_in + 1 : n_in + 1 + n_rows]
    landed, rows_ref, send_a, recv_a, send_b, recv_b = refs[n_in + 1 + n_rows :]
    greet([{"tp": peer} for peer in peers])
    total = sum_over_tp(partial_ref, landed, send_a, recv_a)
    epilogue(total, me, inputs, outputs, rows_ref)
    spread_over_tp(rows_ref, full_ref, send_b, recv_b)


def run_exchange(epilogue, name, collective_id, partial, inputs, row_outputs):
    tp = lax.axis_size("tp")
    tokens, columns = partial.shape
    share = tokens // tp
    partial = partial.reshape(tp, share, columns)
    outs = pl.pallas_call(
        functools.partial(exchange_kernel, epilogue, len(inputs), len(row_outputs)),
        out_shape=(jax.ShapeDtypeStruct((tp, share, columns), BF), *row_outputs),
        in_specs=[pl.BlockSpec(memory_space=pltpu.VMEM)] * (1 + len(inputs)),
        out_specs=tuple([pl.BlockSpec(memory_space=pltpu.VMEM)] * (1 + len(row_outputs))),
        scratch_shapes=[
            pltpu.VMEM((tp - 1, share, columns), BF),
            pltpu.VMEM((share, columns), BF),
            pltpu.SemaphoreType.DMA((tp - 1,)),
            pltpu.SemaphoreType.DMA((tp - 1,)),
            pltpu.SemaphoreType.DMA((tp - 1,)),
            pltpu.SemaphoreType.DMA((tp - 1,)),
        ],
        compiler_params=pltpu.CompilerParams(collective_id=collective_id, has_side_effects=True),
        name=name,
    )(partial, *inputs)
    return (outs[0].reshape(tokens, columns), *outs[1:])


def middle_epilogue(total, me, inputs, outputs, rows_ref):
    hidden_ref, gain_ref = inputs
    (branch_ref,) = outputs
    branch_ref[...] = total
    middle = hidden_ref[me].astype(F32) + total
    scale = lax.rsqrt(jnp.mean(middle * middle, axis=1, keepdims=True) + EPSILON)
    rows_ref[...] = (middle * scale * gain_ref[...]).astype(BF)


def result_epilogue(total, me, inputs, outputs, rows_ref):
    hidden_ref, branch_ref, teacher_out_ref, teacher_mix_ref, cotangent_ref, mask_ref, scale_ref = inputs
    output_ref, grad_ref, losses_ref = outputs
    branch = branch_ref[...]
    result = hidden_ref[me].astype(F32) + branch + total
    output_ref[...] = result.astype(BF)
    mask = mask_ref[me]
    gap = result - teacher_out_ref[me].astype(F32)
    gap_mix = branch - teacher_mix_ref[me].astype(F32)
    loss_out = jnp.sum(mask * (gap * gap), keepdims=True)
    loss_mix = jnp.sum(mask * (gap_mix * gap_mix), keepdims=True)
    lane = lax.broadcasted_iota(jnp.int32, (1, 128), 1)
    losses_ref[...] = jnp.where(lane == 0, loss_out, 0.0) + jnp.where(lane == 1, loss_mix, 0.0)
    grad = cotangent_ref[me].astype(F32) + scale_ref[...] * mask * gap
    grad_ref[...] = grad
    rows_ref[...] = grad.astype(BF)


def norm_back(grad, rows, gain):
    scale = lax.rsqrt(jnp.mean(rows * rows, axis=1, keepdims=True) + EPSILON)
    unit = rows * scale
    gain_grad = jnp.sum(grad * unit, axis=0, keepdims=True)
    inner = grad * gain
    return scale * (inner - unit * jnp.mean(unit * inner, axis=1, keepdims=True)), gain_grad


def branch_epilogue(total, me, inputs, outputs, rows_ref):
    hidden_ref, branch_ref, teacher_mix_ref, grad_ref, mask_ref, scale_ref, gain_ref = inputs
    grad_middle_ref, gain_grad_ref = outputs
    branch = branch_ref[...]
    part, gain_grad = norm_back(total, hidden_ref[me].astype(F32) + branch, gain_ref[...])
    gain_grad_ref[...] = gain_grad
    grad_middle = part + grad_ref[...]
    grad_middle_ref[...] = grad_middle
    gap_mix = branch - teacher_mix_ref[me].astype(F32)
    rows_ref[...] = (grad_middle + scale_ref[...] * mask_ref[me] * gap_mix).astype(BF)


def input_epilogue(total, me, inputs, outputs, rows_ref):
    hidden_ref, grad_middle_ref, gain_ref = inputs
    (gain_grad_ref,) = outputs
    part, gain_grad = norm_back(total, hidden_ref[me].astype(F32), gain_ref[...])
    gain_grad_ref[...] = gain_grad
    rows_ref[...] = (part + grad_middle_ref[...]).astype(BF)


def scatter_kernel(count, inner, *refs):
    sources, rows_ref = refs[:count], refs[count]
    targets, full_ref = refs[count + 1 : 2 * count + 1], refs[2 * count + 1]
    send_sems, recv_sems, send_b, recv_b = refs[2 * count + 2 :]
    shards, ctxs = lax.axis_size("shard"), lax.axis_size("ctx")
    devices = shards * ctxs
    me = lax.axis_index("shard") * ctxs + lax.axis_index("ctx")
    _, across = tp_peers()
    peers = [lax.rem(me + k, devices) for k in range(1, devices)]
    places = [{"shard": lax.div(peer, ctxs), "ctx": lax.rem(peer, ctxs)} for peer in peers]
    greet(places + [{"tp": peer} for peer in across])
    copies = []
    for k, (peer, place) in enumerate(zip(peers, places)):
        for i in range(count):
            copy = pltpu.make_async_remote_copy(
                src_ref=sources[i].at[peer],
                dst_ref=targets[i].at[me],
                send_sem=send_sems.at[i, k],
                recv_sem=recv_sems.at[i, k],
                device_id=place,
                device_id_type=MESH,
            )
            copy.start()
            copies.append(copy)
    for i in range(count):
        targets[i][me] = sources[i][me]
    spread_over_tp(rows_ref, full_ref, send_b, recv_b)
    for copy in copies:
        copy.wait()


def run_scatter(arrays, rows, name, collective_id):
    shards, ctxs, tp = lax.axis_size("shard"), lax.axis_size("ctx"), lax.axis_size("tp")
    devices = shards * ctxs
    count = len(arrays)
    tokens, columns = arrays[0].shape
    step = columns // devices
    blocks = [a.reshape(tokens, devices, step).transpose(1, 0, 2) for a in arrays]
    outs = pl.pallas_call(
        functools.partial(scatter_kernel, count, None),
        out_shape=(
            *[jax.ShapeDtypeStruct((devices, tokens, step), BF)] * count,
            jax.ShapeDtypeStruct((tp, *rows.shape), BF),
        ),
        in_specs=[pl.BlockSpec(memory_space=pltpu.VMEM)] * (count + 1),
        out_specs=tuple([pl.BlockSpec(memory_space=pltpu.VMEM)] * (count + 1)),
        scratch_shapes=[
            pltpu.SemaphoreType.DMA((count, devices - 1)),
            pltpu.SemaphoreType.DMA((count, devices - 1)),
            pltpu.SemaphoreType.DMA((tp - 1,)),
            pltpu.SemaphoreType.DMA((tp - 1,)),
        ],
        compiler_params=pltpu.CompilerParams(collective_id=collective_id, has_side_effects=True),
        name=name,
    )(*blocks, rows)
    return [o.reshape(devices * tokens, step) for o in outs[:count]] + [outs[count].reshape(tp * rows.shape[0], -1)]


def passed_along(value, axis, steps):
    count = lax.axis_size(axis)
    leading, last = (max(0, -steps), min(count, count - steps))
    return lax.ppermute(value, axis, [(source, source + steps) for source in range(leading, last)])


def relay(value, decay, axis, steps):
    carried = passed_along(value, axis, steps)
    for _ in range(lax.axis_size(axis) - 2):
        carried = passed_along(value + decay * carried, axis, steps)
    return carried


GROUPED = ("shard", "ctx")


def gathered(value):
    return lax.all_gather(value, GROUPED, axis=0, tiled=True)


def per_device(
    hidden_in,
    cotangent,
    teacher_out,
    teacher_mix,
    valid_mask,
    doc_start,
    attn_gain,
    w_query,
    w_key,
    w_value,
    w_forget,
    forget_bias,
    head_gain,
    w_outgate,
    w_out,
    mlp_gain,
    w_gate,
    w_up,
    w_down,
):
    tokens, features = hidden_in.shape
    devices = lax.axis_size(GROUPED)
    tp = lax.axis_size("tp")
    share = tokens // tp
    rows = w_query.shape[0]
    width = w_query.shape[1]
    slots = w_forget.shape[1]
    units = w_gate.shape[1]
    tokens_all = tokens * devices
    mask_flat = valid_mask.astype(F32)

    def column(vector):
        flat = vector.reshape(-1, 1).astype(BF)
        return jnp.pad(flat, ((0, rows - flat.shape[0]), (0, 0)))

    count_own = jnp.sum(mask_flat).reshape(1)
    extras = jnp.concatenate(
        [column(attn_gain), column(mlp_gain), column(forget_bias), column(head_gain), column(count_own)], axis=1
    )
    extras = jnp.pad(extras, ((0, 0), (0, 128 - slots - extras.shape[1])))
    first = gathered(jnp.concatenate([w_query, w_key, w_value, w_outgate, w_forget, extras], axis=1))
    pack = jnp.concatenate([w_out, w_gate, w_up, w_down], axis=1)
    pack, first = lax.optimization_barrier((pack, first))
    second = gathered(pack)

    spare = first[:, 4 * width + slots :].astype(F32)
    attn_scale = spare[:, 0].reshape(1, -1)
    mlp_scale = spare[:, 1].reshape(1, -1)
    bias = spare[:, 2].reshape(devices, rows)[:, : slots // devices].reshape(1, slots)
    head_scale = spare[:, 3].reshape(devices, rows)[:, : width // devices].reshape(1, width)
    count_total = jnp.sum(spare[:, 4].reshape(devices, rows)[:, 0])
    loss_scale = (tokens_all / count_total).reshape(1, 1)

    hidden_f = hidden_in.astype(F32)
    scale = lax.rsqrt(jnp.mean(hidden_f * hidden_f, axis=-1, keepdims=True) + EPSILON)
    normed_in = (hidden_f * scale * attn_scale).astype(BF)
    pre_all = dot_nn(normed_in, first)
    query_pre = pre_all[:, :width]
    keys_pre = pre_all[:, width : 2 * width]
    query = jax.nn.silu(query_pre).astype(BF)
    keys = jax.nn.silu(keys_pre).astype(BF)
    values = pre_all[:, 2 * width : 3 * width].astype(BF)
    gate_pre = pre_all[:, 3 * width : 4 * width]
    forget_pre = pre_all[:, 4 * width : 4 * width + slots] + bias
    resets = doc_start.astype(F32)[:, None]

    spans, total, ends = run_ends(forget_pre, resets, keys, values)
    decay = total.reshape(slots, 1)
    state = relay(ends, decay, "ctx", 1)
    probs, pairs, mixing, mix, gated = run_forward(
        query, keys, values, forget_pre, spans, state, gate_pre, head_scale
    )
    out_w = second[:, :width]
    gate_w = second[:, width : width + units]
    up_w = second[:, width + units : width + 2 * units]
    down_w = second[:, width + 2 * units :]

    by_share = lambda tensor: tensor.reshape(tp, share, -1)
    hidden_s, teacher_out_s, teacher_mix_s, cotangent_s = map(by_share, (hidden_in, teacher_out, teacher_mix, cotangent))
    mask_s = by_share(mask_flat)
    narrow = lambda *shape: jax.ShapeDtypeStruct(shape, F32)

    normed_mid, branch = run_exchange(
        middle_epilogue, "sum_branch", 1, dot_nt(gated, out_w).astype(BF), (hidden_s, mlp_scale),
        (narrow(share, features),),
    )
    gate_val = dot_nn(normed_mid, gate_w)
    up_val = dot_nn(normed_mid, up_w)
    hidden_units = (jax.nn.silu(gate_val) * up_val).astype(BF)
    forward_all = gathered(jnp.concatenate([gated, hidden_units], axis=1))
    grad_mlp, output_rows, grad_result, losses = run_exchange(
        result_epilogue, "sum_result", 2, dot_nt(hidden_units, down_w).astype(BF),
        (hidden_s, branch, teacher_out_s, teacher_mix_s, cotangent_s, mask_s, loss_scale),
        (jax.ShapeDtypeStruct((share, features), BF), narrow(share, features), narrow(1, 128)),
    )
    grad_units = dot_nn(grad_mlp, down_w)
    gate_sig = jax.nn.sigmoid(gate_val)
    grad_gate_val = (grad_units * up_val * (gate_sig * (1.0 + gate_val * (1.0 - gate_sig)))).astype(BF)
    grad_up_val = (grad_units * (gate_val * gate_sig)).astype(BF)
    grad_both = jnp.concatenate([grad_gate_val, grad_up_val], axis=1)
    mlp_all = gathered(grad_both)
    grad_branch, grad_middle, mlp_gain_part = run_exchange(
        branch_epilogue, "sum_middle", 3, dot_nt(grad_both, second[:, width : width + 2 * units]).astype(BF),
        (hidden_s, branch, teacher_mix_s, grad_result, mask_s, loss_scale, mlp_scale),
        (narrow(share, features), narrow(1, features)),
    )
    grad_gated = dot_nn(grad_branch, out_w)
    gquery, gkeys, gvalues, ggate, head_gain_part, gwrite, glog, carry = run_backward(
        grad_gated, query, keys, values, forget_pre, spans, state, gate_pre, head_scale, probs, pairs, mixing, mix
    )
    later = relay(carry, decay, "ctx", -1)
    grad_pre = run_finish(
        gquery, gkeys, gvalues, ggate, gwrite, glog, keys, values, forget_pre, spans, query_pre, keys_pre,
        state, total, later,
    )
    attn_all = gathered(grad_pre)
    grad_in, attn_gain_part = run_exchange(
        input_epilogue, "sum_input", 4, dot_nt(grad_pre, first).astype(BF), (hidden_s, grad_middle, attn_scale),
        (narrow(1, features),),
    )
    normed_in_c, normed_mid_c, grad_mlp_c, grad_branch_c, output = run_scatter(
        (normed_in, normed_mid, grad_mlp, grad_branch), output_rows, "spread_rows", 5
    )
    gate_grad = dot_tn(normed_mid_c, mlp_all[:, :units])
    up_grad = dot_tn(normed_mid_c, mlp_all[:, units:])
    out_grad = dot_tn(grad_branch_c, forward_all[:, :width])
    down_grad = dot_tn(grad_mlp_c, forward_all[:, width:])
    query_grad = dot_tn(normed_in_c, attn_all[:, :width])
    keys_grad = dot_tn(normed_in_c, attn_all[:, width : 2 * width])
    values_grad = dot_tn(normed_in_c, attn_all[:, 2 * width : 3 * width])
    outgate_grad = dot_tn(normed_in_c, attn_all[:, 3 * width : 4 * width])
    forget_all = attn_all[:, 4 * width : 4 * width + slots]
    forget_grad = dot_tn(normed_in_c, forget_all)
    index = lax.axis_index(GROUPED)
    bias_grad = jnp.sum(forget_all.astype(F32), axis=0, keepdims=True)
    bias_grad = lax.dynamic_slice_in_dim(bias_grad, index * (slots // devices), slots // devices, axis=1)

    head_slots = jnp.where(jnp.arange(tp)[:, None] == lax.axis_index("tp"), head_gain_part, 0.0)
    packed = jnp.concatenate(
        [attn_gain_part.reshape(-1), mlp_gain_part.reshape(-1), head_slots.reshape(-1), losses.reshape(-1)]
    )
    packed = lax.psum(packed, ("shard", "ctx", "tp"))
    cut = lambda vector, size: lax.dynamic_slice_in_dim(vector, index * size, size)
    attn_gain_grad = cut(packed[:features], features // devices)
    mlp_gain_grad = cut(packed[features : 2 * features], features // devices)
    head_all = packed[2 * features : 2 * features + tp * width].reshape(tp, width)
    head_row = lax.dynamic_slice_in_dim(head_all, lax.axis_index("tp"), 1, axis=0)
    head_gain_grad = lax.dynamic_slice_in_dim(head_row, index * (width // devices), width // devices, axis=1)
    sums = packed[2 * features + tp * width :]
    loss_out = sums[0] / (2.0 * features * count_total)
    loss_mix = sums[1] / (2.0 * features * count_total)
    return (
        output,
        loss_out,
        loss_mix,
        grad_in.astype(F32),
        attn_gain_grad,
        query_grad,
        keys_grad,
        values_grad,
        forget_grad,
        bias_grad,
        head_gain_grad,
        outgate_grad,
        out_grad,
        mlp_gain_grad,
        gate_grad,
        up_grad,
        down_grad,
    )


def solution(mesh):
    return jax.shard_map(
        per_device,
        mesh=mesh,
        in_specs=(
            P(("shard", "ctx"), None),
            P(("shard", "ctx"), None),
            P(("shard", "ctx"), None),
            P(("shard", "ctx"), None),
            P(("shard", "ctx")),
            P(("shard", "ctx")),
            P(("shard", "ctx")),
            P(("shard", "ctx"), "tp"),
            P(("shard", "ctx"), "tp"),
            P(("shard", "ctx"), "tp"),
            P(("shard", "ctx"), "tp"),
            P("tp", ("shard", "ctx")),
            P("tp", ("shard", "ctx")),
            P(("shard", "ctx"), "tp"),
            P(("shard", "ctx"), "tp"),
            P(("shard", "ctx")),
            P(("shard", "ctx"), "tp"),
            P(("shard", "ctx"), "tp"),
            P(("shard", "ctx"), "tp"),
        ),
        out_specs=(
            P(("shard", "ctx"), None),
            P(),
            P(),
            P(("shard", "ctx"), None),
            P(("shard", "ctx")),
            P(("shard", "ctx"), "tp"),
            P(("shard", "ctx"), "tp"),
            P(("shard", "ctx"), "tp"),
            P(("shard", "ctx"), "tp"),
            P("tp", ("shard", "ctx")),
            P("tp", ("shard", "ctx")),
            P(("shard", "ctx"), "tp"),
            P(("shard", "ctx"), "tp"),
            P(("shard", "ctx")),
            P(("shard", "ctx"), "tp"),
            P(("shard", "ctx"), "tp"),
            P(("shard", "ctx"), "tp"),
        ),
        check_vma=False,
    )
```

time: 1490 us -> 638 us (0.43)
  waiting for transfers between devices: 853 us -> 138 us
  Pallas kernels: 0 us -> 306 us
  matrix products: 245 us -> 79.2 us
  other arithmetic: 139 us -> 14.9 us
  local copies, waits for them, and re-layouts: 108 us -> 24.7 us
  blocking collectives: 81.3 us -> 45 us
  loops' own time: 23.3 us -> 0 us
    reduce_scatter x9 -> x0, waiting for transfers between devices: 552 us -> none  [the longest x1 91.2 us: per_device(): lax.psum_scatter(gate_grad, ('shard', 'ctx'), scatter_dimension=0, tiled=...]
    pallas_call x0 -> x9, Pallas kernels: none -> 306 us  [the longest x4 205 us: run_exchange(): pl.pallas_call(functools.partial(exchange_kernel, epilogue, len(inputs),...]
    dot_general x171 -> x18, matrix products: 245 us -> 79.2 us  [the longest x9 32 us: dot_tn(): lax.dot_general(a, b, (((0,), (0,)), ((), ())), preferred_element_type=F32)]
    psum x4 -> x0, waiting for transfers between devices: 159 us -> none  [the longest x1 58.9 us: per_device(): branch = lax.psum(project_back(gated_bf, out_w), 'tp')]
    squeeze x100 -> x0, local copies, waits for them, and re-layouts: 52.9 us -> none  [the longest x76 50.1 us: end_states(): final, _ = lax.scan(jax.checkpoint(end_block), start, pieces)]
    another operation x89 -> x0, other arithmetic: 34.5 us -> none  [the longest x44 17.5 us: group_tail(): cum_log = jnp.cumsum(log_decay, axis=1)]
    all_gather x3 -> x0, blocking collectives: 28.9 us -> none  [the longest x1 10.4 us: per_device(): lax.all_gather(attn_gain, ('shard', 'ctx'), axis=0, tiled=True)]
    reduce_sum x44 -> x4, other arithmetic: 32.4 us -> 3.52 us  [the longest x1 1.33 us: per_device(): bias_grad = jnp.sum(forget_all.astype(F32), axis=0, keepdims=True)]
  transfers between devices with their start and end apart: 26 -> 7, of which waited for: 18 -> 4; matrix products, arithmetic and copies ran while one was open for 21% -> 13% of each run, Pallas kernels for 0% -> 41%
where the time goes in v1:
time: 638 us; the launch traced here: 631 us
  Pallas kernels  306 us (48%)
  waiting for transfers between devices  138 us (22%)
  matrix products  79.2 us (12%)
  blocking collectives  45 us (7%)
  local copies, waits for them, and re-layouts  24.7 us (4%)
  between operations  19.5 us (3%)
  other arithmetic  14.9 us (2%)
    pallas_call x4, Pallas kernels, run_exchange(): pl.pallas_call(functools.partial(exchange_kernel, epilogue, len(inputs),...  205 us
    all_gather x5, waiting for transfers between devices, gathered(): return lax.all_gather(value, GROUPED, axis=0, tiled=True)  135 us
    pallas_call x1, Pallas kernels, run_scatter(): pl.pallas_call(functools.partial(scatter_kernel, count, None), out_shape=...  73.2 us
    psum x1, blocking collectives, per_device(): packed = lax.psum(packed, ('shard', 'ctx', 'tp'))  45 us
    dot_general x9, matrix products, dot_tn(): lax.dot_general(a, b, (((0,), (0,)), ((), ())), preferred_element_type=F32)  32 us
    dot_general x4, matrix products, dot_nt(): lax.dot_general(a, b, (((1,), (1,)), ((), ())), preferred_element_type=F32)  24.4 us
    dot_general x5, matrix products, dot_nn(): lax.dot_general(a, b, (((1,), (0,)), ((), ())), preferred_element_type=F32)  22.8 us
  transfers between devices with their start and end apart: 7, of which 4 were waited for; matrix products, arithmetic and copies ran while one was open for 13% of the time, Pallas kernels for 41%

profile of v1, /device:TPU:0, one launch (start us, length us, event | category | flops | bytes accessed | tf_op | source)
XLA Modules:
  0.0 630.6 jit_solution(6814623653888800635)
XLA Ops:
  7.3 1.0 copy.39
  8.3 0.7 reshape.144
  9.0 0.7 reshape.145
  9.6 0.7 pad.16
  10.3 0.7 pad.17
  10.9 1.3 convert_reduce_fusion.1
  12.2 0.6 pad.18
  13.1 3.2 concatenate.20
  16.4 1.6 pad_maximum_fusion
  18.0 57.7 %all-gather.6.cloned.1.call-done = bf16[2048,2176]{1,0:T(8,128)(2,1)} async-done(((bf16[256,2176]{1,0:T(8,128)(2,1)}), bf16[2048,2176]{1,0:T(8,128)(2,1)}) %all-gather.6.cloned.1.call-update) | async-done | bytes 8912912 | tf_op jit(solution)/shard_map/all_gather | solution.py:573
  76.3 0.8 copy.42.resets_ref
  77.4 1.4 slice_convert_fusion.1
  78.8 2.5 slice_reduce_fusion
  81.7 2.6 fusion.44
  84.4 0.7 slice.216.values_ref
  85.2 0.7 slice_add_fusion.pre_ref
  85.9 1.4 fusion.41
  87.3 3.7 slot_ends.1
  90.9 2.4 collective-permute-start
  93.3 0.7 reshape.149.gain_ref
  94.4 0.7 copy-done.3
  95.2 6.4 %slot_forward.1 = (f32[256,64]{1,0:T(8,128)}, f32[256,256]{1,0:T(8,128)}, bf16[256,256]{1,0:T(8,128)(2,1)}, f32[256,512]{1,0:T(8,128)}, bf16[256,512]{1,0:T(8,128)(2,1)}) custom-call(bf16[256,512]{1,0:T(8,128)(2,1)} %get-tuple-element.93.query_ref, bf16[256,512]{1,0:T(8,128)(2,1)} %get-tuple-element.94.keys_ref, bf16[256,512]{1,0:T(8,128)(2,1)} %slice.216.values_ref, ...), custom_call_target="tpu_custom_call" | custom-call | tf_op jit(solution)/shard_map/slot_forward/pallas_call | solution.py:166
  101.5 76.9 %all-gather.8.cloned.1.call-done = bf16[2048,4736]{1,0:T(8,128)(2,1)} async-done(((bf16[256,4736]{1,0:T(8,128)(2,1)}), bf16[2048,4736]{1,0:T(8,128)(2,1)}) %all-gather.8.cloned.1.call-update) | async-done | bytes 19398672 | tf_op jit(solution)/shard_map/all_gather | solution.py:573
  178.4 3.4 convolution_convert_fusion
  181.8 48.2 %sum_branch.1 = (bf16[4,64,2048]{2,1,0:T(8,128)(2,1)}, f32[64,2048]{1,0:T(8,128)}) custom-call(bf16[4,64,2048]{2,1,0:T(8,128)(2,1)} %bitcast.101, bf16[4,64,2048]{2,1,0:T(8,128)(2,1)} %bitcast.74, f32[1,2048]{1,0:T(1,128)} %bitcast.106), custom_call_target="tpu_custom_call" | custom-call | tf_op jit(solution)/shard_map/sum_branch/pallas_call | solution.py:424
  230.0 4.8 fusion.10
  234.9 6.1 multiply_convert_fusion.2
  241.0 1.0 pad_maximum_fusion.2
  242.5 0.9 reshape.173.refs_5_.refs_4_
  243.4 0.6 slice_reduce_fusion.5
  244.7 5.4 fusion.19
  250.1 54.4 %sum_result.1 = (bf16[4,64,2048]{2,1,0:T(8,128)(2,1)}, bf16[64,2048]{1,0:T(8,128)(2,1)}, f32[64,2048]{1,0:T(8,128)}, f32[1,128]{1,0:T(1,128)}) custom-call(bf16[4,64,2048]{2,1,0:T(8,128)(2,1)} %bitcast.104, bf16[4,64,2048]{2,1,0:T(8,128)(2,1)} %bitcast.75, f32[64,2048]{1,0:T(8,128)} %get-tuple-element.57.refs_1_, bf16[4,64,2048]{2,1,0:T(8,128)(2,1)} %bitcast.102, ...), custom_call_target="tpu_custom_call" | custom-call | tf_op jit(solution)/shard_map/sum_result/pallas_call | solution.py:424
  304.5 5.8 multiply_convert_fusion.1
  310.3 8.4 %fusion.16 = bf16[256,2048]{1,0:T(8,128)(2,1)} fusion(bf16[2048,4736]{1,0:T(8,128)(2,1)} %all-gather.8.cloned.1.call-done, bf16[256,1408]{1,0:T(8,128)(2,1)S(1)} %get-tuple-element.91, bf16[256,1408]{1,0:T(8,128)(2,1)S(1)} %get-tuple-element.90), kind=kOutput, calls=%fused_computation.18 | convolution fusion | flops 2956197888 | bytes 14024704 | tf_op jit(solution)/shard_map/dot_general | solution.py:21
  318.8 53.5 %sum_middle.1 = (bf16[4,64,2048]{2,1,0:T(8,128)(2,1)}, f32[64,2048]{1,0:T(8,128)}, f32[1,2048]{1,0:T(1,128)}) custom-call(bf16[4,64,2048]{2,1,0:T(8,128)(2,1)} %bitcast.86, bf16[4,64,2048]{2,1,0:T(8,128)(2,1)} %bitcast.76, f32[64,2048]{1,0:T(8,128)} %get-tuple-element.57.refs_1_, bf16[4,64,2048]{2,1,0:T(8,128)(2,1)} %bitcast.82, ...), custom_call_target="tpu_custom_call" | custom-call | tf_op jit(solution)/shard_map/sum_middle/pallas_call | solution.py:424
  372.3 3.4 fusion.35.grad_ref
  375.7 12.3 %slot_backward.1 = (f32[256,512]{1,0:T(8,128)}, f32[256,512]{1,0:T(8,128)}, f32[256,512]{1,0:T(8,128)}, bf16[256,512]{1,0:T(8,128)(2,1)}, f32[1,512]{1,0:T(1,128...) custom-call(f32[256,512]{1,0:T(8,128)} %fusion.35.grad_ref, ...), custom_call_target="tpu_custom_call" | custom-call | tf_op jit(solution)/shard_map/slot_backward/pallas_call | solution.py:288
  388.0 1.3 collective-permute-start.1
  389.3 2.5 collective-permute-done.1.ends_ref
  391.7 4.9 slot_finish.1
  396.7 1.2 pad_maximum_fusion.1
  397.9 1.3 copy.41
  400.3 1.2 copy.56
  402.1 1.8 copy_bitcast_fusion
  403.9 73.2 %spread_rows.1 = (bf16[8,256,256]{2,1,0:T(8,128)(2,1)}, bf16[8,256,256]{2,1,0:T(8,128)(2,1)}, bf16[8,256,256]{2,1,0:T(8,128)(2,1)}, bf16[8,256,256]{2,1,0:T(8,128)(2,1)}, bf16[4,64,2048]{2,1,0:T(8,128)(2,1)}) custom-call(bf16[8,256,256]{2,1,0:T(8,128)(2,1)} %bitcast.79, bf16[8,256,256]{2,1,0:T(8,128)(2,1)} %bitcast.80, ...), custom_call_target="tpu_custom_call" | custom-call | tf_op jit(solution)/shard_map/spread_rows/pallas_call | solution.py:536
  477.2 7.2 %convolution_convert_fusion.1 = bf16[256,2048]{1,0:T(8,128)(2,1)} fusion(bf16[256,2176]{1,0:T(8,128)(2,1)S(1)} %copy-done.2, bf16[2048,2176]{1,0:T(8,128)(2,1)} %all-gather.6.cloned.1.call-done), kind=kOutput, calls=%fused_computation.21 | convolution fusion | flops 2282225664 | bytes 11075584 | tf_op jit(solution)/shard_map/dot_general | solution.py:21
  484.4 49.0 %sum_input.1 = (bf16[4,64,2048]{2,1,0:T(8,128)(2,1)}, f32[1,2048]{1,0:T(1,128)}) custom-call(bf16[4,64,2048]{2,1,0:T(8,128)(2,1)} %bitcast.100, bf16[4,64,2048]{2,1,0:T(8,128)(2,1)} %bitcast.77, f32[64,2048]{1,0:T(8,128)} %get-tuple-element.75.refs_1_, f32[1,2048]{1,0:T(1,128)} %bitcast.105), custom_call_target="tpu_custom_call" | custom-call | tf_op jit(solution)/shard_map/sum_input/pallas_call | solution.py:424
  533.5 0.8 pad_maximum_fusion.3
  534.3 45.0 %psum.7 = f32[6272]{0:T(1024)S(1)} all-reduce(f32[6272]{0:T(1024)S(1)} %pad_maximum_fusion.3), channel_id=1, replica_groups=mesh['shard'=4,'ctx'=2,'tp'=4] {'shard','ctx','tp'}, use_global_device_ids=true, to_apply=%region_3.4 | all-reduce | flops 6272 | bytes 50176 | tf_op jit(solution)/shard_map/psum | solution.py:718
  581.2 0.6 dynamic_slice.13
  581.9 0.6 dynamic_slice.16
  583.1 2.8 bitcast_convert_fusion
  585.9 3.2 fusion.25
  589.1 5.7 fusion.2
  594.8 1.3 convert_reduce_fusion
  596.7 2.0 fusion.39
  598.6 3.1 fusion.33
  601.8 3.1 fusion.31
  604.9 3.1 fusion.29
  608.0 3.2 fusion.27
  611.2 5.7 fusion.6
  616.9 0.8 copy-done.20
  617.7 2.9 fusion.4
  620.6 1.0 copy.58
  (88 shorter events, 5.5 us)
Async XLA Ops:
  7.2 9.2 %copy-start.9 = (bf16[256,1408]{1,0:T(8,128)(2,1)S(1)}, bf16[256,1408]{1,0:T(8,128)(2,1)}, u32[]{:S(2)}) copy-start(bf16[256,1408]{1,0:T(8,128)(2,1)} %param.37) | copy-start | bytes 2162692
  7.2 9.2 %copy-start.10 = (bf16[256,1408]{1,0:T(8,128)(2,1)S(1)}, bf16[256,1408]{1,0:T(8,128)(2,1)}, u32[]{:S(2)}) copy-start(bf16[256,1408]{1,0:T(8,128)(2,1)} %param.36) | copy-start | bytes 2162692
  7.2 9.2 %copy-start.11 = (bf16[256,1408]{1,0:T(8,128)(2,1)S(1)}, bf16[256,1408]{1,0:T(8,128)(2,1)}, u32[]{:S(2)}) copy-start(bf16[256,1408]{1,0:T(8,128)(2,1)} %param.35) | copy-start | bytes 2162692
  7.2 9.2 %copy-start.12 = (bf16[256,512]{1,0:T(8,128)(2,1)S(1)}, bf16[256,512]{1,0:T(8,128)(2,1)}, u32[]{:S(2)}) copy-start(bf16[256,512]{1,0:T(8,128)(2,1)} %param.33) | copy-start | bytes 786436
  7.2 68.5 %all-gather.6.cloned.1.call-start = ((), (), s32[]{:S(2)}) async-start(), calls=%async_computation | async-start | bytes 10027008 | tf_op jit(solution)/shard_map/all_gather | solution.py:573
  16.3 162.1 %all-gather.8.cloned.1.call-start = ((), (), s32[]{:S(2)}) async-start(), calls=%async_computation.1 | async-start | bytes 21823488 | tf_op jit(solution)/shard_map/all_gather | solution.py:573
  18.0 57.7 %copy-start = (bf16[256,2048]{1,0:T(8,128)(2,1)S(1)}, bf16[256,2048]{1,0:T(8,128)(2,1)}, u32[]{:S(2)}) copy-start(bf16[256,2048]{1,0:T(8,128)(2,1)} %param.19) | copy-start | bytes 3145732
  18.0 58.3 %copy-start.17 = (s32[256]{0:T(256)S(1)}, s32[256]{0:T(256)}, u32[]{:S(2)}) copy-start(s32[256]{0:T(256)} %param.24) | copy-start | bytes 3076
  75.7 510.2 %all-gather.12.cloned.1.call-start = ((), (), s32[]{:S(2)}) async-start(), calls=%async_computation.3 | async-start | bytes 8847360 | tf_op jit(solution)/shard_map/all_gather | solution.py:573
  77.4 4.3 copy-start.1
  81.4 3.0 copy-start.14
  90.9 3.5 collective-permute-start
  94.4 0.7 copy-start.3
  230.0 4.8 copy-start.4
  234.9 6.1 copy-start.24
  234.9 6.1 copy-start.13
  241.0 1.5 copy-start.18
  242.0 352.7 %all-gather.10.cloned.1.call-start = ((), (), s32[]{:S(2)}) async-start(), calls=%async_computation.2 | async-start | bytes 10027008 | tf_op jit(solution)/shard_map/all_gather | solution.py:573
  388.0 3.8 collective-permute-start.1
  396.6 214.5 %all-gather.14.cloned.1.call-start = ((), (), s32[]{:S(2)}) async-start(), calls=%async_computation.4 | async-start | bytes 12976128 | tf_op jit(solution)/shard_map/all_gather | solution.py:573
  399.2 2.2 copy-start.6
  400.3 1.5 copy-start.5
  403.9 73.3 %copy-start.16 = (f32[1,512]{1,0:T(1,128)S(1)}, f32[1,512]{1,0:T(1,128)}, u32[]{:S(2)}) copy-start(f32[1,512]{1,0:T(1,128)} %get-tuple-element.78) | copy-start | bytes 6148
  403.9 73.3 %copy-start.2 = (bf16[256,2176]{1,0:T(8,128)(2,1)S(1)}, bf16[256,2176]{1,0:T(8,128)(2,1)}, u32[]{:S(2)}) copy-start(bf16[256,2176]{1,0:T(8,128)(2,1)} %slot_finish.1) | copy-start | bytes 3342340
  484.4 49.0 %copy-start.15 = (f32[1,2048]{1,0:T(1,128)S(1)}, f32[1,2048]{1,0:T(1,128)}, u32[]{:S(2)}) copy-start(f32[1,2048]{1,0:T(1,128)} %get-tuple-element.77) | copy-start | bytes 24580
  484.4 49.0 %copy-start.19 = (f32[1,128]{1,0:T(1,128)S(1)}, f32[1,128]{1,0:T(1,128)}, u32[]{:S(2)}) copy-start(f32[1,128]{1,0:T(1,128)} %get-tuple-element.79) | copy-start | bytes 1540
  533.4 52.4 %copy-start.23 = (bf16[8,256,256]{2,1,0:T(8,128)(2,1)S(1)}, bf16[8,256,256]{2,1,0:T(8,128)(2,1)}, u32[]{:S(2)}) copy-start(bf16[8,256,256]{2,1,0:T(8,128)(2,1)} %get-tuple-element.82) | copy-start | bytes 3145732
  585.9 3.2 copy-start.22
  589.1 7.6 %copy-start.8 = (bf16[8,256,256]{2,1,0:T(8,128)(2,1)S(1)}, bf16[8,256,256]{2,1,0:T(8,128)(2,1)}, u32[]{:S(2)}) copy-start(bf16[8,256,256]{2,1,0:T(8,128)(2,1)} %get-tuple-element.81) | copy-start | bytes 3145732
  608.0 3.2 copy-start.21
  611.2 6.5 %copy-start.20 = (bf16[2048,2816]{1,0:T(8,128)(2,1)S(1)}, bf16[2048,2816]{1,0:T(8,128)(2,1)}, u32[]{:S(2)}) copy-start(bf16[2048,2816]{1,0:T(8,128)(2,1)} %all-gather.14.cloned.1.call-done) | copy-start | bytes 34603012
  617.7 2.9 copy-start.7
Sparse Core Ops, SparseCore 0:
  16.4 59.1 all-gather.5
  77.6 100.7 all-gather.7
  242.2 57.0 all-gather.11
  396.8 98.7 all-gather.9
  497.9 68.2 all-gather.13

commit v2 on v1

--- a/solution.py
+++ b/solution.py
@@ -349,6 +349,7 @@
 
 
 MESH = pl.DeviceIdType.MESH
+GROUPED = ("shard", "ctx")
 
 
 def greet(axes_of_peers):
@@ -404,40 +405,157 @@
         copy.wait()
 
 
-def exchange_kernel(epilogue, n_in, n_rows, partial_ref, *refs):
+def plane_peers():
+    shards, ctxs = lax.axis_size("shard"), lax.axis_size("ctx")
+    devices = shards * ctxs
+    me = lax.axis_index("shard") * ctxs + lax.axis_index("ctx")
+    peers = [lax.rem(me + k, devices) for k in range(1, devices)]
+    places = [{"shard": lax.div(peer, ctxs), "ctx": lax.rem(peer, ctxs)} for peer in peers]
+    return me, peers, places
+
+
+def start_scatter(sources, targets, send_sems, recv_sems):
+    me, peers, places = plane_peers()
+    copies = []
+    for i, (source, target) in enumerate(zip(sources, targets)):
+        step = target.shape[2]
+
+        def block(at):
+            if len(source.shape) == 3:
+                return source.at[at]
+            return source.at[:, pl.ds(pl.multiple_of(at * step, step), step)]
+
+        for k, (peer, place) in enumerate(zip(peers, places)):
+            copy = pltpu.make_async_remote_copy(
+                src_ref=block(peer),
+                dst_ref=target.at[me],
+                send_sem=send_sems.at[i, k],
+                recv_sem=recv_sems.at[i, k],
+                device_id=place,
+                device_id_type=MESH,
+            )
+            copy.start()
+            copies.append(copy)
+    for source, target in zip(sources, targets):
+        target[me] = block_of(source, me, target.shape[2])
+    return copies
+
+
+def block_of(source, at, step):
+    if len(source.shape) == 3:
+        return source[at]
+    return source[:, pl.ds(pl.multiple_of(at * step, step), step)]
+
+
+def start_sums(row_ref, landed, send_sems, recv_sems, peers, places, me):
+    copies = []
+    landed[me] = row_ref[...]
+    for k, place in enumerate(places):
+        copy = pltpu.make_async_remote_copy(
+            src_ref=row_ref,
+            dst_ref=landed.at[me],
+            send_sem=send_sems.at[k],
+            recv_sem=recv_sems.at[k],
+            device_id=place,
+            device_id_type=MESH,
+        )
+        copy.start()
+        copies.append(copy)
+    return copies
+
+
+def summed(landed):
+    total = landed[0]
+    for k in range(1, landed.shape[0]):
+        total = total + landed[k]
+    return total
+
+
+def exchange_kernel(epilogue, n_in, n_rows, n_moved, n_sums, partial_ref, *refs):
     me, peers = tp_peers()
-    inputs = refs[:n_in]
-    full_ref = refs[n_in]
-    outputs = refs[n_in + 1 : n_in + 1 + n_rows]
-    landed, rows_ref, send_a, recv_a, send_b, recv_b = refs[n_in + 1 + n_rows :]
-    greet([{"tp": peer} for peer in peers])
+    inputs, refs = refs[:n_in], refs[n_in:]
+    sources, refs = refs[:n_moved], refs[n_moved:]
+    full_ref, refs = refs[0], refs[1:]
+    outputs, refs = refs[:n_rows], refs[n_rows:]
+    targets, refs = refs[:n_moved], refs[n_moved:]
+    sums, refs = refs[: 2 * n_sums], refs[2 * n_sums :]
+    landed, rows_ref, send_a, recv_a, send_b, recv_b, send_m, recv_m = refs[:8]
+    own, plane, places = plane_peers()
+    across = [{"tp": peer} for peer in peers]
+    greet(across + (places if n_moved or n_sums else []))
+    moves = start_scatter(sources, targets, send_m, recv_m)
     total = sum_over_tp(partial_ref, landed, send_a, recv_a)
     epilogue(total, me, inputs, outputs, rows_ref)
+    if n_sums:
+        row_ref, in_plane, plane_row, in_tp, send_p, recv_p, send_t, recv_t = refs[8:]
+        width = outputs[0].shape[1]
+        row_ref[:, :width] = outputs[0][...]
+        row_ref[:, width:] = inputs[-1][...]
+        started = start_sums(row_ref, in_plane, send_p, recv_p, plane, places, own)
     spread_over_tp(rows_ref, full_ref, send_b, recv_b)
-
-
-def run_exchange(epilogue, name, collective_id, partial, inputs, row_outputs):
+    if n_sums:
+        for copy in started:
+            copy.wait()
+        plane_row[...] = summed(in_plane)
+        sums[0][...] = plane_row[...]
+        started = start_sums(plane_row, in_tp, send_t, recv_t, peers, across, me)
+        for copy in started:
+            copy.wait()
+        sums[1][...] = summed(in_tp)
+    for copy in moves:
+        copy.wait()
+
+
+def run_exchange(epilogue, name, collective_id, partial, inputs, row_outputs, moved=(), summing=False):
     tp = lax.axis_size("tp")
+    devices = lax.axis_size(GROUPED)
     tokens, columns = partial.shape
     share = tokens // tp
     partial = partial.reshape(tp, share, columns)
+    step = columns // devices
+    if step % 128:
+        moved = [m.reshape(tokens, devices, step).transpose(1, 0, 2) for m in moved]
+    count = len(moved)
+    scratch = [
+        pltpu.VMEM((tp - 1, share, columns), BF),
+        pltpu.VMEM((share, columns), BF),
+        *[pltpu.SemaphoreType.DMA((tp - 1,))] * 4,
+        *[pltpu.SemaphoreType.DMA((max(count, 1), devices - 1))] * 2,
+    ]
+    extra = ()
+    if summing:
+        row = row_outputs[0].shape[1] + inputs[-1].shape[1]
+        extra = (jax.ShapeDtypeStruct((1, row), F32),) * 2
+        scratch += [
+            pltpu.VMEM((1, row), F32),
+            pltpu.VMEM((devices, 1, row), F32),
+            pltpu.VMEM((1, row), F32),
+            pltpu.VMEM((tp, 1, row), F32),
+            *[pltpu.SemaphoreType.DMA((devices - 1,))] * 2,
+            *[pltpu.SemaphoreType.DMA((tp - 1,))] * 2,
+        ]
+    out_shape = (
+        jax.ShapeDtypeStruct((tp, share, columns), BF),
+        *row_outputs,
+        *[jax.ShapeDtypeStruct((devices, tokens, step), BF)] * count,
+        *extra,
+    )
     outs = pl.pallas_call(
-        functools.partial(exchange_kernel, epilogue, len(inputs), len(row_outputs)),
-        out_shape=(jax.ShapeDtypeStruct((tp, share, columns), BF), *row_outputs),
-        in_specs=[pl.BlockSpec(memory_space=pltpu.VMEM)] * (1 + len(inputs)),
-        out_specs=tuple([pl.BlockSpec(memory_space=pltpu.VMEM)] * (1 + len(row_outputs))),
-        scratch_shapes=[
-            pltpu.VMEM((tp - 1, share, columns), BF),
-            pltpu.VMEM((share, columns), BF),
-            pltpu.SemaphoreType.DMA((tp - 1,)),
-            pltpu.SemaphoreType.DMA((tp - 1,)),
-            pltpu.SemaphoreType.DMA((tp - 1,)),
-            pltpu.SemaphoreType.DMA((tp - 1,)),
-        ],
+        functools.partial(exchange_kernel, epilogue, len(inputs), len(row_outputs), count, int(summing)),
+        out_shape=out_shape,
+        in_specs=[pl.BlockSpec(memory_space=pltpu.VMEM)] * (1 + len(inputs) + count),
+        out_specs=tuple([pl.BlockSpec(memory_space=pltpu.VMEM)] * len(out_shape)),
+        scratch_shapes=scratch,
         compiler_params=pltpu.CompilerParams(collective_id=collective_id, has_side_effects=True),
         name=name,
-    )(partial, *inputs)
-    return (outs[0].reshape(tokens, columns), *outs[1:])
+    )(partial, *inputs, *moved)
+    start = 1 + len(row_outputs)
+    return (
+        outs[0].reshape(tokens, columns),
+        *outs[1:start],
+        *[o.reshape(devices * tokens, step) for o in outs[start : start + count]],
+        *outs[start + count :],
+    )
 
 
 def middle_epilogue(total, me, inputs, outputs, rows_ref):
@@ -488,69 +606,11 @@
 
 
 def input_epilogue(total, me, inputs, outputs, rows_ref):
-    hidden_ref, grad_middle_ref, gain_ref = inputs
+    hidden_ref, grad_middle_ref, gain_ref = inputs[:3]
     (gain_grad_ref,) = outputs
     part, gain_grad = norm_back(total, hidden_ref[me].astype(F32), gain_ref[...])
     gain_grad_ref[...] = gain_grad
     rows_ref[...] = (part + grad_middle_ref[...]).astype(BF)
-
-
-def scatter_kernel(count, inner, *refs):
-    sources, rows_ref = refs[:count], refs[count]
-    targets, full_ref = refs[count + 1 : 2 * count + 1], refs[2 * count + 1]
-    send_sems, recv_sems, send_b, recv_b = refs[2 * count + 2 :]
-    shards, ctxs = lax.axis_size("shard"), lax.axis_size("ctx")
-    devices = shards * ctxs
-    me = lax.axis_index("shard") * ctxs + lax.axis_index("ctx")
-    _, across = tp_peers()
-    peers = [lax.rem(me + k, devices) for k in range(1, devices)]
-    places = [{"shard": lax.div(peer, ctxs), "ctx": lax.rem(peer, ctxs)} for peer in peers]
-    greet(places + [{"tp": peer} for peer in across])
-    copies = []
-    for k, (peer, place) in enumerate(zip(peers, places)):
-        for i in range(count):
-            copy = pltpu.make_async_remote_copy(
-                src_ref=sources[i].at[peer],
-                dst_ref=targets[i].at[me],
-                send_sem=send_sems.at[i, k],
-                recv_sem=recv_sems.at[i, k],
-                device_id=place,
-                device_id_type=MESH,
-            )
-            copy.start()
-            copies.append(copy)
-    for i in range(count):
-        targets[i][me] = sources[i][me]
-    spread_over_tp(rows_ref, full_ref, send_b, recv_b)
-    for copy in copies:
-        copy.wait()
-
-
-def run_scatter(arrays, rows, name, collective_id):
-    shards, ctxs, tp = lax.axis_size("shard"), lax.axis_size("ctx"), lax.axis_size("tp")
-    devices = shards * ctxs
-    count = len(arrays)
-    tokens, columns = arrays[0].shape
-    step = columns // devices
-    blocks = [a.reshape(tokens, devices, step).transpose(1, 0, 2) for a in arrays]
-    outs = pl.pallas_call(
-        functools.partial(scatter_kernel, count, None),
-        out_shape=(
-            *[jax.ShapeDtypeStruct((devices, tokens, step), BF)] * count,
-            jax.ShapeDtypeStruct((tp, *rows.shape), BF),
-        ),
-        in_specs=[pl.BlockSpec(memory_space=pltpu.VMEM)] * (count + 1),
-        out_specs=tuple([pl.BlockSpec(memory_space=pltpu.VMEM)] * (count + 1)),
-        scratch_shapes=[
-            pltpu.SemaphoreType.DMA((count, devices - 1)),
-            pltpu.SemaphoreType.DMA((count, devices - 1)),
-            pltpu.SemaphoreType.DMA((tp - 1,)),
-            pltpu.SemaphoreType.DMA((tp - 1,)),
-        ],
-        compiler_params=pltpu.CompilerParams(collective_id=collective_id, has_side_effects=True),
-        name=name,
-    )(*blocks, rows)
-    return [o.reshape(devices * tokens, step) for o in outs[:count]] + [outs[count].reshape(tp * rows.shape[0], -1)]
 
 
 def passed_along(value, axis, steps):
@@ -564,9 +624,6 @@
     for _ in range(lax.axis_size(axis) - 2):
         carried = passed_along(value + decay * carried, axis, steps)
     return carried
-
-
-GROUPED = ("shard", "ctx")
 
 
 def gathered(value):
@@ -614,11 +671,14 @@
         [column(attn_gain), column(mlp_gain), column(forget_bias), column(head_gain), column(count_own)], axis=1
     )
     extras = jnp.pad(extras, ((0, 0), (0, 128 - slots - extras.shape[1])))
-    first = gathered(jnp.concatenate([w_query, w_key, w_value, w_outgate, w_forget, extras], axis=1))
-    pack = jnp.concatenate([w_out, w_gate, w_up, w_down], axis=1)
+    first = gathered(jnp.concatenate([w_query, w_key, w_value, w_outgate, w_forget, extras, w_out], axis=1))
+    pack = jnp.concatenate([w_gate, w_up, w_down], axis=1)
     pack, first = lax.optimization_barrier((pack, first))
     second = gathered(pack)
 
+    inner = 4 * width + 128
+    out_w = first[:, inner:]
+    first = first[:, :inner]
     spare = first[:, 4 * width + slots :].astype(F32)
     attn_scale = spare[:, 0].reshape(1, -1)
     mlp_scale = spare[:, 1].reshape(1, -1)
@@ -646,10 +706,9 @@
     probs, pairs, mixing, mix, gated = run_forward(
         query, keys, values, forget_pre, spans, state, gate_pre, head_scale
     )
-    out_w = second[:, :width]
-    gate_w = second[:, width : width + units]
-    up_w = second[:, width + units : width + 2 * units]
-    down_w = second[:, width + 2 * units :]
+    gate_w = second[:, :units]
+    up_w = second[:, units : 2 * units]
+    down_w = second[:, 2 * units :]
 
     by_share = lambda tensor: tensor.reshape(tp, share, -1)
     hidden_s, teacher_out_s, teacher_mix_s, cotangent_s = map(by_share, (hidden_in, teacher_out, teacher_mix, cotangent))
@@ -664,21 +723,24 @@
     up_val = dot_nn(normed_mid, up_w)
     hidden_units = (jax.nn.silu(gate_val) * up_val).astype(BF)
     forward_all = gathered(jnp.concatenate([gated, hidden_units], axis=1))
-    grad_mlp, output_rows, grad_result, losses = run_exchange(
+    grad_mlp, output_rows, grad_result, losses, normed_in_c, normed_mid_c = run_exchange(
         result_epilogue, "sum_result", 2, dot_nt(hidden_units, down_w).astype(BF),
         (hidden_s, branch, teacher_out_s, teacher_mix_s, cotangent_s, mask_s, loss_scale),
         (jax.ShapeDtypeStruct((share, features), BF), narrow(share, features), narrow(1, 128)),
-    )
+        moved=(normed_in, normed_mid),
+    )
+    output = lax.all_gather(output_rows, "tp", axis=0, tiled=True)
     grad_units = dot_nn(grad_mlp, down_w)
     gate_sig = jax.nn.sigmoid(gate_val)
     grad_gate_val = (grad_units * up_val * (gate_sig * (1.0 + gate_val * (1.0 - gate_sig)))).astype(BF)
     grad_up_val = (grad_units * (gate_val * gate_sig)).astype(BF)
     grad_both = jnp.concatenate([grad_gate_val, grad_up_val], axis=1)
     mlp_all = gathered(grad_both)
-    grad_branch, grad_middle, mlp_gain_part = run_exchange(
-        branch_epilogue, "sum_middle", 3, dot_nt(grad_both, second[:, width : width + 2 * units]).astype(BF),
+    grad_branch, grad_middle, mlp_gain_part, grad_mlp_c = run_exchange(
+        branch_epilogue, "sum_middle", 3, dot_nt(grad_both, second[:, : 2 * units]).astype(BF),
         (hidden_s, branch, teacher_mix_s, grad_result, mask_s, loss_scale, mlp_scale),
         (narrow(share, features), narrow(1, features)),
+        moved=(grad_mlp,),
     )
     grad_gated = dot_nn(grad_branch, out_w)
     gquery, gkeys, gvalues, ggate, head_gain_part, gwrite, glog, carry = run_backward(
@@ -689,13 +751,12 @@
         gquery, gkeys, gvalues, ggate, gwrite, glog, keys, values, forget_pre, spans, query_pre, keys_pre,
         state, total, later,
     )
+    mlp_all, grad_pre = lax.optimization_barrier((mlp_all, grad_pre))
     attn_all = gathered(grad_pre)
-    grad_in, attn_gain_part = run_exchange(
-        input_epilogue, "sum_input", 4, dot_nt(grad_pre, first).astype(BF), (hidden_s, grad_middle, attn_scale),
-        (narrow(1, features),),
-    )
-    normed_in_c, normed_mid_c, grad_mlp_c, grad_branch_c, output = run_scatter(
-        (normed_in, normed_mid, grad_mlp, grad_branch), output_rows, "spread_rows", 5
+    grad_in, _, grad_branch_c, plane_sums, all_sums = run_exchange(
+        input_epilogue, "sum_input", 4, dot_nt(grad_pre, first).astype(BF),
+        (hidden_s, grad_middle, attn_scale, jnp.concatenate([mlp_gain_part, head_gain_part, losses], axis=1)),
+        (narrow(1, features),), moved=(grad_branch,), summing=True,
     )
     gate_grad = dot_tn(normed_mid_c, mlp_all[:, :units])
     up_grad = dot_tn(normed_mid_c, mlp_all[:, units:])
@@ -711,18 +772,11 @@
     bias_grad = jnp.sum(forget_all.astype(F32), axis=0, keepdims=True)
     bias_grad = lax.dynamic_slice_in_dim(bias_grad, index * (slots // devices), slots // devices, axis=1)
 
-    head_slots = jnp.where(jnp.arange(tp)[:, None] == lax.axis_index("tp"), head_gain_part, 0.0)
-    packed = jnp.concatenate(
-        [attn_gain_part.reshape(-1), mlp_gain_part.reshape(-1), head_slots.reshape(-1), losses.reshape(-1)]
-    )
-    packed = lax.psum(packed, ("shard", "ctx", "tp"))
-    cut = lambda vector, size: lax.dynamic_slice_in_dim(vector, index * size, size)
-    attn_gain_grad = cut(packed[:features], features // devices)
-    mlp_gain_grad = cut(packed[features : 2 * features], features // devices)
-    head_all = packed[2 * features : 2 * features + tp * width].reshape(tp, width)
-    head_row = lax.dynamic_slice_in_dim(head_all, lax.axis_index("tp"), 1, axis=0)
-    head_gain_grad = lax.dynamic_slice_in_dim(head_row, index * (width // devices), width // devices, axis=1)
-    sums = packed[2 * features + tp * width :]
+    cut = lambda row, size: lax.dynamic_slice_in_dim(row, index * size, size, axis=1)
+    attn_gain_grad = cut(all_sums[:, :features], features // devices).reshape(-1)
+    mlp_gain_grad = cut(all_sums[:, features : 2 * features], features // devices).reshape(-1)
+    head_gain_grad = cut(plane_sums[:, 2 * features : 2 * features + width], width // devices)
+    sums = all_sums[0, 2 * features + width :]
     loss_out = sums[0] / (2.0 * features * count_total)
     loss_mix = sums[1] / (2.0 * features * count_total)
     return (

time: 638 us -> 548 us (0.86)
  Pallas kernels: 306 us -> 240 us
  blocking collectives: 45 us -> 0 us
  waiting for transfers between devices: 138 us -> 157 us
  matrix products: 79.2 us -> 86.9 us
    pallas_call x1 -> x0, Pallas kernels: 73.2 us -> none  [run_scatter(): pl.pallas_call(functools.partial(scatter_kernel, count, None), out_shape=...]
    psum x1 -> x0, blocking collectives: 45 us -> none  [per_device(): packed = lax.psum(packed, ('shard', 'ctx', 'tp'))]
    all_gather x0 -> x1, waiting for transfers between devices: none -> 21.9 us  [per_device(): output = lax.all_gather(output_rows, 'tp', axis=0, tiled=True)]
    pallas_call x4, Pallas kernels: 205 us -> 212 us  [run_exchange(): pl.pallas_call(functools.partial(exchange_kernel, epilogue, len(inputs),...]
  transfers between devices with their start and end apart: 7 -> 8, of which waited for: 4 -> 5; matrix products, arithmetic and copies ran while one was open for 13% -> 13% of each run, Pallas kernels for 41% -> 35%
where the time goes in v2:
time: 548 us; the launch traced here: 541 us
  Pallas kernels  240 us (44%)
  waiting for transfers between devices  157 us (29%)
  matrix products  86.9 us (16%)
  local copies, waits for them, and re-layouts  20.5 us (4%)
  between operations  19.8 us (4%)
  other arithmetic  13.1 us (2%)
    pallas_call x4, Pallas kernels, run_exchange(): pl.pallas_call(functools.partial(exchange_kernel, epilogue, len(inputs),...  212 us
    all_gather x5, waiting for transfers between devices, gathered(): return lax.all_gather(value, GROUPED, axis=0, tiled=True)  132 us
    dot_general x9, matrix products, dot_tn(): lax.dot_general(a, b, (((0,), (0,)), ((), ())), preferred_element_type=F32)  34.9 us
    dot_general x5, matrix products, dot_nn(): lax.dot_general(a, b, (((1,), (0,)), ((), ())), preferred_element_type=F32)  27.3 us
    dot_general x4, matrix products, dot_nt(): lax.dot_general(a, b, (((1,), (1,)), ((), ())), preferred_element_type=F32)  24.8 us
    all_gather x1, waiting for transfers between devices, per_device(): output = lax.all_gather(output_rows, 'tp', axis=0, tiled=True)  21.9 us
    pallas_call x1, Pallas kernels, run_backward(): pl.pallas_call(backward_kernel, out_shape=(wide, wide, wide, jax.ShapeDty...  12.4 us
  transfers between devices with their start and end apart: 8, of which 5 were waited for; matrix products, arithmetic and copies ran while one was open for 13% of the time, Pallas kernels for 35%

profile of v2, /device:TPU:0, one launch (start us, length us, event | category | flops | bytes accessed | tf_op | source)
XLA Modules:
  0.0 541.3 jit_solution(4059566151591936505)
XLA Ops:
  7.2 1.3 convert_reduce_fusion.1
  8.5 0.6 pad.18
  9.2 0.7 pad.16
  9.8 0.7 pad.17
  10.5 0.7 reshape.126
  11.2 0.7 reshape.127
  12.0 1.0 copy.38
  13.1 3.4 concatenate.20
  16.6 1.5 pad_maximum_fusion
  18.1 66.6 %all-gather.7.cloned.1.call-done = bf16[2048,2688]{1,0:T(8,128)(2,1)} async-done(((bf16[256,2688]{1,0:T(8,128)(2,1)}), bf16[2048,2688]{1,0:T(8,128)(2,1)}) %all-gather.7.cloned.1.call-update) | async-done | bytes 11010064 | tf_op jit(solution)/shard_map/all_gather | solution.py:630
  84.8 0.8 copy.40.resets_ref
  85.9 1.2 slice_convert_fusion.1
  87.2 2.5 slice_reduce_fusion
  90.2 7.1 %fusion.4 = f32[256,2176]{1,0:T(8,128)S(1)} fusion(bf16[256,2048]{1,0:T(8,128)(2,1)S(1)} %fusion.31.refs_7_, bf16[2048,2688]{1,0:T(8,128)(2,1)} %all-gather.7.cloned.1.call-done), kind=kOutput, calls=%fused_computation.4 | convolution fusion | flops 2281701376 | bytes 12189696 | tf_op jit(solution)/shard_map/dot_general | solution.py:17
  97.3 0.7 slice.221.values_ref
  98.0 0.7 slice_add_fusion.pre_ref
  98.7 1.4 fusion.48
  100.1 3.6 slot_ends.1
  103.7 2.3 collective-permute-start
  106.0 0.9 reshape.151.refs_5_.refs_4_
  106.8 0.7 reshape.130.gain_ref
  107.5 0.6 slice_reduce_fusion.5
  108.8 0.7 copy-done.3
  109.5 6.4 %slot_forward.1 = (f32[256,64]{1,0:T(8,128)}, f32[256,256]{1,0:T(8,128)}, bf16[256,256]{1,0:T(8,128)(2,1)}, f32[256,512]{1,0:T(8,128)}, bf16[256,512]{1,0:T(8,128)(2,1)}) custom-call(bf16[256,512]{1,0:T(8,128)(2,1)} %get-tuple-element.97.query_ref, bf16[256,512]{1,0:T(8,128)(2,1)} %get-tuple-element.98.keys_ref, bf16[256,512]{1,0:T(8,128)(2,1)} %slice.221.values_ref, ...), custom_call_target="tpu_custom_call" | custom-call | tf_op jit(solution)/shard_map/slot_forward/pallas_call | solution.py:166
  115.9 3.4 convolution_convert_fusion
  119.3 47.3 %sum_branch.1 = (bf16[4,64,2048]{2,1,0:T(8,128)(2,1)}, f32[64,2048]{1,0:T(8,128)}) custom-call(bf16[4,64,2048]{2,1,0:T(8,128)(2,1)} %bitcast.68, bf16[4,64,2048]{2,1,0:T(8,128)(2,1)} %bitcast.48, f32[1,2048]{1,0:T(1,128)} %bitcast.73), custom_call_target="tpu_custom_call" | custom-call | tf_op jit(solution)/shard_map/sum_branch/pallas_call | solution.py:543
  166.6 12.0 %all-gather.9.cloned.1.call-done = bf16[2048,4224]{1,0:T(8,128)(2,1)} async-done(((bf16[256,4224]{1,0:T(8,128)(2,1)}), bf16[2048,4224]{1,0:T(8,128)(2,1)}) %all-gather.9.cloned.1.call-update) | async-done | bytes 17301520 | tf_op jit(solution)/shard_map/all_gather | solution.py:630
  178.6 4.8 fusion.10
  183.5 6.1 %multiply_convert_fusion.2 = (bf16[256,1408]{1,0:T(8,128)(2,1)S(1)}, f32[256,1408]{1,0:T(8,128)}) fusion(f32[256,1408]{1,0:T(8,128)S(1)} %fusion.10, bf16[256,2048]{1,0:T(8,128)(2,1)S(1)} %bitcast.60, bf16[2048,4224]{1,0:T(8,128)(2,1)} %all-gather.9.cloned.1.call-done), kind=kOutput, calls=%fused_computation.46 | convolution fusion | flops 1478557696 | bytes 10420224 | tf_op jit(solution)/shard_map/dot_general | solution.py:17
  189.5 5.4 %fusion.23 = bf16[256,2048]{1,0:T(8,128)(2,1)} fusion(bf16[256,1408]{1,0:T(8,128)(2,1)S(1)} %get-tuple-element.105, bf16[2048,4224]{1,0:T(8,128)(2,1)} %all-gather.9.cloned.1.call-done), kind=kOutput, calls=%fused_computation.24 | convolution fusion | flops 1476919296 | bytes 7536640 | tf_op jit(solution)/shard_map/dot_general | solution.py:21
  195.0 51.6 %sum_result.1 = (bf16[4,64,2048]{2,1,0:T(8,128)(2,1)}, bf16[64,2048]{1,0:T(8,128)(2,1)}, f32[64,2048]{1,0:T(8,128)}, f32[1,128]{1,0:T(1,128)}, bf16[8,256,256]{2...) custom-call(bf16[4,64,2048]{2,1,0:T(8,128)(2,1)} %bitcast.62, bf16[4,64,2048]{2,1,0:T(8,128)(2,1)} %bitcast.49, ...), custom_call_target="tpu_custom_call" | custom-call | tf_op jit(solution)/shard_map/sum_result/pallas_call | solution.py:543
  246.5 5.8 %multiply_convert_fusion.1 = (bf16[256,1408]{1,0:T(8,128)(2,1)S(1)}, bf16[256,1408]{1,0:T(8,128)(2,1)S(1)}) fusion(f32[256,1408]{1,0:T(8,128)} %copy-done.21, f32[256,1408]{1,0:T(8,128)} %get-tuple-element.106, bf16[256,2048]{1,0:T(8,128)(2,1)} %bitcast.69, bf16[2048,4224]{1,0:T(8,128)(2,1)} %all-gather.9.cloned.1.call-done), kind=kOutput, calls=%fused_computation.45 | convolution fusion | flops 1481080832 | bytes 11141120 | tf_op jit(solution)/shard_map/dot_general | solution.py:17
  252.4 1.2 pad_maximum_fusion.1
  254.2 1.0 pad_maximum_fusion.2
  255.5 8.4 %fusion.20 = bf16[256,2048]{1,0:T(8,128)(2,1)} fusion(bf16[2048,4224]{1,0:T(8,128)(2,1)} %all-gather.9.cloned.1.call-done, bf16[256,1408]{1,0:T(8,128)(2,1)S(1)} %get-tuple-element.95, bf16[256,1408]{1,0:T(8,128)(2,1)S(1)} %get-tuple-element.94), kind=kOutput, calls=%fused_computation.22 | convolution fusion | flops 2956197888 | bytes 14024704 | tf_op jit(solution)/shard_map/dot_general | solution.py:21
  263.9 54.0 %sum_middle.1 = (bf16[4,64,2048]{2,1,0:T(8,128)(2,1)}, f32[64,2048]{1,0:T(8,128)}, f32[1,2048]{1,0:T(1,128)}, bf16[8,256,256]{2,1,0:T(8,128)(2,1)}) custom-call(bf16[4,64,2048]{2,1,0:T(8,128)(2,1)} %bitcast.71, bf16[4,64,2048]{2,1,0:T(8,128)(2,1)} %bitcast.50, f32[64,2048]{1,0:T(8,128)} %get-tuple-element.59.refs_1_, bf16[4,64,2048]{2,1,0:T(8,128)(2,1)} %bitcast.53, ...), custom_call_target="tpu_custom_call" | custom-call | tf_op jit(solution)/shard_map/sum_middle/pallas_call | solution.py:543
  317.9 3.4 fusion.42.grad_ref
  321.4 12.4 %slot_backward.1 = (f32[256,512]{1,0:T(8,128)}, f32[256,512]{1,0:T(8,128)}, f32[256,512]{1,0:T(8,128)}, bf16[256,512]{1,0:T(8,128)(2,1)}, f32[1,512]{1,0:T(1,128...) custom-call(f32[256,512]{1,0:T(8,128)} %fusion.42.grad_ref, ...), custom_call_target="tpu_custom_call" | custom-call | tf_op jit(solution)/shard_map/slot_backward/pallas_call | solution.py:288
  333.7 1.3 collective-permute-start.1
  335.0 2.3 collective-permute-done.1.ends_ref
  337.4 0.7 copy-done.12
  338.1 4.9 slot_finish.1
  343.7 0.6 pad_maximum_fusion.3.refs_3_
  344.3 21.9 %all-gather.11.cloned.1.call-done = bf16[256,2048]{1,0:T(8,128)(2,1)} async-done(((bf16[64,2048]{1,0:T(8,128)(2,1)}), bf16[256,2048]{1,0:T(8,128)(2,1)}) %all-gather.11.cloned.1.call-update) | async-done | bytes 1048592 | tf_op jit(solution)/shard_map/all_gather | solution.py:732
  366.3 53.8 %all-gather.17.cloned.1.call-done = bf16[2048,1920]{1,0:T(8,128)(2,1)} async-done(((bf16[256,1920]{1,0:T(8,128)(2,1)}), bf16[2048,1920]{1,0:T(8,128)(2,1)}) %all-gather.17.cloned.1.call-update) | async-done | bytes 7864336 | tf_op jit(solution)/shard_map/all_gather | solution.py:630
  420.1 5.6 %fusion.6 = f32[256,1408]{1,0:T(8,128)} fusion(bf16[2048,256]{1,0:T(8,128)(2,1)S(1)} %bitcast.82, bf16[2048,1920]{1,0:T(8,128)(2,1)} %all-gather.17.cloned.1.call-done), kind=kOutput, calls=%fused_computation.6 | convolution fusion | flops 1476395008 | bytes 8257536 | tf_op jit(solution)/shard_map/dot_general | solution.py:25
  425.7 7.5 %fusion.26 = bf16[256,2048]{1,0:T(8,128)(2,1)} fusion(bf16[256,2176]{1,0:T(8,128)(2,1)S(1)} %copy-done.1, bf16[2048,2688]{1,0:T(8,128)(2,1)} %all-gather.7.cloned.1.call-done), kind=kOutput, calls=%fused_computation.25 | convolution fusion | flops 2282225664 | bytes 11075584 | tf_op jit(solution)/shard_map/dot_general | solution.py:21
  433.2 59.6 %sum_input.1 = (bf16[4,64,2048]{2,1,0:T(8,128)(2,1)}, f32[1,2048]{1,0:T(1,128)}, bf16[8,256,256]{2,1,0:T(8,128)(2,1)}, f32[1,4736]{1,0:T(1,128)}, f32[1,4736]{1,0:T(1,128)}) custom-call(bf16[4,64,2048]{2,1,0:T(8,128)(2,1)} %bitcast.61, bf16[4,64,2048]{2,1,0:T(8,128)(2,1)} %bitcast.51, f32[64,2048]{1,0:T(8,128)} %get-tuple-element.77.refs_1_, ...), custom_call_target="tpu_custom_call" | custom-call | tf_op jit(solution)/shard_map/sum_input/pallas_call | solution.py:543
  492.8 0.7 slice.136
  493.5 1.3 fusion.50
  496.1 0.6 constant_dynamic-slice_fusion.1
  496.7 0.7 fusion.49
  498.0 3.5 fusion.32
  501.5 1.6 bitcast_convert_fusion
  503.1 5.6 %fusion.12 = f32[256,1408]{1,0:T(8,128)} fusion(bf16[2048,256]{1,0:T(8,128)(2,1)S(1)} %bitcast.80, bf16[2048,2816]{1,0:T(8,128)(2,1)} %all-gather.13.cloned.1.call-done), kind=kOutput, calls=%fused_computation.12 | convolution fusion | flops 1476395008 | bytes 8257536 | tf_op jit(solution)/shard_map/dot_general | solution.py:25
  508.7 5.7 %fusion.14 = f32[256,1408]{1,0:T(8,128)} fusion(bf16[2048,256]{1,0:T(8,128)(2,1)S(1)} %bitcast.81, bf16[2048,2816]{1,0:T(8,128)(2,1)} %all-gather.13.cloned.1.call-done), kind=kOutput, calls=%fused_computation.14 | convolution fusion | flops 1476395008 | bytes 8257536 | tf_op jit(solution)/shard_map/dot_general | solution.py:25
  514.4 1.3 convert_reduce_fusion
  515.7 0.6 dynamic-slice_bitcast_fusion
  516.3 3.1 fusion.34
  519.4 2.0 fusion.46
  521.4 3.1 fusion.36
  524.5 3.1 fusion.38
  527.6 3.2 fusion.40
  530.8 1.0 copy.45
  (72 shorter events, 2.6 us)
Async XLA Ops:
  7.2 77.6 %all-gather.7.cloned.1.call-start = ((), (), s32[]{:S(2)}) async-start(), calls=%async_computation | async-start | bytes 12386304 | tf_op jit(solution)/shard_map/all_gather | solution.py:630
  12.0 4.6 copy-start.8
  12.0 4.6 copy-start.9
  12.0 4.6 copy-start.10
  16.5 162.1 %all-gather.9.cloned.1.call-start = ((), (), s32[]{:S(2)}) async-start(), calls=%async_computation.1 | async-start | bytes 19464192 | tf_op jit(solution)/shard_map/all_gather | solution.py:630
  18.1 66.7 %copy-start.16 = (s32[256]{0:T(256)S(1)}, s32[256]{0:T(256)}, u32[]{:S(2)}) copy-start(s32[256]{0:T(256)} %param.24) | copy-start | bytes 3076
  18.1 67.5 %copy-start = (bf16[256,2048]{1,0:T(8,128)(2,1)S(1)}, bf16[256,2048]{1,0:T(8,128)(2,1)}, u32[]{:S(2)}) copy-start(bf16[256,2048]{1,0:T(8,128)(2,1)} %param.19) | copy-start | bytes 3145732
  84.8 258.3 %all-gather.13.cloned.1.call-start = ((), (), s32[]{:S(2)}) async-start(), calls=%async_computation.3 | async-start | bytes 12976128 | tf_op jit(solution)/shard_map/all_gather | solution.py:630
  89.7 7.6 %copy-start.13 = (f32[2048]{0:T(1024)}, f32[2048]{0:T(1024)S(1)}, u32[]{:S(2)}) copy-start(f32[2048]{0:T(1024)S(1)} %get-tuple-element.93) | copy-start | bytes 24580
  90.1 7.2 %copy-start.2 = (bf16[256,2048]{1,0:T(8,128)(2,1)}, bf16[256,2048]{1,0:T(8,128)(2,1)S(1)}, u32[]{:S(2)}) copy-start(bf16[256,2048]{1,0:T(8,128)(2,1)S(1)} %fusion.31.refs_7_) | copy-start | bytes 3145732
  98.7 7.3 %copy-start.17 = (s32[256]{0:T(256)S(1)}, s32[256]{0:T(256)}, u32[]{:S(2)}) copy-start(s32[256]{0:T(256)} %param.23) | copy-start | bytes 3076
  103.7 5.2 collective-permute-start
  108.8 0.7 copy-start.3
  178.6 4.8 copy-start.5
  183.4 6.1 %copy-start.21 = (f32[256,1408]{1,0:T(8,128)}, f32[256,1408]{1,0:T(8,128)S(1)}, u32[]{:S(2)}) copy-start(f32[256,1408]{1,0:T(8,128)S(1)} %fusion.10) | copy-start | bytes 4325380
  252.3 1.9 copy-start.11
  253.6 112.7 %all-gather.11.cloned.1.call-start = ((), (), s32[]{:S(2)}) async-start(), calls=%async_computation.2 | async-start | bytes 1310720 | tf_op jit(solution)/shard_map/all_gather | solution.py:732
  254.2 165.9 %all-gather.17.cloned.1.call-start = ((), (), s32[]{:S(2)}) async-start(), calls=%async_computation.5 | async-start | bytes 8847360 | tf_op jit(solution)/shard_map/all_gather | solution.py:630
  255.3 259.1 %all-gather.15.cloned.1.call-start = ((), (), s32[]{:S(2)}) async-start(), calls=%async_computation.4 | async-start | bytes 10027008 | tf_op jit(solution)/shard_map/all_gather | solution.py:630
  333.7 3.6 collective-permute-start.1
  337.4 0.7 copy-start.12
  338.1 5.6 %copy-start.14 = (f32[1,2048]{1,0:T(1,128)S(1)}, f32[1,2048]{1,0:T(1,128)}, u32[]{:S(2)}) copy-start(f32[1,2048]{1,0:T(1,128)} %get-tuple-element.78) | copy-start | bytes 24580
  338.1 5.6 %copy-start.15 = (f32[1,512]{1,0:T(1,128)S(1)}, f32[1,512]{1,0:T(1,128)}, u32[]{:S(2)}) copy-start(f32[1,512]{1,0:T(1,128)} %get-tuple-element.79) | copy-start | bytes 6148
  338.1 5.7 %copy-start.18 = (f32[1,128]{1,0:T(1,128)S(1)}, f32[1,128]{1,0:T(1,128)}, u32[]{:S(2)}) copy-start(f32[1,128]{1,0:T(1,128)} %get-tuple-element.80) | copy-start | bytes 1540
  338.1 82.0 %copy-start.20 = (bf16[8,256,256]{2,1,0:T(8,128)(2,1)S(1)}, bf16[8,256,256]{2,1,0:T(8,128)(2,1)}, u32[]{:S(2)}) copy-start(bf16[8,256,256]{2,1,0:T(8,128)(2,1)} %get-tuple-element.88) | copy-start | bytes 3145732
  420.1 5.7 %copy-start.1 = (bf16[256,2176]{1,0:T(8,128)(2,1)S(1)}, bf16[256,2176]{1,0:T(8,128)(2,1)}, u32[]{:S(2)}) copy-start(bf16[256,2176]{1,0:T(8,128)(2,1)} %slot_finish.1) | copy-start | bytes 3342340
  498.0 3.5 copy-start.4
  501.5 1.6 copy-start.19
  508.7 7.6 %copy-start.6 = (bf16[8,256,256]{2,1,0:T(8,128)(2,1)S(1)}, bf16[8,256,256]{2,1,0:T(8,128)(2,1)}, u32[]{:S(2)}) copy-start(bf16[8,256,256]{2,1,0:T(8,128)(2,1)} %get-tuple-element.83) | copy-start | bytes 3145732
  527.6 3.2 copy-start.7
Sparse Core Ops, SparseCore 0:
  16.6 68.0 all-gather.6
  86.6 91.9 all-gather.8
  253.7 83.1 all-gather.12
  338.3 27.9 all-gather.10
  368.6 51.4 all-gather.16
  421.8 67.7 all-gather.14

commit v3 on v2

--- a/solution.py
+++ b/solution.py
@@ -365,44 +365,128 @@
     return me, [lax.rem(me + k, count) for k in range(1, count)]
 
 
-def sum_over_tp(partial_ref, landed, send_sems, recv_sems):
-    me, peers = tp_peers()
-    copies = []
-    for k, peer in enumerate(peers):
-        copy = pltpu.make_async_remote_copy(
-            src_ref=partial_ref.at[peer],
-            dst_ref=landed.at[k],
-            send_sem=send_sems.at[k],
-            recv_sem=recv_sems.at[k],
-            device_id={"tp": peer},
+CHUNKS = 2
+LAG = 2
+
+
+def tp_line(partial_ref, full_ref, riders, arrived, staged, sums_ref, finish, send_a, recv_a, send_b, recv_b):
+    count = lax.axis_size("tp")
+    me = lax.axis_index("tp")
+    rows = partial_ref.shape[1] // CHUNKS
+    places = [(me, lax.rem(me + 1, count)), (count - 1 - me, lax.rem(me + count - 1, count))]
+
+    def block_at(side, place):
+        return place if side == 0 else count - 1 - place
+
+    def cut(chunk):
+        return pl.ds(chunk * rows, rows)
+
+    def sum_copy(side, hop, chunk, source):
+        return pltpu.make_async_remote_copy(
+            src_ref=source,
+            dst_ref=arrived.at[side, hop, chunk],
+            send_sem=send_a.at[side, hop, chunk],
+            recv_sem=recv_a.at[side, hop, chunk],
+            device_id={"tp": places[side][1]},
             device_id_type=MESH,
         )
-        copy.start()
-        copies.append(copy)
-    total = partial_ref[me].astype(F32)
-    for k, copy in enumerate(copies):
-        copy.wait()
-        total = total + landed[k].astype(F32)
-    return total
-
-
-def spread_over_tp(rows_ref, full_ref, send_sems, recv_sems):
-    me, peers = tp_peers()
-    copies = []
-    for k, peer in enumerate(peers):
-        copy = pltpu.make_async_remote_copy(
-            src_ref=rows_ref,
-            dst_ref=full_ref.at[me],
-            send_sem=send_sems.at[k],
-            recv_sem=recv_sems.at[k],
-            device_id={"tp": peer},
+
+    def add_hop(chunk, hop):
+        for side, (place, _) in enumerate(places):
+            block = block_at(side, count - 1 - hop)
+            own = partial_ref.at[block, cut(chunk)]
+            slot = staged.at[side, hop, chunk]
+
+            @pl.when((place > 0) & (count - 1 - hop >= place))
+            def _():
+                sum_copy(side, hop, chunk, slot).wait_recv()
+
+            @pl.when((place == 0) & (count - 1 - hop > place))
+            def _():
+                sum_copy(side, hop, chunk, own).start()
+
+            @pl.when((place > 0) & (count - 1 - hop > place))
+            def _():
+                slot[...] = (own[...].astype(F32) + arrived[side, hop, chunk].astype(F32)).astype(BF)
+                sum_copy(side, hop, chunk, slot).start()
+
+    def close(chunk):
+        sums_ref[...] = partial_ref[me, cut(chunk)].astype(F32)
+        for side, (place, _) in enumerate(places):
+
+            @pl.when(place > 0)
+            def _():
+                sums_ref[...] += arrived[side, count - 1 - place, chunk].astype(F32)
+
+        finish(chunk, sums_ref[...])
+
+    gathers = [(full_ref, cut(chunk)) for chunk in range(CHUNKS)]
+    gathers += [(full, pl.ds(0, full.shape[1])) for _, full in riders]
+
+    def row_copy(side, hop, which, block):
+        full, part = gathers[which]
+        return pltpu.make_async_remote_copy(
+            src_ref=full.at[block, part],
+            dst_ref=full.at[block, part],
+            send_sem=send_b.at[side, hop, which],
+            recv_sem=recv_b.at[side, hop, which],
+            device_id={"tp": places[side][1]},
             device_id_type=MESH,
         )
-        copy.start()
-        copies.append(copy)
-    full_ref[me] = rows_ref[...]
-    for copy in copies:
-        copy.wait()
+
+    def offer(which):
+        for side, (place, _) in enumerate(places):
+
+            @pl.when(place < count - 1)
+            def _():
+                row_copy(side, 0, which, me).start()
+
+    def forward(which, hop):
+        for side, (place, _) in enumerate(places):
+            block = block_at(side, jnp.maximum(place - hop, 0))
+
+            @pl.when(place >= hop)
+            def _():
+                row_copy(side, hop - 1, which, block).wait_recv()
+
+            if hop < count - 1:
+
+                @pl.when((place >= hop) & (place < count - 1))
+                def _():
+                    row_copy(side, hop, which, block).start()
+
+    for rows_ref, full in riders:
+        full[me] = rows_ref[...]
+    steps = []
+    for chunk in range(CHUNKS):
+        run = [functools.partial(add_hop, chunk, hop) for hop in range(count - 1)]
+        run += [functools.partial(close, chunk), functools.partial(offer, chunk)]
+        run += [functools.partial(forward, chunk, hop) for hop in range(1, count)]
+        steps.append(run)
+    for rider in range(CHUNKS, len(gathers)):
+        steps.append([functools.partial(offer, rider), *[functools.partial(forward, rider, hop) for hop in range(1, count)]])
+    length = max(LAG * at + len(run) for at, run in enumerate(steps))
+    for tick in range(length):
+        for at, run in enumerate(steps):
+            if 0 <= tick - LAG * at < len(run):
+                run[tick - LAG * at]()
+
+    def drain():
+        for side, (place, _) in enumerate(places):
+            for hop in range(count - 1):
+
+                @pl.when(count - 1 - hop > place)
+                def _():
+                    for chunk in range(CHUNKS):
+                        sum_copy(side, hop, chunk, staged.at[side, hop, chunk]).wait_send()
+
+                @pl.when((place >= hop) & (place < count - 1))
+                def _():
+                    block = block_at(side, jnp.maximum(place - hop, 0))
+                    for which in range(len(gathers)):
+                        row_copy(side, hop, which, block).wait_send()
+
+    return drain
 
 
 def plane_peers():
@@ -471,42 +555,52 @@
     return total
 
 
-def exchange_kernel(epilogue, n_in, n_rows, n_moved, n_sums, partial_ref, *refs):
+def exchange_kernel(epilogue, n_in, n_rows, n_moved, n_riders, n_sums, partial_ref, *refs):
     me, peers = tp_peers()
     inputs, refs = refs[:n_in], refs[n_in:]
     sources, refs = refs[:n_moved], refs[n_moved:]
+    riders, refs = refs[:n_riders], refs[n_riders:]
     full_ref, refs = refs[0], refs[1:]
     outputs, refs = refs[:n_rows], refs[n_rows:]
     targets, refs = refs[:n_moved], refs[n_moved:]
+    fulls, refs = refs[:n_riders], refs[n_riders:]
     sums, refs = refs[: 2 * n_sums], refs[2 * n_sums :]
-    landed, rows_ref, send_a, recv_a, send_b, recv_b, send_m, recv_m = refs[:8]
+    arrived, staged, sums_ref, send_a, recv_a, send_b, recv_b, send_m, recv_m = refs[:9]
     own, plane, places = plane_peers()
     across = [{"tp": peer} for peer in peers]
     greet(across + (places if n_moved or n_sums else []))
     moves = start_scatter(sources, targets, send_m, recv_m)
-    total = sum_over_tp(partial_ref, landed, send_a, recv_a)
-    epilogue(total, me, inputs, outputs, rows_ref)
+    rows = full_ref.shape[1] // CHUNKS
+    started = []
+
+    def finish(chunk, total):
+        part = pl.ds(chunk * rows, rows)
+        full_ref[me, part] = epilogue(total, me, part, chunk == 0, inputs, outputs)
+        if n_sums and chunk == CHUNKS - 1:
+            row_ref, in_plane, _, _, send_p, recv_p = refs[9:15]
+            width = outputs[0].shape[1]
+            row_ref[:, :width] = outputs[0][...]
+            row_ref[:, width:] = inputs[-1][...]
+            started.extend(start_sums(row_ref, in_plane, send_p, recv_p, plane, places, own))
+
+    drain = tp_line(
+        partial_ref, full_ref, list(zip(riders, fulls)), arrived, staged, sums_ref, finish, send_a, recv_a, send_b, recv_b
+    )
     if n_sums:
-        row_ref, in_plane, plane_row, in_tp, send_p, recv_p, send_t, recv_t = refs[8:]
-        width = outputs[0].shape[1]
-        row_ref[:, :width] = outputs[0][...]
-        row_ref[:, width:] = inputs[-1][...]
-        started = start_sums(row_ref, in_plane, send_p, recv_p, plane, places, own)
-    spread_over_tp(rows_ref, full_ref, send_b, recv_b)
-    if n_sums:
+        row_ref, in_plane, plane_row, in_tp, send_p, recv_p, send_t, recv_t = refs[9:]
         for copy in started:
             copy.wait()
         plane_row[...] = summed(in_plane)
         sums[0][...] = plane_row[...]
-        started = start_sums(plane_row, in_tp, send_t, recv_t, peers, across, me)
-        for copy in started:
+        for copy in start_sums(plane_row, in_tp, send_t, recv_t, peers, across, me):
             copy.wait()
         sums[1][...] = summed(in_tp)
+    drain()
     for copy in moves:
         copy.wait()
 
 
-def run_exchange(epilogue, name, collective_id, partial, inputs, row_outputs, moved=(), summing=False):
+def run_exchange(epilogue, name, collective_id, partial, inputs, row_outputs, moved=(), riders=(), summing=False):
     tp = lax.axis_size("tp")
     devices = lax.axis_size(GROUPED)
     tokens, columns = partial.shape
@@ -517,9 +611,10 @@
         moved = [m.reshape(tokens, devices, step).transpose(1, 0, 2) for m in moved]
     count = len(moved)
     scratch = [
-        pltpu.VMEM((tp - 1, share, columns), BF),
-        pltpu.VMEM((share, columns), BF),
-        *[pltpu.SemaphoreType.DMA((tp - 1,))] * 4,
+        *[pltpu.VMEM((2, tp - 1, CHUNKS, share // CHUNKS, columns), BF)] * 2,
+        pltpu.VMEM((share // CHUNKS, columns), F32),
+        *[pltpu.SemaphoreType.DMA((2, tp - 1, CHUNKS))] * 2,
+        *[pltpu.SemaphoreType.DMA((2, tp - 1, CHUNKS + len(riders)))] * 2,
         *[pltpu.SemaphoreType.DMA((max(count, 1), devices - 1))] * 2,
     ]
     extra = ()
@@ -538,51 +633,56 @@
         jax.ShapeDtypeStruct((tp, share, columns), BF),
         *row_outputs,
         *[jax.ShapeDtypeStruct((devices, tokens, step), BF)] * count,
+        *[jax.ShapeDtypeStruct((tp, *r.shape), BF) for r in riders],
         *extra,
     )
     outs = pl.pallas_call(
-        functools.partial(exchange_kernel, epilogue, len(inputs), len(row_outputs), count, int(summing)),
+        functools.partial(
+            exchange_kernel, epilogue, len(inputs), len(row_outputs), count, len(riders), int(summing)
+        ),
         out_shape=out_shape,
-        in_specs=[pl.BlockSpec(memory_space=pltpu.VMEM)] * (1 + len(inputs) + count),
+        in_specs=[pl.BlockSpec(memory_space=pltpu.VMEM)] * (1 + len(inputs) + count + len(riders)),
         out_specs=tuple([pl.BlockSpec(memory_space=pltpu.VMEM)] * len(out_shape)),
         scratch_shapes=scratch,
         compiler_params=pltpu.CompilerParams(collective_id=collective_id, has_side_effects=True),
         name=name,
-    )(partial, *inputs, *moved)
+    )(partial, *inputs, *moved, *riders)
     start = 1 + len(row_outputs)
     return (
         outs[0].reshape(tokens, columns),
         *outs[1:start],
         *[o.reshape(devices * tokens, step) for o in outs[start : start + count]],
-        *outs[start + count :],
-    )
-
-
-def middle_epilogue(total, me, inputs, outputs, rows_ref):
+        *[o.reshape(tokens, -1) for o in outs[start + count : start + count + len(riders)]],
+        *outs[start + count + len(riders) :],
+    )
+
+
+def middle_epilogue(total, me, part, first, inputs, outputs):
     hidden_ref, gain_ref = inputs
     (branch_ref,) = outputs
-    branch_ref[...] = total
-    middle = hidden_ref[me].astype(F32) + total
+    branch_ref[part, :] = total
+    middle = hidden_ref[me, part].astype(F32) + total
     scale = lax.rsqrt(jnp.mean(middle * middle, axis=1, keepdims=True) + EPSILON)
-    rows_ref[...] = (middle * scale * gain_ref[...]).astype(BF)
-
-
-def result_epilogue(total, me, inputs, outputs, rows_ref):
+    return (middle * scale * gain_ref[...]).astype(BF)
+
+
+def result_epilogue(total, me, part, first, inputs, outputs):
     hidden_ref, branch_ref, teacher_out_ref, teacher_mix_ref, cotangent_ref, mask_ref, scale_ref = inputs
     output_ref, grad_ref, losses_ref = outputs
-    branch = branch_ref[...]
-    result = hidden_ref[me].astype(F32) + branch + total
-    output_ref[...] = result.astype(BF)
-    mask = mask_ref[me]
-    gap = result - teacher_out_ref[me].astype(F32)
-    gap_mix = branch - teacher_mix_ref[me].astype(F32)
+    branch = branch_ref[part, :]
+    result = hidden_ref[me, part].astype(F32) + branch + total
+    output_ref[part, :] = result.astype(BF)
+    mask = mask_ref[me, part]
+    gap = result - teacher_out_ref[me, part].astype(F32)
+    gap_mix = branch - teacher_mix_ref[me, part].astype(F32)
     loss_out = jnp.sum(mask * (gap * gap), keepdims=True)
     loss_mix = jnp.sum(mask * (gap_mix * gap_mix), keepdims=True)
     lane = lax.broadcasted_iota(jnp.int32, (1, 128), 1)
-    losses_ref[...] = jnp.where(lane == 0, loss_out, 0.0) + jnp.where(lane == 1, loss_mix, 0.0)
-    grad = cotangent_ref[me].astype(F32) + scale_ref[...] * mask * gap
-    grad_ref[...] = grad
-    rows_ref[...] = grad.astype(BF)
+    losses = jnp.where(lane == 0, loss_out, 0.0) + jnp.where(lane == 1, loss_mix, 0.0)
+    losses_ref[...] = losses if first else losses_ref[...] + losses
+    grad = cotangent_ref[me, part].astype(F32) + scale_ref[...] * mask * gap
+    grad_ref[part, :] = grad
+    return grad.astype(BF)
 
 
 def norm_back(grad, rows, gain):
@@ -593,24 +693,24 @@
     return scale * (inner - unit * jnp.mean(unit * inner, axis=1, keepdims=True)), gain_grad
 
 
-def branch_epilogue(total, me, inputs, outputs, rows_ref):
+def branch_epilogue(total, me, part, first, inputs, outputs):
     hidden_ref, branch_ref, teacher_mix_ref, grad_ref, mask_ref, scale_ref, gain_ref = inputs
     grad_middle_ref, gain_grad_ref = outputs
-    branch = branch_ref[...]
-    part, gain_grad = norm_back(total, hidden_ref[me].astype(F32) + branch, gain_ref[...])
-    gain_grad_ref[...] = gain_grad
-    grad_middle = part + grad_ref[...]
-    grad_middle_ref[...] = grad_middle
-    gap_mix = branch - teacher_mix_ref[me].astype(F32)
-    rows_ref[...] = (grad_middle + scale_ref[...] * mask_ref[me] * gap_mix).astype(BF)
-
-
-def input_epilogue(total, me, inputs, outputs, rows_ref):
+    branch = branch_ref[part, :]
+    back, gain_grad = norm_back(total, hidden_ref[me, part].astype(F32) + branch, gain_ref[...])
+    gain_grad_ref[...] = gain_grad if first else gain_grad_ref[...] + gain_grad
+    grad_middle = back + grad_ref[part, :]
+    grad_middle_ref[part, :] = grad_middle
+    gap_mix = branch - teacher_mix_ref[me, part].astype(F32)
+    return (grad_middle + scale_ref[...] * mask_ref[me, part] * gap_mix).astype(BF)
+
+
+def input_epilogue(total, me, part, first, inputs, outputs):
     hidden_ref, grad_middle_ref, gain_ref = inputs[:3]
     (gain_grad_ref,) = outputs
-    part, gain_grad = norm_back(total, hidden_ref[me].astype(F32), gain_ref[...])
-    gain_grad_ref[...] = gain_grad
-    rows_ref[...] = (part + grad_middle_ref[...]).astype(BF)
+    back, gain_grad = norm_back(total, hidden_ref[me, part].astype(F32), gain_ref[...])
+    gain_grad_ref[...] = gain_grad if first else gain_grad_ref[...] + gain_grad
+    return (back + grad_middle_ref[part, :]).astype(BF)
 
 
 def passed_along(value, axis, steps):
@@ -729,7 +829,7 @@
         (jax.ShapeDtypeStruct((share, features), BF), narrow(share, features), narrow(1, 128)),
         moved=(normed_in, normed_mid),
     )
-    output = lax.all_gather(output_rows, "tp", axis=0, tiled=True)
+    forward_all, grad_mlp = lax.optimization_barrier((forward_all, grad_mlp))
     grad_units = dot_nn(grad_mlp, down_w)
     gate_sig = jax.nn.sigmoid(gate_val)
     grad_gate_val = (grad_units * up_val * (gate_sig * (1.0 + gate_val * (1.0 - gate_sig)))).astype(BF)
@@ -753,10 +853,10 @@
     )
     mlp_all, grad_pre = lax.optimization_barrier((mlp_all, grad_pre))
     attn_all = gathered(grad_pre)
-    grad_in, _, grad_branch_c, plane_sums, all_sums = run_exchange(
+    grad_in, _, grad_branch_c, output, plane_sums, all_sums = run_exchange(
         input_epilogue, "sum_input", 4, dot_nt(grad_pre, first).astype(BF),
         (hidden_s, grad_middle, attn_scale, jnp.concatenate([mlp_gain_part, head_gain_part, losses], axis=1)),
-        (narrow(1, features),), moved=(grad_branch,), summing=True,
+        (narrow(1, features),), moved=(grad_branch,), riders=(output_rows,), summing=True,
     )
     gate_grad = dot_tn(normed_mid_c, mlp_all[:, :units])
     up_grad = dot_tn(normed_mid_c, mlp_all[:, units:])

time: 548 us -> 647 us (1.18)
  Pallas kernels: 240 us -> 425 us
  waiting for transfers between devices: 157 us -> 69.5 us
    pallas_call x4, Pallas kernels: 212 us -> 398 us  [run_exchange(): pl.pallas_call(functools.partial(exchange_kernel, epilogue, len(inputs),...]
    all_gather x5, waiting for transfers between devices: 132 us -> 66.7 us  [gathered(): return lax.all_gather(value, GROUPED, axis=0, tiled=True)]
    all_gather x1 -> x0, waiting for transfers between devices: 21.9 us -> none  [per_device(): output = lax.all_gather(output_rows, 'tp', axis=0, tiled=True)]
  transfers between devices with their start and end apart: 8 -> 7, of which waited for: 5 -> 3; matrix products, arithmetic and copies ran while one was open for 13% -> 12% of each run, Pallas kernels for 35% -> 67%
where the time goes in v3:
time: 647 us; the launch traced here: 638 us
  Pallas kernels  425 us (66%)
  matrix products  85.9 us (13%)
  waiting for transfers between devices  69.5 us (11%)
  local copies, waits for them, and re-layouts  20.4 us (3%)
  between operations  19.5 us (3%)
  other arithmetic  13.1 us (2%)
    pallas_call x4, Pallas kernels, run_exchange(): pl.pallas_call(functools.partial(exchange_kernel, epilogue, len(inputs),...  398 us
    all_gather x5, waiting for transfers between devices, gathered(): return lax.all_gather(value, GROUPED, axis=0, tiled=True)  66.7 us
    dot_general x9, matrix products, dot_tn(): lax.dot_general(a, b, (((0,), (0,)), ((), ())), preferred_element_type=F32)  35 us
    dot_general x5, matrix products, dot_nn(): lax.dot_general(a, b, (((1,), (0,)), ((), ())), preferred_element_type=F32)  26.4 us
    dot_general x4, matrix products, dot_nt(): lax.dot_general(a, b, (((1,), (1,)), ((), ())), preferred_element_type=F32)  24.5 us
  transfers between devices with their start and end apart: 7, of which 3 were waited for; matrix products, arithmetic and copies ran while one was open for 12% of the time, Pallas kernels for 67%

profile of v3, /device:TPU:0, one launch (start us, length us, event | category | flops | bytes accessed | tf_op | source)
XLA Modules:
  0.0 637.6 jit_solution(11671198557154346801)
XLA Ops:
  7.2 1.3 convert_reduce_fusion.1
  8.5 0.6 pad.18
  9.2 0.7 pad.16
  9.8 0.7 pad.17
  10.5 0.7 reshape.129
  11.2 0.7 reshape.130
  12.0 1.0 copy.38
  13.1 3.4 concatenate.20
  16.6 1.5 pad_maximum_fusion
  18.1 66.6 %all-gather.6.cloned.1.call-done = bf16[2048,2688]{1,0:T(8,128)(2,1)} async-done(((bf16[256,2688]{1,0:T(8,128)(2,1)}), bf16[2048,2688]{1,0:T(8,128)(2,1)}) %all-gather.6.cloned.1.call-update) | async-done | bytes 11010064 | tf_op jit(solution)/shard_map/all_gather | solution.py:730
  84.8 0.8 copy.40.resets_ref
  85.9 1.2 slice_convert_fusion.1
  87.2 2.5 slice_reduce_fusion
  89.8 0.3 fusion.31.refs_7_
  90.2 7.1 %fusion.4 = f32[256,2176]{1,0:T(8,128)S(1)} fusion(bf16[256,2048]{1,0:T(8,128)(2,1)S(1)} %fusion.31.refs_7_, bf16[2048,2688]{1,0:T(8,128)(2,1)} %all-gather.6.cloned.1.call-done), kind=kOutput, calls=%fused_computation.4 | convolution fusion | flops 2281701376 | bytes 12189696 | tf_op jit(solution)/shard_map/dot_general | solution.py:17
  97.3 0.7 slice.219.values_ref
  98.0 0.7 slice_add_fusion.pre_ref
  98.7 1.4 fusion.48
  100.1 3.6 slot_ends.1
  103.6 2.1 collective-permute-start
  105.8 0.7 reshape.133.gain_ref
  106.5 0.7 collective-permute-done.state_ref
  107.1 0.7 copy-done.3
  107.8 6.4 slot_forward.1
  114.2 3.4 convolution_convert_fusion
  117.6 96.7 %sum_branch.1 = (bf16[4,64,2048]{2,1,0:T(8,128)(2,1)}, f32[64,2048]{1,0:T(8,128)}) custom-call(bf16[4,64,2048]{2,1,0:T(8,128)(2,1)} %bitcast.67, bf16[4,64,2048]{2,1,0:T(8,128)(2,1)} %bitcast.49, f32[1,2048]{1,0:T(1,128)} %bitcast.75), custom_call_target="tpu_custom_call" | custom-call | tf_op jit(solution)/shard_map/sum_branch/pallas_call | solution.py:639
  214.3 4.8 fusion.8
  219.1 5.6 multiply_convert_fusion.2
  224.7 1.0 pad_maximum_fusion.2
  225.8 0.9 reshape.155.refs_5_.refs_4_
  226.7 0.6 slice_reduce_fusion.5
  228.0 5.6 fusion.23
  233.6 97.9 %sum_result.1 = (bf16[4,64,2048]{2,1,0:T(8,128)(2,1)}, bf16[64,2048]{1,0:T(8,128)(2,1)}, f32[64,2048]{1,0:T(8,128)}, f32[1,128]{1,0:T(1,128)}, bf16[8,256,256]{2...) custom-call(bf16[4,64,2048]{2,1,0:T(8,128)(2,1)} %bitcast.60, bf16[4,64,2048]{2,1,0:T(8,128)(2,1)} %bitcast.50, ...), custom_call_target="tpu_custom_call" | custom-call | tf_op jit(solution)/shard_map/sum_result/pallas_call | solution.py:639
  331.5 5.4 multiply_convert_fusion.1
  336.9 1.2 pad_maximum_fusion.1
  338.2 8.4 %fusion.20 = bf16[256,2048]{1,0:T(8,128)(2,1)} fusion(bf16[2048,4224]{1,0:T(8,128)(2,1)} %all-gather.8.cloned.1.call-done, bf16[256,1408]{1,0:T(8,128)(2,1)S(1)} %get-tuple-element.101, bf16[256,1408]{1,0:T(8,128)(2,1)S(1)} %get-tuple-element.100), kind=kOutput, calls=%fused_computation.22 | convolution fusion | flops 2956197888 | bytes 14024704 | tf_op jit(solution)/shard_map/dot_general | solution.py:21
  346.6 98.0 %sum_middle.1 = (bf16[4,64,2048]{2,1,0:T(8,128)(2,1)}, f32[64,2048]{1,0:T(8,128)}, f32[1,2048]{1,0:T(1,128)}, bf16[8,256,256]{2,1,0:T(8,128)(2,1)}) custom-call(bf16[4,64,2048]{2,1,0:T(8,128)(2,1)} %bitcast.72, bf16[4,64,2048]{2,1,0:T(8,128)(2,1)} %bitcast.51, f32[64,2048]{1,0:T(8,128)} %get-tuple-element.62.refs_1_, bf16[4,64,2048]{2,1,0:T(8,128)(2,1)} %bitcast.54, ...), custom_call_target="tpu_custom_call" | custom-call | tf_op jit(solution)/shard_map/sum_middle/pallas_call | solution.py:639
  444.6 3.4 fusion.42.grad_ref
  448.0 12.1 %slot_backward.1 = (f32[256,512]{1,0:T(8,128)}, f32[256,512]{1,0:T(8,128)}, f32[256,512]{1,0:T(8,128)}, bf16[256,512]{1,0:T(8,128)(2,1)}, f32[1,512]{1,0:T(1,128...) custom-call(f32[256,512]{1,0:T(8,128)} %fusion.42.grad_ref, ...), custom_call_target="tpu_custom_call" | custom-call | tf_op jit(solution)/shard_map/slot_backward/pallas_call | solution.py:288
  460.2 1.5 collective-permute-start.1
  461.7 2.1 collective-permute-done.1.ends_ref
  463.8 0.7 copy-done.12
  464.5 4.9 slot_finish.1
  470.2 0.6 pad_maximum_fusion.3.refs_3_
  470.8 5.7 fusion.10
  476.5 7.1 %fusion.26 = bf16[256,2048]{1,0:T(8,128)(2,1)} fusion(bf16[256,2176]{1,0:T(8,128)(2,1)S(1)} %copy-done.1, bf16[2048,2688]{1,0:T(8,128)(2,1)} %all-gather.6.cloned.1.call-done), kind=kOutput, calls=%fused_computation.25 | convolution fusion | flops 2282225664 | bytes 11075584 | tf_op jit(solution)/shard_map/dot_general | solution.py:21
  483.7 105.8 %sum_input.1 = (bf16[4,64,2048]{2,1,0:T(8,128)(2,1)}, f32[1,2048]{1,0:T(1,128)}, bf16[8,256,256]{2,1,0:T(8,128)(2,1)}, bf16[4,64,2048]{2,1,0:T(8,128)(2,1)}, f32[1,4736]{1,0:T(1,128)}, /*index=5*/f32[1,4736]{1,0:T(1,128)}) custom-call(bf16[4,64,2048]{2,1,0:T(8,128)(2,1)} %bitcast.73, bf16[4,64,2048]{2,1,0:T(8,128)(2,1)} %bitcast.52, ...), custom_call_target="tpu_custom_call" | custom-call | tf_op jit(solution)/shard_map/sum_input/pallas_call | solution.py:639
  589.4 1.3 fusion.50
  592.0 0.7 slice.136
  592.7 0.6 constant_dynamic-slice_fusion.1
  593.3 0.7 fusion.49
  594.0 0.6 constant_dynamic-slice_fusion
  594.6 3.5 fusion.40
  598.1 1.6 bitcast_convert_fusion
  599.7 5.6 fusion.12
  605.3 5.7 fusion.14
  611.0 1.3 convert_reduce_fusion
  612.3 0.6 dynamic-slice_bitcast_fusion
  612.9 3.1 fusion.32
  616.0 2.0 fusion.46
  618.0 3.1 fusion.34
  621.1 3.1 fusion.36
  624.2 3.2 fusion.38
  627.4 1.0 copy.45
  (67 shorter events, 1.0 us)
Async XLA Ops:
  7.2 77.6 %all-gather.6.cloned.1.call-start = ((), (), s32[]{:S(2)}) async-start(), calls=%async_computation | async-start | bytes 12386304 | tf_op jit(solution)/shard_map/all_gather | solution.py:730
  12.0 4.6 copy-start.8
  12.0 4.6 copy-start.9
  12.0 4.6 copy-start.10
  16.5 197.7 %all-gather.8.cloned.1.call-start = ((), (), s32[]{:S(2)}) async-start(), calls=%async_computation.1 | async-start | bytes 19464192 | tf_op jit(solution)/shard_map/all_gather | solution.py:730
  18.1 66.7 %copy-start.16 = (s32[256]{0:T(256)S(1)}, s32[256]{0:T(256)}, u32[]{:S(2)}) copy-start(s32[256]{0:T(256)} %param.24) | copy-start | bytes 3076
  18.1 67.5 %copy-start = (bf16[256,2048]{1,0:T(8,128)(2,1)S(1)}, bf16[256,2048]{1,0:T(8,128)(2,1)}, u32[]{:S(2)}) copy-start(bf16[256,2048]{1,0:T(8,128)(2,1)} %param.19) | copy-start | bytes 3145732
  84.8 246.7 %all-gather.10.cloned.1.call-start = ((), (), s32[]{:S(2)}) async-start(), calls=%async_computation.2 | async-start | bytes 8847360 | tf_op jit(solution)/shard_map/all_gather | solution.py:730
  89.7 7.6 %copy-start.13 = (f32[2048]{0:T(1024)}, f32[2048]{0:T(1024)S(1)}, u32[]{:S(2)}) copy-start(f32[2048]{0:T(1024)S(1)} %get-tuple-element.99) | copy-start | bytes 24580
  90.1 7.1 %copy-start.2 = (bf16[256,2048]{1,0:T(8,128)(2,1)}, bf16[256,2048]{1,0:T(8,128)(2,1)S(1)}, u32[]{:S(2)}) copy-start(bf16[256,2048]{1,0:T(8,128)(2,1)S(1)} %fusion.31.refs_7_) | copy-start | bytes 3145732
  103.6 3.5 collective-permute-start
  107.1 0.7 copy-start.3
  214.3 4.8 copy-start.4
  219.1 5.6 copy-start.11
  224.7 1.1 copy-start.17
  225.8 243.7 %all-gather.12.cloned.1.call-start = ((), (), s32[]{:S(2)}) async-start(), calls=%async_computation.3 | async-start | bytes 12976128 | tf_op jit(solution)/shard_map/all_gather | solution.py:730
  338.1 272.8 %all-gather.14.cloned.1.call-start = ((), (), s32[]{:S(2)}) async-start(), calls=%async_computation.4 | async-start | bytes 10027008 | tf_op jit(solution)/shard_map/all_gather | solution.py:730
  460.2 3.6 collective-permute-start.1
  463.8 0.7 copy-start.12
  464.5 5.6 copy-start.14
  464.5 5.6 copy-start.15
  464.5 5.7 copy-start.18
  464.5 6.3 copy-start.20
  470.8 5.7 copy-start.1
  594.6 3.5 copy-start.5
  598.1 1.6 copy-start.19
  605.3 7.6 %copy-start.6 = (bf16[8,256,256]{2,1,0:T(8,128)(2,1)S(1)}, bf16[8,256,256]{2,1,0:T(8,128)(2,1)}, u32[]{:S(2)}) copy-start(bf16[8,256,256]{2,1,0:T(8,128)(2,1)} %get-tuple-element.88) | copy-start | bytes 3145732
  624.2 3.2 copy-start.7
Sparse Core Ops, SparseCore 0:
  16.6 68.0 all-gather.5
  86.6 91.9 all-gather.7
  225.9 66.5 all-gather.9
  338.3 77.4 all-gather.11
  469.6 60.5 all-gather.13

commit v4 on v3

--- a/solution.py
+++ b/solution.py
@@ -391,32 +391,33 @@
             device_id_type=MESH,
         )
 
-    def add_hop(chunk, hop):
+    def add_hop(chunk, tick):
         for side, (place, _) in enumerate(places):
+            hop = jnp.clip(tick - place, 0, count - 2)
             block = block_at(side, count - 1 - hop)
             own = partial_ref.at[block, cut(chunk)]
             slot = staged.at[side, hop, chunk]
-
-            @pl.when((place > 0) & (count - 1 - hop >= place))
+            if tick < count - 1:
+
+                @pl.when(place == 0)
+                def _():
+                    sum_copy(side, hop, chunk, own).start()
+
+            @pl.when((place > 0) & (place <= tick))
             def _():
                 sum_copy(side, hop, chunk, slot).wait_recv()
-
-            @pl.when((place == 0) & (count - 1 - hop > place))
-            def _():
-                sum_copy(side, hop, chunk, own).start()
-
-            @pl.when((place > 0) & (count - 1 - hop > place))
-            def _():
                 slot[...] = (own[...].astype(F32) + arrived[side, hop, chunk].astype(F32)).astype(BF)
                 sum_copy(side, hop, chunk, slot).start()
 
     def close(chunk):
         sums_ref[...] = partial_ref[me, cut(chunk)].astype(F32)
         for side, (place, _) in enumerate(places):
+            hop = jnp.minimum(count - 1 - place, count - 2)
 
             @pl.when(place > 0)
             def _():
-                sums_ref[...] += arrived[side, count - 1 - place, chunk].astype(F32)
+                sum_copy(side, hop, chunk, staged.at[side, hop, chunk]).wait_recv()
+                sums_ref[...] += arrived[side, hop, chunk].astype(F32)
 
         finish(chunk, sums_ref[...])
 
@@ -460,7 +461,7 @@
     steps = []
     for chunk in range(CHUNKS):
         run = [functools.partial(add_hop, chunk, hop) for hop in range(count - 1)]
-        run += [functools.partial(close, chunk), functools.partial(offer, chunk)]
+        run += [lambda chunk=chunk: (close(chunk), offer(chunk))]
         run += [functools.partial(forward, chunk, hop) for hop in range(1, count)]
         steps.append(run)
     for rider in range(CHUNKS, len(gathers)):

time: 647 us -> 481 us (0.74)
  Pallas kernels: 425 us -> 232 us
  waiting for transfers between devices: 69.5 us -> 96.5 us
    pallas_call x4, Pallas kernels: 398 us -> 205 us  [run_exchange(): pl.pallas_call(functools.partial(exchange_kernel, epilogue, len(inputs),...]
    all_gather x5, waiting for transfers between devices: 66.7 us -> 93.7 us  [gathered(): return lax.all_gather(value, GROUPED, axis=0, tiled=True)]
  transfers between devices with their start and end apart: 7 -> 7, of which waited for: 3 -> 5; matrix products, arithmetic and copies ran while one was open for 12% -> 16% of each run, Pallas kernels for 67% -> 49%
where the time goes in v4:
time: 481 us; the launch traced here: 471 us
  Pallas kernels  232 us (48%)
  waiting for transfers between devices  96.5 us (20%)
  matrix products  86.1 us (18%)
  local copies, waits for them, and re-layouts  20.4 us (4%)
  between operations  19.5 us (4%)
  other arithmetic  13.1 us (3%)
    pallas_call x4, Pallas kernels, run_exchange(): pl.pallas_call(functools.partial(exchange_kernel, epilogue, len(inputs),...  205 us
    all_gather x5, waiting for transfers between devices, gathered(): return lax.all_gather(value, GROUPED, axis=0, tiled=True)  93.7 us
    dot_general x9, matrix products, dot_tn(): lax.dot_general(a, b, (((0,), (0,)), ((), ())), preferred_element_type=F32)  34.9 us
    dot_general x5, matrix products, dot_nn(): lax.dot_general(a, b, (((1,), (0,)), ((), ())), preferred_element_type=F32)  26.4 us
    dot_general x4, matrix products, dot_nt(): lax.dot_general(a, b, (((1,), (1,)), ((), ())), preferred_element_type=F32)  24.8 us
    pallas_call x1, Pallas kernels, run_backward(): pl.pallas_call(backward_kernel, out_shape=(wide, wide, wide, jax.ShapeDty...  12.1 us
  transfers between devices with their start and end apart: 7, of which 5 were waited for; matrix products, arithmetic and copies ran while one was open for 16% of the time, Pallas kernels for 49%

profile of v4, /device:TPU:0, one launch (start us, length us, event | category | flops | bytes accessed | tf_op | source)
XLA Modules:
  0.0 471.4 jit_solution(3911845447669666784)
XLA Ops:
  7.2 1.3 convert_reduce_fusion.1
  8.5 0.6 pad.18
  9.2 0.7 pad.16
  9.8 0.7 pad.17
  10.5 0.7 reshape.129
  11.2 0.7 reshape.130
  12.0 1.0 copy.38
  13.1 3.4 concatenate.20
  16.6 1.5 pad_maximum_fusion
  18.1 66.6 %all-gather.6.cloned.1.call-done = bf16[2048,2688]{1,0:T(8,128)(2,1)} async-done(((bf16[256,2688]{1,0:T(8,128)(2,1)}), bf16[2048,2688]{1,0:T(8,128)(2,1)}) %all-gather.6.cloned.1.call-update) | async-done | bytes 11010064 | tf_op jit(solution)/shard_map/all_gather | solution.py:731
  84.8 0.8 copy.40.resets_ref
  85.9 1.2 slice_convert_fusion.1
  87.2 2.5 slice_reduce_fusion
  90.2 7.1 %fusion.4 = f32[256,2176]{1,0:T(8,128)S(1)} fusion(bf16[256,2048]{1,0:T(8,128)(2,1)S(1)} %fusion.31.refs_7_, bf16[2048,2688]{1,0:T(8,128)(2,1)} %all-gather.6.cloned.1.call-done), kind=kOutput, calls=%fused_computation.4 | convolution fusion | flops 2281701376 | bytes 12189696 | tf_op jit(solution)/shard_map/dot_general | solution.py:17
  97.3 0.7 slice.219.values_ref
  98.0 0.7 slice_add_fusion.pre_ref
  98.7 1.4 fusion.48
  100.1 3.6 slot_ends.1
  103.6 2.1 collective-permute-start
  105.8 0.7 reshape.133.gain_ref
  106.5 0.7 collective-permute-done.state_ref
  107.1 0.7 copy-done.3
  107.8 6.4 %slot_forward.1 = (f32[256,64]{1,0:T(8,128)}, f32[256,256]{1,0:T(8,128)}, bf16[256,256]{1,0:T(8,128)(2,1)}, f32[256,512]{1,0:T(8,128)}, bf16[256,512]{1,0:T(8,128)(2,1)}) custom-call(bf16[256,512]{1,0:T(8,128)(2,1)} %get-tuple-element.103.query_ref, bf16[256,512]{1,0:T(8,128)(2,1)} %get-tuple-element.104.keys_ref, bf16[256,512]{1,0:T(8,128)(2,1)} %slice.219.values_ref, ...), custom_call_target="tpu_custom_call" | custom-call | tf_op jit(solution)/shard_map/slot_forward/pallas_call | solution.py:166
  114.2 3.4 convolution_convert_fusion
  117.6 46.0 %sum_branch.1 = (bf16[4,64,2048]{2,1,0:T(8,128)(2,1)}, f32[64,2048]{1,0:T(8,128)}) custom-call(bf16[4,64,2048]{2,1,0:T(8,128)(2,1)} %bitcast.67, bf16[4,64,2048]{2,1,0:T(8,128)(2,1)} %bitcast.49, f32[1,2048]{1,0:T(1,128)} %bitcast.75), custom_call_target="tpu_custom_call" | custom-call | tf_op jit(solution)/shard_map/sum_branch/pallas_call | solution.py:640
  163.6 15.0 %all-gather.8.cloned.1.call-done = bf16[2048,4224]{1,0:T(8,128)(2,1)} async-done(((bf16[256,4224]{1,0:T(8,128)(2,1)}), bf16[2048,4224]{1,0:T(8,128)(2,1)}) %all-gather.8.cloned.1.call-update) | async-done | bytes 17301520 | tf_op jit(solution)/shard_map/all_gather | solution.py:731
  178.6 4.8 %fusion.8 = f32[256,1408]{1,0:T(8,128)S(1)} fusion(bf16[256,2048]{1,0:T(8,128)(2,1)} %bitcast.57, bf16[2048,4224]{1,0:T(8,128)(2,1)} %all-gather.8.cloned.1.call-done), kind=kOutput, calls=%fused_computation.8 | convolution fusion | flops 1476395008 | bytes 8257536 | tf_op jit(solution)/shard_map/dot_general | solution.py:17
  183.5 5.6 %multiply_convert_fusion.2 = (bf16[256,1408]{1,0:T(8,128)(2,1)S(1)}, f32[256,1408]{1,0:T(8,128)}) fusion(f32[256,1408]{1,0:T(8,128)S(1)} %fusion.8, bf16[256,2048]{1,0:T(8,128)(2,1)S(1)} %bitcast.59, bf16[2048,4224]{1,0:T(8,128)(2,1)} %all-gather.8.cloned.1.call-done), kind=kOutput, calls=%fused_computation.46 | convolution fusion | flops 1478557696 | bytes 10420224 | tf_op jit(solution)/shard_map/dot_general | solution.py:17
  189.1 1.0 pad_maximum_fusion.2
  190.2 0.9 reshape.155.refs_5_.refs_4_
  191.0 0.6 slice_reduce_fusion.5
  192.3 5.4 %fusion.23 = bf16[256,2048]{1,0:T(8,128)(2,1)} fusion(bf16[256,1408]{1,0:T(8,128)(2,1)S(1)} %get-tuple-element.111, bf16[2048,4224]{1,0:T(8,128)(2,1)} %all-gather.8.cloned.1.call-done), kind=kOutput, calls=%fused_computation.24 | convolution fusion | flops 1476919296 | bytes 7536640 | tf_op jit(solution)/shard_map/dot_general | solution.py:21
  197.8 49.2 %sum_result.1 = (bf16[4,64,2048]{2,1,0:T(8,128)(2,1)}, bf16[64,2048]{1,0:T(8,128)(2,1)}, f32[64,2048]{1,0:T(8,128)}, f32[1,128]{1,0:T(1,128)}, bf16[8,256,256]{2...) custom-call(bf16[4,64,2048]{2,1,0:T(8,128)(2,1)} %bitcast.60, bf16[4,64,2048]{2,1,0:T(8,128)(2,1)} %bitcast.50, ...), custom_call_target="tpu_custom_call" | custom-call | tf_op jit(solution)/shard_map/sum_result/pallas_call | solution.py:640
  247.0 12.1 %all-gather.10.cloned.1.call-done = bf16[2048,1920]{1,0:T(8,128)(2,1)} async-done(((bf16[256,1920]{1,0:T(8,128)(2,1)}), bf16[2048,1920]{1,0:T(8,128)(2,1)}) %all-gather.10.cloned.1.call-update) | async-done | bytes 7864336 | tf_op jit(solution)/shard_map/all_gather | solution.py:731
  259.0 5.4 %multiply_convert_fusion.1 = (bf16[256,1408]{1,0:T(8,128)(2,1)S(1)}, bf16[256,1408]{1,0:T(8,128)(2,1)S(1)}) fusion(f32[256,1408]{1,0:T(8,128)S(1)} %fusion.8, f32[256,1408]{1,0:T(8,128)} %get-tuple-element.112, bf16[256,2048]{1,0:T(8,128)(2,1)} %bitcast.70, bf16[2048,4224]{1,0:T(8,128)(2,1)} %all-gather.8.cloned.1.call-done), kind=kOutput, calls=%fused_computation.45 | convolution fusion | flops 1481080832 | bytes 11141120 | tf_op jit(solution)/shard_map/dot_general | solution.py:17
  264.4 1.2 pad_maximum_fusion.1
  265.7 8.4 %fusion.20 = bf16[256,2048]{1,0:T(8,128)(2,1)} fusion(bf16[2048,4224]{1,0:T(8,128)(2,1)} %all-gather.8.cloned.1.call-done, bf16[256,1408]{1,0:T(8,128)(2,1)S(1)} %get-tuple-element.101, bf16[256,1408]{1,0:T(8,128)(2,1)S(1)} %get-tuple-element.100), kind=kOutput, calls=%fused_computation.22 | convolution fusion | flops 2956197888 | bytes 14024704 | tf_op jit(solution)/shard_map/dot_general | solution.py:21
  274.1 48.3 %sum_middle.1 = (bf16[4,64,2048]{2,1,0:T(8,128)(2,1)}, f32[64,2048]{1,0:T(8,128)}, f32[1,2048]{1,0:T(1,128)}, bf16[8,256,256]{2,1,0:T(8,128)(2,1)}) custom-call(bf16[4,64,2048]{2,1,0:T(8,128)(2,1)} %bitcast.72, bf16[4,64,2048]{2,1,0:T(8,128)(2,1)} %bitcast.51, f32[64,2048]{1,0:T(8,128)} %get-tuple-element.62.refs_1_, bf16[4,64,2048]{2,1,0:T(8,128)(2,1)} %bitcast.54, ...), custom_call_target="tpu_custom_call" | custom-call | tf_op jit(solution)/shard_map/sum_middle/pallas_call | solution.py:640
  322.4 3.4 fusion.42.grad_ref
  325.9 12.1 %slot_backward.1 = (f32[256,512]{1,0:T(8,128)}, f32[256,512]{1,0:T(8,128)}, f32[256,512]{1,0:T(8,128)}, bf16[256,512]{1,0:T(8,128)(2,1)}, f32[1,512]{1,0:T(1,128...) custom-call(f32[256,512]{1,0:T(8,128)} %fusion.42.grad_ref, ...), custom_call_target="tpu_custom_call" | custom-call | tf_op jit(solution)/shard_map/slot_backward/pallas_call | solution.py:288
  338.0 1.5 collective-permute-start.1
  339.5 2.1 collective-permute-done.1.ends_ref
  341.6 0.7 copy-done.12
  342.3 5.1 %slot_finish.1 = bf16[256,2176]{1,0:T(8,128)(2,1)} custom-call(f32[256,512]{1,0:T(8,128)} %get-tuple-element.71.gquery_ref, f32[256,512]{1,0:T(8,128)} %get-tuple-element.72.gkeys_ref, f32[256,512]{1,0:T(8,128)} %get-tuple-element.73.gvalues_ref, bf16[256,512]{1,0:T(8,128)(2,1)} %get-tuple-element.74.ggate_ref, f32[256,64]{1,0:T(8,128)} %get-tuple-element.75.gwrite_ref, ...), custom_call_target="tpu_custom_call" | custom-call | tf_op jit(solution)/shard_map/slot_finish/pallas_call | solution.py:344
  348.1 0.6 pad_maximum_fusion.3.refs_3_
  348.8 5.6 %fusion.10 = f32[256,1408]{1,0:T(8,128)} fusion(bf16[2048,256]{1,0:T(8,128)(2,1)S(1)} %bitcast.84, bf16[2048,1920]{1,0:T(8,128)(2,1)} %all-gather.10.cloned.1.call-done), kind=kOutput, calls=%fused_computation.10 | convolution fusion | flops 1476395008 | bytes 8257536 | tf_op jit(solution)/shard_map/dot_general | solution.py:25
  354.4 7.5 %fusion.26 = bf16[256,2048]{1,0:T(8,128)(2,1)} fusion(bf16[256,2176]{1,0:T(8,128)(2,1)S(1)} %copy-done.1, bf16[2048,2688]{1,0:T(8,128)(2,1)} %all-gather.6.cloned.1.call-done), kind=kOutput, calls=%fused_computation.25 | convolution fusion | flops 2282225664 | bytes 11075584 | tf_op jit(solution)/shard_map/dot_general | solution.py:21
  361.9 61.3 %sum_input.1 = (bf16[4,64,2048]{2,1,0:T(8,128)(2,1)}, f32[1,2048]{1,0:T(1,128)}, bf16[8,256,256]{2,1,0:T(8,128)(2,1)}, bf16[4,64,2048]{2,1,0:T(8,128)(2,1)}, f32[1,4736]{1,0:T(1,128)}, /*index=5*/f32[1,4736]{1,0:T(1,128)}) custom-call(bf16[4,64,2048]{2,1,0:T(8,128)(2,1)} %bitcast.73, bf16[4,64,2048]{2,1,0:T(8,128)(2,1)} %bitcast.52, ...), custom_call_target="tpu_custom_call" | custom-call | tf_op jit(solution)/shard_map/sum_input/pallas_call | solution.py:640
  423.2 1.3 fusion.50
  425.8 0.7 slice.136
  426.5 0.6 constant_dynamic-slice_fusion.1
  427.1 0.7 fusion.49
  428.3 3.5 fusion.40
  431.9 1.6 bitcast_convert_fusion
  433.5 5.6 %fusion.12 = f32[256,1408]{1,0:T(8,128)} fusion(bf16[2048,256]{1,0:T(8,128)(2,1)S(1)} %bitcast.82, bf16[2048,2816]{1,0:T(8,128)(2,1)} %all-gather.12.cloned.1.call-done), kind=kOutput, calls=%fused_computation.12 | convolution fusion | flops 1476395008 | bytes 8257536 | tf_op jit(solution)/shard_map/dot_general | solution.py:25
  439.1 5.7 %fusion.14 = f32[256,1408]{1,0:T(8,128)} fusion(bf16[2048,256]{1,0:T(8,128)(2,1)S(1)} %bitcast.83, bf16[2048,2816]{1,0:T(8,128)(2,1)} %all-gather.12.cloned.1.call-done), kind=kOutput, calls=%fused_computation.14 | convolution fusion | flops 1476395008 | bytes 8257536 | tf_op jit(solution)/shard_map/dot_general | solution.py:25
  444.7 1.3 convert_reduce_fusion
  446.1 0.6 dynamic-slice_bitcast_fusion
  446.7 3.1 fusion.32
  449.8 2.0 fusion.46
  451.7 3.1 fusion.34
  454.9 3.1 fusion.36
  458.0 3.2 fusion.38
  461.2 1.0 copy.45
  (67 shorter events, 1.8 us)
Async XLA Ops:
  7.2 77.6 %all-gather.6.cloned.1.call-start = ((), (), s32[]{:S(2)}) async-start(), calls=%async_computation | async-start | bytes 12386304 | tf_op jit(solution)/shard_map/all_gather | solution.py:731
  12.0 4.6 copy-start.8
  12.0 4.6 copy-start.9
  12.0 4.6 copy-start.10
  16.5 162.1 %all-gather.8.cloned.1.call-start = ((), (), s32[]{:S(2)}) async-start(), calls=%async_computation.1 | async-start | bytes 19464192 | tf_op jit(solution)/shard_map/all_gather | solution.py:731
  18.1 66.7 %copy-start.16 = (s32[256]{0:T(256)S(1)}, s32[256]{0:T(256)}, u32[]{:S(2)}) copy-start(s32[256]{0:T(256)} %param.24) | copy-start | bytes 3076
  18.1 67.5 %copy-start = (bf16[256,2048]{1,0:T(8,128)(2,1)S(1)}, bf16[256,2048]{1,0:T(8,128)(2,1)}, u32[]{:S(2)}) copy-start(bf16[256,2048]{1,0:T(8,128)(2,1)} %param.19) | copy-start | bytes 3145732
  84.8 174.3 %all-gather.10.cloned.1.call-start = ((), (), s32[]{:S(2)}) async-start(), calls=%async_computation.2 | async-start | bytes 8847360 | tf_op jit(solution)/shard_map/all_gather | solution.py:731
  89.7 7.6 %copy-start.13 = (f32[2048]{0:T(1024)}, f32[2048]{0:T(1024)S(1)}, u32[]{:S(2)}) copy-start(f32[2048]{0:T(1024)S(1)} %get-tuple-element.99) | copy-start | bytes 24580
  90.1 7.1 %copy-start.2 = (bf16[256,2048]{1,0:T(8,128)(2,1)}, bf16[256,2048]{1,0:T(8,128)(2,1)S(1)}, u32[]{:S(2)}) copy-start(bf16[256,2048]{1,0:T(8,128)(2,1)S(1)} %fusion.31.refs_7_) | copy-start | bytes 3145732
  103.6 3.5 collective-permute-start
  107.1 0.7 copy-start.3
  178.6 4.8 %copy-start.4 = (bf16[4,64,2048]{2,1,0:T(8,128)(2,1)S(1)}, bf16[4,64,2048]{2,1,0:T(8,128)(2,1)}, u32[]{:S(2)}) copy-start(bf16[4,64,2048]{2,1,0:T(8,128)(2,1)} %get-tuple-element.60) | copy-start | bytes 3145732
  183.4 5.6 %copy-start.11 = (bf16[256,512]{1,0:T(8,128)(2,1)S(1)}, bf16[256,512]{1,0:T(8,128)(2,1)}, u32[]{:S(2)}) copy-start(bf16[256,512]{1,0:T(8,128)(2,1)} %get-tuple-element.59) | copy-start | bytes 786436
  189.1 1.1 copy-start.17
  190.1 157.3 %all-gather.12.cloned.1.call-start = ((), (), s32[]{:S(2)}) async-start(), calls=%async_computation.3 | async-start | bytes 12976128 | tf_op jit(solution)/shard_map/all_gather | solution.py:731
  265.7 179.1 %all-gather.14.cloned.1.call-start = ((), (), s32[]{:S(2)}) async-start(), calls=%async_computation.4 | async-start | bytes 10027008 | tf_op jit(solution)/shard_map/all_gather | solution.py:731
  338.0 3.6 collective-permute-start.1
  341.6 0.7 copy-start.12
  342.3 5.8 %copy-start.14 = (f32[1,2048]{1,0:T(1,128)S(1)}, f32[1,2048]{1,0:T(1,128)}, u32[]{:S(2)}) copy-start(f32[1,2048]{1,0:T(1,128)} %get-tuple-element.81) | copy-start | bytes 24580
  342.3 5.8 %copy-start.15 = (f32[1,512]{1,0:T(1,128)S(1)}, f32[1,512]{1,0:T(1,128)}, u32[]{:S(2)}) copy-start(f32[1,512]{1,0:T(1,128)} %get-tuple-element.82) | copy-start | bytes 6148
  342.3 5.8 %copy-start.18 = (f32[1,128]{1,0:T(1,128)S(1)}, f32[1,128]{1,0:T(1,128)}, u32[]{:S(2)}) copy-start(f32[1,128]{1,0:T(1,128)} %get-tuple-element.83) | copy-start | bytes 1540
  342.3 6.5 %copy-start.20 = (bf16[8,256,256]{2,1,0:T(8,128)(2,1)S(1)}, bf16[8,256,256]{2,1,0:T(8,128)(2,1)}, u32[]{:S(2)}) copy-start(bf16[8,256,256]{2,1,0:T(8,128)(2,1)} %get-tuple-element.94) | copy-start | bytes 3145732
  348.8 5.6 %copy-start.1 = (bf16[256,2176]{1,0:T(8,128)(2,1)S(1)}, bf16[256,2176]{1,0:T(8,128)(2,1)}, u32[]{:S(2)}) copy-start(bf16[256,2176]{1,0:T(8,128)(2,1)} %slot_finish.1) | copy-start | bytes 3342340
  428.3 3.5 copy-start.5
  431.9 1.6 copy-start.19
  439.1 7.6 %copy-start.6 = (bf16[8,256,256]{2,1,0:T(8,128)(2,1)S(1)}, bf16[8,256,256]{2,1,0:T(8,128)(2,1)}, u32[]{:S(2)}) copy-start(bf16[8,256,256]{2,1,0:T(8,128)(2,1)} %get-tuple-element.88) | copy-start | bytes 3145732
  458.0 3.2 copy-start.7
Sparse Core Ops, SparseCore 0:
  16.6 68.0 all-gather.5
  86.6 91.9 all-gather.7
  190.2 68.7 all-gather.9
  265.8 78.7 all-gather.11
  347.6 64.4 all-gather.13
